TPU v7x, 32 devices: a whole 2x2x4 slice. The times are simulated.
32 devices in a mesh: wide: 4 (over z), narrow: 8 (over y, x, core).
Axes of the slice: x: 2, y: 2, z: 4, core: 2. Of those that a mesh axis runs over, the one named last changes fastest.
Arguments:
- src_design: float32 [5, 4194304], P(None, ('wide', 'narrow')), may hold values from -6 to 6
- att_design: float32 [16, 4194304], P(None, ('wide', 'narrow')), may hold values from -3 to 3
- right_side: float32 [4194304], P(('wide', 'narrow')), may hold values from -6 to 6
- block_source: int32 [65536], P(('wide', 'narrow')), may hold values from 0 to 65535, as said below
- block_segment: int32 [65536], P(('wide', 'narrow')), may hold values from 0 to 8191, as said below
- block_count: int32 [65536], P(('wide', 'narrow')), may hold values from 8 to 64
Outputs:
- sol_src: float32 [5, 65536], P(None, ('wide', 'narrow'))
- sol_att: float32 [16, 8192], P(None, 'narrow')
- dir_src: float32 [5, 65536], P(None, ('wide', 'narrow'))
- dir_att: float32 [16, 8192], P(None, 'narrow')
Inputs may be any that keep to these rules, and one draw needn't show every extreme that they name: `block_source`: A block held by the device at index w of wide names a source in [w * 2048 * 8, (w + 1) * 2048 * 8); of the 2048 blocks of one device, exactly 2048 / 8 name sources in [(w * 8 + m) * 2048, (w * 8 + m + 1) * 2048) for each m in 0 to 8 - 1; the lowest and highest source of the partition are named on every device. `block_segment`: A block held by the device at index n of narrow names a segment in [n * 1024, (n + 1) * 1024); the lowest and highest of that range are named on every device.
All inputs are finite; a program needn't handle non-finite values.
Results may differ from a plain program's by a relative error of at most 0.00018.
Values sent between devices are 32-bit elements; how exact they have to be, the bound alone decides.
No kernel may reach another device: no remote copies, remote signals or barrier semaphores. Data moves between devices by JAX's collectives and lax.ppermute only.
A program may use at most 192 MiB of HBM per device.

v0:
```python
import jax
import jax.numpy as jnp
from jax import lax
from jax.sharding import PartitionSpec as P

ITERS = 2
SRC_DEV = 2048
SEG_DEV = 1024


def on_device(src_design, att_design, right_side, block_source, block_segment, block_count):
    block_total = block_source.shape[0]
    narrow_size = lax.axis_size("narrow")
    group_size = SRC_DEV * narrow_size
    wide_at = lax.axis_index("wide")
    narrow_at = lax.axis_index("narrow")
    src_index = block_source - wide_at * group_size
    seg_index = block_segment - narrow_at * SEG_DEV
    src_blocks = src_design.reshape(src_design.shape[0], block_total, -1)
    att_blocks = att_design.reshape(att_design.shape[0], block_total, -1)
    param_rows = src_blocks.shape[0]
    obs_width = src_blocks.shape[2]
    live_rows = (jnp.arange(obs_width, dtype=jnp.int32)[None, :] < block_count[:, None]).astype(
        jnp.float32
    )
    att_weight = (wide_at == 0).astype(jnp.float32)
    src_weight = jnp.float32(1.0)

    def transposed(obs_vec):
        src_part = jnp.sum(src_blocks * obs_vec[None], axis=2)
        att_part = jnp.sum(att_blocks * obs_vec[None], axis=2)
        att_total = (
            jnp.zeros((att_blocks.shape[0], SEG_DEV), jnp.float32).at[:, seg_index].add(att_part)
        )
        att_vec = lax.psum(att_total, "wide")
        src_total = jnp.zeros((param_rows, group_size), jnp.float32).at[:, src_index].add(src_part)
        src_vec = lax.psum_scatter(src_total, "narrow", scatter_dimension=1, tiled=True)
        return (src_vec, att_vec)

    def param_dot(first_src, first_att, second_src, second_att):
        return src_weight * jnp.sum(first_src * second_src) + att_weight * jnp.sum(
            first_att * second_att
        )

    def merged_total(first, second, third, fourth):
        return lax.psum((first, second, third, fourth), ("wide", "narrow"))

    obs_vec = right_side.reshape(block_total, obs_width) * live_rows
    src_raw, att_raw = transposed(obs_vec)
    zero_val = jnp.float32(0.0)
    totals = merged_total(
        jnp.sum(obs_vec * obs_vec),
        param_dot(src_raw, att_raw, src_raw, att_raw),
        zero_val,
        zero_val,
    )
    beta_norm = jnp.sqrt(totals[0])
    alpha_norm = jnp.sqrt(totals[1]) / beta_norm
    obs_vec = obs_vec / beta_norm
    src_vec = src_raw / beta_norm / alpha_norm
    att_vec = att_raw / beta_norm / alpha_norm
    dir_src, dir_att = (src_vec, att_vec)
    sol_src = jnp.zeros_like(src_vec)
    sol_att = jnp.zeros_like(att_vec)
    phi_bar = beta_norm
    rho_bar = alpha_norm
    for step in range(ITERS):
        whole_src = lax.all_gather(src_vec, "narrow", axis=1, tiled=True)
        src_vals = jnp.take(whole_src, src_index, axis=1)
        att_vals = jnp.take(att_vec, seg_index, axis=1)
        image = jnp.sum(src_blocks * src_vals[:, :, None], axis=0)
        image = image + jnp.sum(att_blocks * att_vals[:, :, None], axis=0)
        obs_raw = image * live_rows - alpha_norm * obs_vec
        src_raw, att_raw = transposed(obs_raw)
        totals = merged_total(
            jnp.sum(obs_raw * obs_raw),
            param_dot(src_raw, att_raw, src_raw, att_raw),
            param_dot(src_raw, att_raw, src_vec, att_vec),
            param_dot(src_vec, att_vec, src_vec, att_vec),
        )
        beta_norm = jnp.sqrt(totals[0])
        alpha_square = (
            totals[1] / (beta_norm * beta_norm)
            - 2.0 * totals[2]
            + beta_norm * beta_norm * totals[3]
        )
        alpha_norm = jnp.sqrt(alpha_square)
        obs_vec = obs_raw / beta_norm
        src_vec = (src_raw / beta_norm - beta_norm * src_vec) / alpha_norm
        att_vec = (att_raw / beta_norm - beta_norm * att_vec) / alpha_norm
        rho_val = jnp.sqrt(rho_bar * rho_bar + beta_norm * beta_norm)
        cosine = rho_bar / rho_val
        sine_part = beta_norm / rho_val
        theta_val = sine_part * alpha_norm
        rho_bar = -cosine * alpha_norm
        phi_val = cosine * phi_bar
        phi_bar = sine_part * phi_bar
        sol_src = sol_src + phi_val / rho_val * dir_src
        sol_att = sol_att + phi_val / rho_val * dir_att
        dir_src = src_vec - theta_val / rho_val * dir_src
        dir_att = att_vec - theta_val / rho_val * dir_att
    return (sol_src, sol_att, dir_src, dir_att)


def solution(mesh):
    in_specs = (
        P(None, ("wide", "narrow")),
        P(None, ("wide", "narrow")),
        P(("wide", "narrow")),
        P(("wide", "narrow")),
        P(("wide", "narrow")),
        P(("wide", "narrow")),
    )
    out_specs = (
        P(None, ("wide", "narrow")),
        P(None, "narrow"),
        P(None, ("wide", "narrow")),
        P(None, "narrow"),
    )
    return jax.shard_map(
        on_device, mesh=mesh, in_specs=in_specs, out_specs=out_specs, check_vma=False
    )
```

profile of v0, /device:TPU:0, one launch (start us, length us, event | category | flops | bytes accessed | tf_op | source)
XLA Modules:
  0.0 607.7 jit_solution(5175881611888121235)
XLA Ops:
  8.1 17.4 %reshape.145 = f32[16,2048,64]{2,1,0:T(8,128)} reshape(f32[16,131072]{1,0:T(8,128)} %param.11) | data formatting | bytes 16777216 | tf_op jit(solution)/shard_map/reshape | solution.py:20
  26.1 8.2 %multiply_reduce_fusion.2 = f32[16,2048]{1,0:T(8,128)S(1)} fusion(f32[16,2048,64]{2,1,0:T(8,128)} %reshape.145, f32[2048,64]{1,0:T(8,128)S(1)} %fusion.6), kind=kLoop, calls=%fused_computation.12 | loop fusion | flops 4161536 | bytes 9043968 | tf_op jit(solution)/shard_map/reduce_sum | solution.py:31
  35.7 12.0 %scatter_custom_fusion.1 = f32[16,1024]{0,1:T(8,128)S(1)} fusion(s32[2048]{0:T(1024)S(1)} %get-tuple-element.45, f32[2048,16]{1,0:T(8,128)} %copy.42, f32[]{:T(128)} %constant.27.clone.1), kind=kCustom, calls=%fused_computation.43 | custom fusion | flops 32768 | bytes 66048 | tf_op jit(solution)/shard_map/scatter-add | solution.py:33
  59.7 15.2 %scatter_custom_fusion = f32[5,16384]{0,1:T(8,128)} fusion(s32[2048]{0:T(1024)S(1)} %get-tuple-element.47, f32[2048,5]{1,0:T(8,128)S(1)} %copy.40, f32[]{:T(128)} %constant.27.clone.1), kind=kCustom, calls=%fused_computation.24 | custom fusion | flops 10240 | bytes 327684 | tf_op jit(solution)/shard_map/scatter-add | solution.py:36
  87.8 30.0 %reduce-scatter.4.cloned.1.call-done = f32[5,2048]{1,0:T(8,128)} async-done(((f32[5,16384]{1,0:T(8,128)}), f32[5,2048]{1,0:T(8,128)}) %reduce-scatter.4.cloned.1.call-update) | async-done | bytes 40976 | tf_op jit(solution)/shard_map/reduce_scatter | solution.py:37
  119.9 39.6 %all-reduce.2 = (f32[]{:T(128)}, f32[]{:T(128)}) all-reduce(f32[]{:T(128)} %multiply_reduce_fusion.12, f32[]{:T(128)S(6)} %add.133), channel_id=1, replica_groups=mesh['wide'=4,'narrow'=8] {'wide','narrow'}, use_global_device_ids=true, to_apply=%region_10.0 | all-reduce | flops 2 | bytes 16 | tf_op jit(solution)/shard_map/psum | solution.py:46
  161.7 10.8 %all_gather.6 = f32[5,16384]{1,0:T(8,128)S(1)} all-gather(f32[5,2048]{1,0:T(8,128)S(1)} %broadcast_divide_fusion.1), channel_id=1, replica_groups=mesh['wide'=4,'narrow'=8] {'narrow'}, dimensions={1}, use_global_device_ids=true | all-gather | bytes 368640 | tf_op jit(solution)/shard_map/all_gather | solution.py:68
  178.2 11.0 %gather_fusion = f32[2048,5]{1,0:T(8,128)} fusion(f32[5,16384]{0,1:T(8,128)} %copy.44, s32[2048]{0:T(1024)S(1)} %broadcast_clamp_fusion.1), kind=kCustom, calls=%fused_computation.clone | custom fusion | bytes 90112 | tf_op jit(solution)/shard_map/jit(_take)/gather | solution.py:69
  216.1 8.3 %mul.348 = f32[16,2048,64]{2,1,0:T(8,128)} broadcast(f32[16,2048]{1,0:T(8,128)S(1)} %copy.47), dimensions={0,1} | broadcast | bytes 8519680 | tf_op jit(solution)/shard_map/mul | solution.py:72
  224.4 15.5 %mul.349 = f32[16,131072]{1,0:T(8,128)} reshape(f32[16,2048,64]{2,1,0:T(8,128)} %mul.348) | data formatting | bytes 16777216 | tf_op jit(solution)/shard_map/mul | solution.py:72
  251.1 8.4 %multiply_reduce_fusion.1 = f32[16,2048]{1,0:T(8,128)S(1)} fusion(f32[16,2048,64]{2,1,0:T(8,128)} %reshape.145, f32[2048,64]{1,0:T(8,128)S(1)} %multiply_subtract_fusion.1), kind=kLoop, calls=%fused_computation.11 | loop fusion | flops 4161536 | bytes 9043968 | tf_op jit(solution)/shard_map/reduce_sum | solution.py:31
  260.8 12.0 %scatter_custom_fusion.3 = f32[16,1024]{0,1:T(8,128)S(1)} fusion(s32[2048]{0:T(1024)S(1)} %get-tuple-element.45, f32[2048,16]{1,0:T(8,128)} %copy.50, f32[]{:T(128)} %constant.27.clone.1), kind=kCustom, calls=%fused_computation.41 | custom fusion | flops 32768 | bytes 66048 | tf_op jit(solution)/shard_map/scatter-add | solution.py:33
  278.0 15.2 %scatter_custom_fusion.2 = f32[5,16384]{0,1:T(8,128)} fusion(s32[2048]{0:T(1024)S(1)} %get-tuple-element.47, f32[2048,5]{1,0:T(8,128)S(1)} %copy.48, f32[]{:T(128)} %constant.27.clone.1), kind=kCustom, calls=%fused_computation.22 | custom fusion | flops 10240 | bytes 327684 | tf_op jit(solution)/shard_map/scatter-add | solution.py:36
  310.5 21.9 %reduce-scatter.6.cloned.1.call-done = f32[5,2048]{1,0:T(8,128)} async-done(((f32[5,16384]{1,0:T(8,128)}), f32[5,2048]{1,0:T(8,128)}) %reduce-scatter.6.cloned.1.call-update) | async-done | bytes 40976 | tf_op jit(solution)/shard_map/reduce_scatter | solution.py:37
  335.9 39.6 %all-reduce.1 = (f32[]{:T(128)}, f32[]{:T(128)}, f32[]{:T(128)}, f32[]{:T(128)}) all-reduce(f32[]{:T(128)S(6)} %add.137, f32[]{:T(128)} %get-tuple-element.42, f32[]{:T(128)S(6)} %add.138, f32[]{:T(128)S(6)} %add.139), channel_id=1, replica_groups=mesh['wide'=4,'narrow'=8] {'wide','narrow'}, use_global_device_ids=true, to_apply=%region_23.26 | all-reduce | flops 4 | bytes 32 | tf_op jit(solution)/shard_map/psum | solution.py:46
  389.2 9.2 %mul.384 = f32[16,2048,64]{2,1,0:T(8,128)} broadcast(f32[16,2048]{1,0:T(8,128)} %copy.55), dimensions={0,1} | broadcast | bytes 8519680 | tf_op jit(solution)/shard_map/mul | solution.py:72
  398.4 15.5 %mul.385 = f32[16,131072]{1,0:T(8,128)} reshape(f32[16,2048,64]{2,1,0:T(8,128)} %mul.384) | data formatting | bytes 16777216 | tf_op jit(solution)/shard_map/mul | solution.py:72
  413.9 8.2 %multiply_reduce_fusion.3 = f32[131072]{0:T(1024)} fusion(f32[16,131072]{1,0:T(8,128)} %param.11, f32[16,131072]{1,0:T(8,128)} %mul.385), kind=kLoop, calls=%fused_computation.13 | loop fusion | flops 4063232 | bytes 17301504 | tf_op jit(solution)/shard_map/reduce_sum | solution.py:72
  422.1 10.9 %all_gather.7 = f32[5,16384]{1,0:T(8,128)S(1)} all-gather(f32[5,2048]{1,0:T(8,128)S(1)} %subtract_divide_fusion.1), channel_id=1, replica_groups=mesh['wide'=4,'narrow'=8] {'narrow'}, dimensions={1}, use_global_device_ids=true | all-gather | bytes 368640 | tf_op jit(solution)/shard_map/all_gather | solution.py:68
  438.5 11.0 %gather_fusion.2 = f32[2048,5]{1,0:T(8,128)} fusion(f32[5,16384]{0,1:T(8,128)} %copy.52, s32[2048]{0:T(1024)S(1)} %broadcast_clamp_fusion.1), kind=kCustom, calls=%fused_computation.2.clone | custom fusion | bytes 90112 | tf_op jit(solution)/shard_map/jit(_take)/gather | solution.py:69
  479.3 11.7 %scatter_custom_fusion.5 = f32[16,1024]{0,1:T(8,128)S(1)} fusion(s32[2048]{0:T(1024)} %copy-done.7, f32[2048,16]{1,0:T(8,128)S(1)} %copy.58, f32[]{:T(128)} %constant.27.clone.1), kind=kCustom, calls=%fused_computation.39 | custom fusion | flops 32768 | bytes 66048 | tf_op jit(solution)/shard_map/scatter-add | solution.py:33
  496.2 15.6 %scatter_custom_fusion.4 = f32[5,16384]{0,1:T(8,128)} fusion(s32[2048]{0:T(1024)} %copy-done.8, f32[2048,5]{1,0:T(8,128)S(1)} %copy.56, f32[]{:T(128)} %constant.27.clone.1), kind=kCustom, calls=%fused_computation.20 | custom fusion | flops 10240 | bytes 328192 | tf_op jit(solution)/shard_map/scatter-add | solution.py:36
  528.8 22.3 %reduce-scatter.8.cloned.1.call-done = f32[5,2048]{1,0:T(8,128)} async-done(((f32[5,16384]{1,0:T(8,128)}), f32[5,2048]{1,0:T(8,128)}) %reduce-scatter.8.cloned.1.call-update) | async-done | bytes 40976 | tf_op jit(solution)/shard_map/reduce_scatter | solution.py:37
  554.5 39.6 %all-reduce = (f32[]{:T(128)}, f32[]{:T(128)}, f32[]{:T(128)}, f32[]{:T(128)}) all-reduce(f32[]{:T(128)} %get-tuple-element.40, f32[]{:T(128)S(6)} %add.146, f32[]{:T(128)S(6)} %add.147, f32[]{:T(128)S(6)} %add.148), channel_id=1, replica_groups=mesh['wide'=4,'narrow'=8] {'wide','narrow'}, use_global_device_ids=true, to_apply=%region_33.36 | all-reduce | flops 4 | bytes 32 | tf_op jit(solution)/shard_map/psum | solution.py:46
  (104 shorter events, 166.7 us)
Async XLA Ops:
  8.0 77.6 %all-reduce.7.cloned.1.call-start = ((), (), s32[]{:S(2)}) async-start(), calls=%async_computation.4 | async-start | bytes 131072 | tf_op jit(solution)/shard_map/psum | solution.py:35
  8.0 17.4 %copy-start = (f32[131072]{0:T(1024)S(1)}, f32[131072]{0:T(1024)}, u32[]{:S(2)}) copy-start(f32[131072]{0:T(1024)} %param.12) | copy-start | bytes 1572868
  8.1 17.6 %copy-start.6 = (s32[2048]{0:T(1024)S(1)}, s32[2048]{0:T(1024)}, u32[]{:S(2)}) copy-start(s32[2048]{0:T(1024)} %param.15) | copy-start | bytes 24580
  26.0 9.6 %copy-start.10 = (s32[2048]{0:T(1024)S(1)}, s32[2048]{0:T(1024)}, u32[]{:S(2)}) copy-start(s32[2048]{0:T(1024)} %param.14) | copy-start | bytes 24580
  35.6 225.2 %copy-start.7 = (s32[2048]{0:T(1024)}, s32[2048]{0:T(1024)S(1)}, u32[]{:S(2)}) copy-start(s32[2048]{0:T(1024)S(1)} %get-tuple-element.45) | copy-start | bytes 24580
  35.7 23.6 %copy-start.11 = (s32[2048]{0:T(1024)S(1)}, s32[2048]{0:T(1024)}, u32[]{:S(2)}) copy-start(s32[2048]{0:T(1024)} %param.13) | copy-start | bytes 24580
  48.5 69.3 %reduce-scatter.4.cloned.1.call-start = ((), (), s32[]{:S(2)}) async-start(), calls=%async_computation.3 | async-start | bytes 589824 | tf_op jit(solution)/shard_map/reduce_scatter | solution.py:37
  59.3 129.9 %copy-start.9 = (pred[2048]{0:T(1024)(128)(4,1)}, pred[2048]{0:T(1024)(128)(4,1)S(1)}, u32[]{:S(2)}) copy-start(pred[2048]{0:T(1024)(128)(4,1)S(1)} %get-tuple-element.46) | copy-start | bytes 6148
  59.3 218.7 %copy-start.8 = (s32[2048]{0:T(1024)}, s32[2048]{0:T(1024)S(1)}, u32[]{:S(2)}) copy-start(s32[2048]{0:T(1024)S(1)} %get-tuple-element.47) | copy-start | bytes 24580
  80.9 226.2 %all-reduce.9.cloned.1.call-start = ((), (), s32[]{:S(2)}) async-start(), calls=%async_computation.6 | async-start | bytes 131072 | tf_op jit(solution)/shard_map/psum | solution.py:35
  194.5 11.9 %copy-start.3 = (f32[16,1024]{1,0:T(8,128)S(1)}, f32[16,1024]{1,0:T(8,128)}, u32[]{:S(2)}) copy-start(f32[16,1024]{1,0:T(8,128)} %all-reduce.7.cloned.1.call-done) | copy-start | bytes 196612
  239.9 7.6 %copy-start.1 = (f32[131072]{0:T(1024)S(1)}, f32[131072]{0:T(1024)}, u32[]{:S(2)}) copy-start(f32[131072]{0:T(1024)} %multiply_reduce_fusion.9) | copy-start | bytes 1572868
  273.6 58.8 %reduce-scatter.6.cloned.1.call-start = ((), (), s32[]{:S(2)}) async-start(), calls=%async_computation.5 | async-start | bytes 589824 | tf_op jit(solution)/shard_map/reduce_scatter | solution.py:37
  278.0 54.5 %copy-start.4 = (f32[5,2048]{1,0:T(8,128)S(1)}, f32[5,2048]{1,0:T(8,128)}, u32[]{:S(2)}) copy-start(f32[5,2048]{1,0:T(8,128)} %reduce-scatter.4.cloned.1.call-done) | copy-start | bytes 122884
  299.2 226.2 %all-reduce.11.cloned.1.call-start = ((), (), s32[]{:S(2)}) async-start(), calls=%async_computation.8 | async-start | bytes 131072 | tf_op jit(solution)/shard_map/psum | solution.py:35
  413.9 8.2 %copy-start.5 = (f32[5,2048]{1,0:T(8,128)S(1)}, f32[5,2048]{1,0:T(8,128)}, u32[]{:S(2)}) copy-start(f32[5,2048]{1,0:T(8,128)} %reduce-scatter.6.cloned.1.call-done) | copy-start | bytes 122884
  456.1 11.2 %copy-start.2 = (f32[131072]{0:T(1024)S(1)}, f32[131072]{0:T(1024)}, u32[]{:S(2)}) copy-start(f32[131072]{0:T(1024)} %multiply_reduce_fusion.3) | copy-start | bytes 1572868
  491.8 59.2 %reduce-scatter.8.cloned.1.call-start = ((), (), s32[]{:S(2)}) async-start(), calls=%async_computation.7 | async-start | bytes 589824 | tf_op jit(solution)/shard_map/reduce_scatter | solution.py:37
Sparse Core Ops, SparseCore 0:
  48.6 37.0 all-reduce.6
  273.7 33.3 all-reduce.8
  492.0 33.3 all-reduce.10
Sparse Core Ops, SparseCore 1:
  81.0 36.8 reduce-scatter.3
  299.3 33.1 reduce-scatter.5
  517.8 33.1 reduce-scatter.7
where the time goes:
time: 616 us; the launch traced here: 608 us
  local copies, waits for them, and re-layouts  171 us (28%)
  other arithmetic  171 us (28%)
  blocking collectives  140 us (23%)
  waiting for transfers between devices  92.8 us (15%)
  between operations  32.3 us (5%)
    psum x3, blocking collectives, merged_total(): return lax.psum((first, second, third, fourth), ('wide', 'narrow'))  119 us
    reduce_scatter x3, waiting for transfers between devices, transposed(): lax.psum_scatter(src_total, 'narrow', scatter_dimension=1, tiled=True)  74.2 us
    mul x4, local copies, waits for them, and re-layouts, on_device(): image = image + jnp.sum(att_blocks * att_vals[:, :, None], axis=0)  48.4 us
    scatter-add x3, other arithmetic, transposed(): jnp.zeros((param_rows, group_size), jnp.float32).at[:, src_index]  45.9 us
    scatter-add x3, other arithmetic, transposed(): jnp.zeros((att_blocks.shape[0], SEG_DEV), jnp.float32).at[:, seg_index]  35.6 us
    reduce_sum x3, other arithmetic, transposed(): att_part = jnp.sum(att_blocks * obs_vec[None], axis=2)  24.9 us
    gather x2, local copies, waits for them, and re-layouts, on_device(): src_vals = jnp.take(whole_src, src_index, axis=1)  21.9 us
    all_gather x2, blocking collectives, on_device(): whole_src = lax.all_gather(src_vec, 'narrow', axis=1, tiled=True)  21.7 us
  transfers between devices with their start and end apart: 6, of which 6 were waited for; matrix products, arithmetic and copies ran while one was open for 15% of the time, Pallas kernels for 0%

commit v1 on v0

v1 whole, which is shorter than its diff:
```python
import functools

import jax
import jax.numpy as jnp
from jax import lax
from jax.experimental import pallas as pl
from jax.experimental.pallas import tpu as pltpu
from jax.sharding import PartitionSpec as P

SRC_DEV = 2048
SEG_DEV = 1024
LANE = 128
HIGH = 256
F32 = jnp.float32
BF16 = jnp.bfloat16
I32 = jnp.int32
MIB = 1 << 20


def lanes_of(values, index):
    return jnp.take_along_axis(values, index, axis=1, mode="promise_in_bounds")


def row_iota(rows, columns=LANE):
    return lax.broadcasted_iota(I32, (rows, columns), 0)


def lane_iota(rows, columns=LANE):
    return lax.broadcasted_iota(I32, (rows, columns), 1)


def to_tiles(rows):
    count = rows.shape[0]
    lane = lane_iota(count)
    first = lanes_of(rows, (2 * lane) % LANE)
    second = lanes_of(rows, (2 * lane + 1) % LANE)
    head = lane < LANE // 2
    even = jnp.where(head, first, pltpu.roll(first, count - 1, 0))
    odd = jnp.where(head, pltpu.roll(second, 1, 0), second)
    return jnp.where(row_iota(count) % 2 == 0, even, odd)


def split_three(values):
    top = values.astype(BF16).astype(F32)
    rest = values - top
    middle = rest.astype(BF16).astype(F32)
    return top, middle, rest - middle


def dot_lanes(left, right):
    return lax.dot_general(left, right, (((1,), (1,)), ((), ())), preferred_element_type=F32)


def spread_rows(store, picked, row, column, levels):
    rows = picked.shape[0]
    for part, piece in enumerate(split_three(picked)):
        for level in range(levels):
            at = (part * levels + level) * rows
            kept = jnp.where(row == level, piece, 0.0)
            store[pl.ds(at, rows), pl.ds(column, LANE)] = kept.astype(BF16)


def index_kernel(narrow, source_ref, segment_ref, pos_ref, seg_ref, order_ref, ids_ref, left, right):
    tiles = source_ref.shape[0]
    cap = tiles * LANE // narrow
    local = to_tiles(source_ref[...]) & (SRC_DEV * narrow - 1)
    seg_ref[...] = to_tiles(segment_ref[...]) & (SEG_DEV - 1)
    owner = local // SRC_DEV
    inner = local & (SRC_DEV - 1)
    marks = jnp.concatenate([jnp.where(owner == m, 1.0, 0.0) for m in range(narrow)], axis=0)
    marks = marks.astype(BF16)
    total = narrow * tiles
    before = jnp.where(row_iota(LANE) < lane_iota(LANE), 1.0, 0.0).astype(BF16)
    in_row = jnp.dot(marks, before, preferred_element_type=F32)
    at_row, at_lane = row_iota(total, total), lane_iota(total, total)
    earlier = (at_row // tiles == at_lane // tiles) & (at_lane < at_row)
    ahead = jnp.dot(jnp.where(earlier, 1.0, 0.0).astype(BF16), marks, preferred_element_type=F32)
    ahead = jnp.dot(ahead.astype(BF16), jnp.ones((LANE, LANE), BF16), preferred_element_type=F32)
    rank = (in_row + ahead).astype(I32)
    pos = jnp.zeros((tiles, LANE), I32)
    for m in range(narrow):
        pos = jnp.where(owner == m, m * cap + rank[m * tiles : (m + 1) * tiles], pos)
    pos_ref[...] = pos
    levels = tiles * LANE // HIGH
    high_at = row_iota(HIGH)
    lane = lane_iota(1).astype(F32)
    for t in range(tiles):
        here = pos[t : t + 1]
        level = row_iota(levels) == here // HIGH
        mine = inner[t : t + 1]
        pieces = (
            jnp.full((1, LANE), float(t), F32),
            lane,
            (mine // LANE).astype(F32),
            (mine % LANE).astype(F32),
        )
        for part, piece in enumerate(pieces):
            left[part * levels : (part + 1) * levels, t * LANE : (t + 1) * LANE] = jnp.where(
                level, piece, 0.0
            ).astype(BF16)
        right[:, t * LANE : (t + 1) * LANE] = jnp.where(high_at == here % HIGH, 1.0, 0.0).astype(
            BF16
        )
    found = dot_lanes(left[...], right[...])
    tile_at, lane_at = found[:levels], found[levels : 2 * levels]
    order = (tile_at * LANE + lane_at).astype(I32)
    ids = found[2 * levels : 3 * levels] * LANE + found[3 * levels :]
    for level in range(levels):
        for half in range(HIGH // LANE):
            row = level * (HIGH // LANE) + half
            cut = slice(half * LANE, (half + 1) * LANE)
            order_ref[row : row + 1, :] = order[level : level + 1, cut]
            ids_ref[row : row + 1, :] = ids[level : level + 1, cut]


def scatter_att(blocks, seg_ref, out_ref, left, right):
    tiles = seg_ref.shape[0]
    levels = SEG_DEV // HIGH
    high_at = row_iota(HIGH)

    def fill(t, carry):
        here = seg_ref[pl.ds(t, 1), :]
        column = pl.multiple_of(t * LANE, LANE)
        spread_rows(left, blocks[t, 0:16, :], here // HIGH, column, levels)
        right[:, pl.ds(column, LANE)] = jnp.where(high_at == here % HIGH, 1.0, 0.0).astype(BF16)
        return carry

    lax.fori_loop(0, tiles, fill, 0)
    sums = dot_lanes(left[...], right[...])
    size = 16 * levels
    sums = sums[:size] + (sums[size : 2 * size] + sums[2 * size :])
    for level in range(levels):
        out_ref[:, level * HIGH : (level + 1) * HIGH] = sums[level * 16 : (level + 1) * 16]


def pick(tables, count, index):
    low = index & (LANE - 1)
    high = index // LANE
    rows = tables(0).shape[0]
    low = jnp.broadcast_to(low, (rows, LANE))
    out = lanes_of(tables(0), low)
    for c in range(1, count):
        out = jnp.where(high == c, lanes_of(tables(c), low), out)
    return out


def send_sorted(narrow, blocks, order_ref, extra, out_ref):
    tiles = order_ref.shape[0]
    cap = tiles * LANE // narrow
    per = cap // LANE
    keep = row_iota(8) < 5
    for t in range(tiles):
        values = pick(lambda c: blocks[c, 16:24, :], tiles, order_ref[t : t + 1, :])
        values = jnp.where(keep, values, extra(t))
        out_ref[t // per, :, (t % per) * LANE : (t % per + 1) * LANE] = values


def entry(ref, per, t):
    return ref[t // per, :, (t % per) * LANE : (t % per + 1) * LANE]


def start_kernel(att_ref, src_ref, rhs_ref, count_ref, table_ref, first_ref, square_ref, counts):
    step = pl.program_id(0)

    @pl.when(step == 0)
    def _():
        counts[...] = to_tiles(count_ref[...])
        square_ref[...] = jnp.zeros_like(square_ref)

    wide_rhs = rhs_ref[...].T
    place = row_iota(64)
    live, obs = [], []
    for half in range(2):
        alive = place < counts[pl.ds(step * 2 + half, 1), :]
        live.append(alive)
        part = jnp.where(alive, wide_rhs[half * 64 : half * 64 + 64], 0.0)
        obs.append(part)
        square = part * part
        total = square[0:8]
        for at in range(8, 64, 8):
            total = total + square[at : at + 8]
        square_ref[...] += total
    att_rows = 16
    for i in range(att_rows + src_ref.shape[1]):
        if i < att_rows:
            values = att_ref[i // 8, :, i % 8, :]
        else:
            values = src_ref[:, i - att_rows, :]
        turned = values.T
        for half in range(2):
            part = jnp.where(live[half], turned[half * 64 : half * 64 + 64], 0.0)
            table_ref[half, i] = part
            first_ref[half, i : i + 1, :] = jnp.sum(part * obs[half], axis=0, keepdims=True)
    for half in range(2):
        first_ref[half, 21:24, :] = jnp.zeros((3, LANE), F32)


def first_send_kernel(
    narrow, blocks, seg_ref, order_ref, ids_ref, square_ref, att_ref, send_ref, left, right
):
    scatter_att(blocks, seg_ref, att_ref, left, right)
    lane = lane_iota(16)
    att_ref[:, SEG_DEV:] = jnp.where(lane == 0, jnp.sum(square_ref[...]), 0.0)
    row = row_iota(8)
    send_sorted(
        narrow,
        blocks,
        order_ref,
        lambda t: jnp.where(row == 5, ids_ref[t : t + 1, :], 0.0),
        send_ref,
    )


def owner_kernel(
    narrow, first, recv_ref, half_ref, other_ref, given_ref, src_ref, back_ref, att_ref, out_ref,
    left, right,
):
    tiles, cap = given_ref.shape[0], recv_ref.shape[2]
    per = cap // LANE
    levels = SRC_DEV // HIGH
    high_at = row_iota(HIGH)
    keep = row_iota(8) < 5
    att_ref[...] = half_ref[...] + other_ref[...]
    if first:
        for t in range(tiles):
            out_ref[t : t + 1, :] = entry(recv_ref, per, t)[5:6].astype(I32)
        index_ref = out_ref
    else:
        index_ref = given_ref
        known = recv_ref[0, :, 0:LANE]
        for n in range(1, narrow):
            known = known + recv_ref[n, :, 0:LANE]
        out_ref[...] = known
    for t in range(tiles):
        here = index_ref[t : t + 1, :]
        values = jnp.where(keep, entry(recv_ref, per, t), 0.0)
        spread_rows(left, values, here // HIGH, t * LANE, levels)
        right[:, t * LANE : (t + 1) * LANE] = jnp.where(high_at == here % HIGH, 1.0, 0.0).astype(
            BF16
        )
    sums = dot_lanes(left[...], right[...])
    size = 8 * levels
    sums = sums[:size] + (sums[size : 2 * size] + sums[2 * size :])
    for level in range(levels):
        src_ref[:, level * HIGH : (level + 1) * HIGH] = sums[level * 8 : (level + 1) * 8]
    if back_ref is None:
        return
    square = jnp.sum(src_ref[...] * src_ref[...]) if first else 0.0
    mark = jnp.where((row_iota(8) == 6) & (lane_iota(8) == 0), square, 0.0)
    for t in range(tiles):
        values = pick(
            lambda c: src_ref[:, c * LANE : (c + 1) * LANE],
            SRC_DEV // LANE,
            index_ref[t : t + 1, :],
        )
        values = jnp.where(keep, values, mark)
        back_ref[t // per, :, (t % per) * LANE : (t % per + 1) * LANE] = values


def lane_value(row, at):
    return jnp.sum(jnp.where(lane_iota(1) == at, row, 0.0), axis=1, keepdims=True)


def product_kernel(
    narrow, first, recv_ref, half_ref, other_ref, known_ref, pos_ref, seg_ref, order_ref, table_ref,
    full_ref, att_ref, send_ref, scale_ref, vec, blocks, left, right, held, sems,
):
    tiles, rows = pos_ref.shape[0], held.shape[1]
    cap = recv_ref.shape[2]
    per = cap // LANE

    def copy(t):
        return pltpu.make_async_copy(table_ref.at[t], held.at[t], sems.at[t])

    def begin(t, carry):
        copy(t).start()
        return carry

    lax.fori_loop(0, tiles, begin, 0)
    full = half_ref[...] + other_ref[...]
    full_ref[...] = full[:, :SEG_DEV]
    notes = full[0:1, SEG_DEV:]
    if first:
        scale = jnp.ones((1, 1), F32)
        square_src = recv_ref[0, 6:7, 0:LANE]
        for n in range(1, narrow):
            square_src = square_src + recv_ref[n, 6:7, 0:LANE]
        square_src = lane_value(square_src, 0)
        square_att = jnp.sum(full[:, :SEG_DEV] * full[:, :SEG_DEV], keepdims=True)
        rhs_square = lane_value(notes, 0)
        att_note = jnp.where(lane_iota(16) == 1, square_src, 0.0)
        send_note = jnp.where(
            row_iota(8) == 6,
            jnp.where(lane_iota(8) == 0, rhs_square, jnp.where(lane_iota(8) == 1, square_att, 0.0)),
            0.0,
        )
    else:
        known = known_ref[6:7, :]
        square = lane_value(notes, 1) + lane_value(known, 1)
        scale = lane_value(known, 0) / square
        att_note = jnp.zeros((16, LANE), F32)
        send_note = jnp.zeros((8, LANE), F32)
    scale_ref[...] = jnp.broadcast_to(scale, (8, LANE))

    def gather(t, carry):
        where_src = pos_ref[pl.ds(t, 1), :]
        where_att = seg_ref[pl.ds(t, 1), :]
        for top in range(0, 16, 8):
            picked = pick(
                lambda c: full_ref[top : top + 8, c * LANE : (c + 1) * LANE],
                SEG_DEV // LANE,
                where_att,
            )
            vec[t, top : top + 8, :] = picked * scale
        vec[t, 16:24, :] = pick(lambda c: entry(recv_ref, per, c), tiles, where_src) * scale
        return carry

    lax.fori_loop(0, tiles, gather, 0)

    def multiply(t, carry):
        copy(t).wait()
        image = held[t, 0] * vec[t, 0:1, :]
        for i in range(1, rows):
            image = image + held[t, i] * vec[t, i : i + 1, :]
        for i in range(rows):
            blocks[t, i : i + 1, :] = jnp.sum(held[t, i] * image, axis=0, keepdims=True)
        blocks[t, rows:24, :] = jnp.zeros((24 - rows, LANE), F32)
        return carry

    lax.fori_loop(0, tiles, multiply, 0)
    scatter_att(blocks, seg_ref, att_ref, left, right)
    att_ref[:, SEG_DEV:] = att_note
    send_sorted(narrow, blocks, order_ref, lambda t: send_note, send_ref)


def dots_kernel(
    src0, src1, src2, att0, att1, att2a, att2b, square_ref, scale_ref, weight_ref, out_ref, att2
):
    att2[...] = (att2a[...] + att2b[...])[:, :SEG_DEV]
    scale = scale_ref[0:1, 0:1]
    weight = weight_ref[0:1, 0:1]
    src = (src0[...], src1[...] * scale, src2[...] * scale)
    att = (att0[...], att1[...] * scale, att2[...] * scale)
    out = jnp.where(lane_iota(1) == 0, jnp.sum(square_ref[...], keepdims=True), 0.0)
    for at, (one, two) in enumerate(((0, 0), (0, 1), (1, 1), (1, 2), (2, 2))):
        total = jnp.sum(src[one] * src[two], keepdims=True)
        total = total + weight * jnp.sum(att[one] * att[two], keepdims=True)
        out = jnp.where(lane_iota(1) == at + 1, total, out)
    out_ref[...] = jnp.broadcast_to(out, out_ref.shape)


def finish_kernel(
    dots_ref, scale_ref, src0, src1, src2, att0, att1, att2, sol_src, sol_att, dir_src, dir_att
):
    sums = jnp.sum(dots_ref[...], axis=0, keepdims=True)
    rhs_square, m0, m1, m2, m3, m4 = [lane_value(sums, at) for at in range(6)]
    scale = scale_ref[0:1, 0:1]
    mean = m1 / m0
    ww = m2 - mean * m1
    wz = m3 - 2.0 * mean * m2 + mean * mean * m1
    zz = m4 - 2.0 * mean * m3 + mean * mean * m2
    root0, root1 = jnp.sqrt(m0), jnp.sqrt(ww)
    beta1 = jnp.sqrt(rhs_square)
    alpha1 = root0 / beta1
    beta2 = jnp.sqrt(mean / scale - alpha1 * alpha1)
    cross = root1 / (scale * root0)
    alpha2 = cross / beta2
    quotient = wz / ww / scale
    beta3 = jnp.sqrt(quotient - alpha2 * alpha2)
    third = zz / ww / (scale * scale) - quotient * quotient - cross * cross
    alpha3 = jnp.sqrt(third) / beta3
    phi_bar, rho_bar = beta1, alpha1
    steps, turns = [], []
    for beta, alpha in ((beta2, alpha2), (beta3, alpha3)):
        rho = jnp.sqrt(rho_bar * rho_bar + beta * beta)
        cosine, sine = rho_bar / rho, beta / rho
        theta = sine * alpha
        rho_bar = -cosine * alpha
        steps.append(cosine * phi_bar / rho)
        turns.append(theta / rho)
        phi_bar = sine * phi_bar
    sides = (
        (src0, src1, src2, sol_src, dir_src),
        (att0, att1, att2, sol_att, dir_att),
    )
    for zero, one, two, sol, direction in sides:
        rows = sol.shape[0]
        base, once, twice = zero[0:rows], one[0:rows] * scale, two[0:rows] * scale
        v1 = base / root0
        v2 = (once - mean * base) / root1
        v3 = ((twice - mean * once) / (scale * root1) - quotient * v2 - cross * v1) / (
            beta3 * alpha3
        )
        turned = v2 - turns[0] * v1
        sol[...] = steps[0] * v1 + steps[1] * turned
        direction[...] = v3 - turns[1] * turned


def sds(shape, dtype=F32):
    return jax.ShapeDtypeStruct(shape, dtype)


def call(kernel, outs, scratch=(), limit=24, **more):
    return pl.pallas_call(
        kernel,
        out_shape=outs,
        scratch_shapes=list(scratch),
        compiler_params=pltpu.CompilerParams(vmem_limit_bytes=limit * MIB),
        **more,
    )


def on_device(src_design, att_design, right_side, block_source, block_segment, block_count):
    narrow, wide = lax.axis_size("narrow"), lax.axis_size("wide")
    devices = narrow * wide
    blocks = block_source.shape[0]
    tiles = blocks // LANE
    cap = blocks // narrow
    src_rows, att_rows = src_design.shape[0], att_design.shape[0]
    rows = src_rows + att_rows
    columns = right_side.shape[0] // LANE
    groups = columns // LANE
    obs = right_side.shape[0] // blocks

    def across(values, step):
        return lax.ppermute(values, "wide", [(i, i ^ step) for i in range(wide)])

    def exchange(values):
        return lax.all_to_all(values, "narrow", 0, 0)

    tile_rows = lambda values: values.reshape(tiles, LANE)
    att_view = att_design.reshape(att_rows // 8, 8, columns, LANE).transpose(0, 2, 1, 3)
    src_view = src_design.reshape(src_rows, columns, LANE).transpose(1, 0, 2)

    table, first, square = call(
        start_kernel,
        (sds((tiles, rows, obs, LANE)), sds((tiles, 24, LANE)), sds((8, LANE))),
        [pltpu.VMEM((tiles, LANE), I32)],
        grid=(groups,),
        in_specs=[
            pl.BlockSpec((att_rows // 8, LANE, 8, LANE), lambda g: (0, g, 0, 0)),
            pl.BlockSpec((LANE, src_rows, LANE), lambda g: (g, 0, 0)),
            pl.BlockSpec((LANE, LANE), lambda g: (g, 0)),
            pl.BlockSpec((tiles, LANE), lambda g: (0, 0)),
        ],
        out_specs=(
            pl.BlockSpec((2, rows, obs, LANE), lambda g: (g, 0, 0, 0)),
            pl.BlockSpec((2, 24, LANE), lambda g: (g, 0, 0)),
            pl.BlockSpec((8, LANE), lambda g: (0, 0)),
        ),
    )(att_view, src_view, right_side.reshape(columns, LANE), tile_rows(block_count))

    right_store = pltpu.VMEM((HIGH, blocks), BF16)
    att_left = pltpu.VMEM((3 * 16 * SEG_DEV // HIGH, blocks), BF16)
    src_left = pltpu.VMEM((3 * 8 * SRC_DEV // HIGH, blocks), BF16)
    tile_int = sds((tiles, LANE), I32)
    pos, seg, order, ids = call(
        functools.partial(index_kernel, narrow),
        (tile_int, tile_int, tile_int, sds((tiles, LANE))),
        [pltpu.VMEM((4 * blocks // HIGH, blocks), BF16), right_store],
    )(tile_rows(block_source), tile_rows(block_segment))

    send_shape = sds((narrow, 8, cap))
    att_shape = sds((16, SEG_DEV + LANE))
    src_shape = sds((8, SRC_DEV))
    part, send = call(
        functools.partial(first_send_kernel, narrow),
        (att_shape, send_shape),
        [att_left, right_store],
    )(first, seg, order, ids, square)

    given = ids_known = None
    results = []
    scale = None
    for step in range(3):
        other = across(part, 1)
        arrived = exchange(send)
        first_time = step == 0
        last_time = step == 2
        outs = [src_shape]
        if not last_time:
            outs.append(send_shape)
        outs.append(att_shape)
        outs.append(tile_int if first_time else sds((8, LANE)))
        kernel = functools.partial(owner_kernel, narrow, first_time)
        if last_time:
            whole = lambda *refs, k=kernel: k(*refs[:5], None, *refs[5:])
        else:
            whole = kernel
        given_in = seg if first_time else given
        made = call(whole, tuple(outs), [src_left, right_store])(arrived, part, other, given_in)
        src_sum, half, note = made[0], made[-2], made[-1]
        if first_time:
            given = note
            note = jnp.zeros((8, LANE), F32)
        later = None
        total = half
        jump = 2
        while jump < wide:
            if later is not None:
                total = total + later
            later = across(total, jump)
            jump *= 2
        if later is None:
            later = jnp.zeros_like(total)
        if last_time:
            results.append((src_sum, total, later))
            break
        back = exchange(made[1])
        att_sum, part, send, scale = call(
            functools.partial(product_kernel, narrow, first_time),
            (sds((16, SEG_DEV)), att_shape, send_shape, sds((8, LANE))),
            [
                pltpu.VMEM((tiles, 24, LANE), F32),
                pltpu.VMEM((tiles, 24, LANE), F32),
                att_left,
                right_store,
                pltpu.VMEM((tiles, rows, obs, LANE), F32),
                pltpu.SemaphoreType.DMA((tiles,)),
            ],
            in_specs=[pl.BlockSpec(memory_space=pltpu.VMEM)] * 7
            + [pl.BlockSpec(memory_space=pl.ANY)],
        )(back, total, later, note, pos, seg, order, table)
        results.append((src_sum, att_sum))

    weight = jnp.where(lax.axis_index("wide") == 0, 1.0, 0.0).astype(F32) * jnp.ones((8, LANE), F32)
    (src0, att0), (src1, att1), (src2, att2a, att2b) = results
    dots, att2 = call(dots_kernel, (sds((devices, LANE)), sds((16, SEG_DEV))))(
        src0, src1, src2, att0, att1, att2a, att2b, square, scale, weight
    )
    dots = lax.all_to_all(dots, ("wide", "narrow"), 0, 0, tiled=True)
    sol_src, sol_att, dir_src, dir_att = call(
        finish_kernel,
        (
            sds((src_rows, SRC_DEV)),
            sds((att_rows, SEG_DEV)),
            sds((src_rows, SRC_DEV)),
            sds((att_rows, SEG_DEV)),
        ),
    )(dots, scale, src0, src1, src2, att0, att1, att2)
    return (sol_src, sol_att, dir_src, dir_att)


def solution(mesh):
    both = ("wide", "narrow")
    in_specs = (P(None, both), P(None, both), P(both), P(both), P(both), P(both))
    out_specs = (P(None, both), P(None, "narrow"), P(None, both), P(None, "narrow"))
    return jax.shard_map(
        on_device, mesh=mesh, in_specs=in_specs, out_specs=out_specs, check_vma=False
    )
```

time: 616 us -> 109 us (0.18); the launches traced: 608 us -> 108 us
  other arithmetic: 171 us -> 0 us
  local copies, waits for them, and re-layouts: 171 us -> 8.69 us
  blocking collectives: 140 us -> 48.5 us
  waiting for transfers between devices: 92.8 us -> 3.6 us
  Pallas kernels: 0 us -> 35.8 us
  between operations: 32.3 us -> 0.7 us
  starting transfers between devices: 0.46 us -> 10.9 us
    psum x3 -> x0, blocking collectives: 119 us -> none  [merged_total(): return lax.psum((first, second, third, fourth), ('wide', 'narrow'))]
    scatter-add x6 -> x0, other arithmetic: 81.5 us -> none  [the longest x3 45.9 us: transposed(): jnp.zeros((param_rows, group_size), jnp.float32).at[:, src_index]]
    reduce_sum x19 -> x0, other arithmetic: 75.6 us -> none  [the longest x3 24.9 us: transposed(): att_part = jnp.sum(att_blocks * obs_vec[None], axis=2)]
    reduce_scatter x3 -> x0, waiting for transfers between devices: 74.2 us -> none  [transposed(): lax.psum_scatter(src_total, 'narrow', scatter_dimension=1, tiled=True)]
    mul x8 -> x1, local copies, waits for them, and re-layouts: 68.3 us -> 0.01 us  [on_device(): jnp.where(lax.axis_index('wide') == 0, 1.0, 0.0).astype(F32)]
    all_to_all x0 -> x6, blocking collectives: none -> 48.5 us  [the longest x5 38.1 us: exchange(): return lax.all_to_all(values, 'narrow', 0, 0)]
    gather x4 -> x0, local copies, waits for them, and re-layouts: 37 us -> none  [the longest x2 21.9 us: on_device(): src_vals = jnp.take(whole_src, src_index, axis=1)]
    pallas_call x0 -> x10, Pallas kernels: none -> 35.8 us  [the longest x2 18.4 us: on_device(): call(functools.partial(product_kernel, narrow, first_time), (sds((16, SEG...]
  transfers between devices with their start and end apart: 6 -> 6, of which waited for: 6 -> 1; matrix products, arithmetic and copies ran while one was open for 15% -> 0% of each run, Pallas kernels for 0% -> 0%
where the time goes in v1:
time: 109 us; the launch traced here: 108 us
  blocking collectives  48.5 us (44%)
  Pallas kernels  35.8 us (33%)
  starting transfers between devices  10.9 us (10%)
  local copies, waits for them, and re-layouts  8.69 us (8%)
  waiting for transfers between devices  3.6 us (3%)
    all_to_all x5, blocking collectives, exchange(): return lax.all_to_all(values, 'narrow', 0, 0)  38.1 us
    pallas_call x2, Pallas kernels, on_device(): call(functools.partial(product_kernel, narrow, first_time), (sds((16, SEG...  18.4 us
    ppermute x6, starting transfers between devices, across(): return lax.ppermute(values, 'wide', [(i, i ^ step) for i in range(wide)])  10.9 us
    all_to_all x1, blocking collectives, on_device(): dots = lax.all_to_all(dots, ('wide', 'narrow'), 0, 0, tiled=True)  10.4 us
    pallas_call x1, Pallas kernels, on_device(): call(start_kernel, (sds((tiles, rows, obs, LANE)), sds((tiles, 24, LANE))...  9.58 us
    unnamed x12, local copies, waits for them, and re-layouts  8.69 us
    pallas_call x3, Pallas kernels, on_device(): call(whole, tuple(outs), [src_left, right_store])  4.56 us
    ppermute x6, waiting for transfers between devices, across(): return lax.ppermute(values, 'wide', [(i, i ^ step) for i in range(wide)])  3.6 us
  transfers between devices with their start and end apart: 6, of which 1 were waited for; matrix products, arithmetic and copies ran while one was open for 0% of the time, Pallas kernels for 0%

profile of v1, /device:TPU:0, one launch (start us, length us, event | category | flops | bytes accessed | tf_op | source)
XLA Modules:
  0.0 108.2 jit_solution(12144443495164384094)
XLA Ops:
  1.3 0.7 copy-done.4
  2.0 0.9 shard_map.94
  3.0 3.4 %copy-done = f32[16,131072]{1,0:T(8,128)S(1)} copy-done((f32[16,131072]{1,0:T(8,128)S(1)}, f32[16,131072]{1,0:T(8,128)}, u32[]{:S(2)}) %copy-start) | copy-done | bytes 8388632
  6.3 2.2 %copy-done.1 = f32[5,131072]{1,0:T(8,128)S(1)} copy-done((f32[5,131072]{1,0:T(8,128)S(1)}, f32[5,131072]{1,0:T(8,128)}, u32[]{:S(2)}) %copy-start.1) | copy-done | bytes 2621464
  8.5 1.0 copy-done.2
  10.3 9.6 %shard_map.93 = (f32[16,21,64,128]{3,2,1,0:T(8,128)S(1)}, f32[16,24,128]{2,1,0:T(8,128)S(1)}, f32[8,128]{1,0:T(8,128)S(1)}) custom-call(f32[2,1024,8,128]{3,2,1,0:T(8,128)S(1)} %bitcast.14, f32[1024,5,128]{2,1,0:T(8,128)S(1)} %bitcast.15, f32[1024,128]{1,0:T(8,128)S(1)} %bitcast.16, s32[16,128]{1,0:T(8,128)S(1)} %bitcast.21), custom_call_target="tpu_custom_call" | custom-call | tf_op jit(solution)/shard_map/pallas_call | solution.py:435
  19.9 1.2 %shard_map.95 = (f32[16,1152]{1,0:T(8,128)S(1)}, f32[8,8,256]{2,1,0:T(8,128)S(1)}) custom-call(f32[16,24,128]{2,1,0:T(8,128)S(1)} %get-tuple-element.32.blocks, s32[16,128]{1,0:T(8,128)S(1)} %get-tuple-element.33.seg_ref.given_ref, s32[16,128]{1,0:T(8,128)S(1)} %get-tuple-element.34.order_ref, f32[16,128]{1,0:T(8,128)S(1)} %get-tuple-element.35.ids_ref, ...), custom_call_target="tpu_custom_call" | custom-call | tf_op jit(solution)/shard_map/pallas_call | solution.py:466
  21.1 3.1 %collective-permute-start = (f32[16,1152]{1,0:T(8,128)S(1)}, f32[16,1152]{1,0:T(8,128)S(1)}, u32[]{:S(2)}, u32[]{:S(2)}) collective-permute-start(f32[16,1152]{1,0:T(8,128)S(1)} %get-tuple-element.38.half_ref), channel_id=1, source_target_pairs={{0,8},{8,0},{16,24},{24,16},{1,9},{9,1},{17,25},{25,17},{2,10},{10... | collective-permute-start | bytes 221192 | tf_op jit(solution)/shard_map/ppermute | solution.py:426
  24.2 8.5 %all_to_all.36.recv_ref = f32[8,8,256]{2,1,0:T(8,128)S(1)} all-to-all(f32[8,8,256]{2,1,0:T(8,128)S(1)} %get-tuple-element.37), channel_id=1, replica_groups=mesh['wide'=4,'narrow'=8] {'narrow'}, dimensions={0} | all-to-all | bytes 131072 | tf_op jit(solution)/shard_map/all_to_all | solution.py:429
  32.7 1.6 %shard_map.96 = (f32[8,2048]{1,0:T(8,128)S(1)}, f32[8,8,256]{2,1,0:T(8,128)S(1)}, f32[16,1152]{1,0:T(8,128)S(1)}, s32[16,128]{1,0:T(8,128)S(1)}) custom-call(f32[8,8,256]{2,1,0:T(8,128)S(1)} %all_to_all.36.recv_ref, f32[16,1152]{1,0:T(8,128)S(1)} %get-tuple-element.38.half_ref, f32[16,1152]{1,0:T(8,128)S(1)} %collective-permute-done.other_ref, ...), custom_call_target="tpu_custom_call" | custom-call | tf_op jit(solution)/shard_map/pallas_call | solution.py:491
  34.3 2.7 %collective-permute-start.1 = (f32[16,1152]{1,0:T(8,128)S(1)}, f32[16,1152]{1,0:T(8,128)S(1)}, u32[]{:S(2)}, u32[]{:S(2)}) collective-permute-start(f32[16,1152]{1,0:T(8,128)S(1)} %get-tuple-element.41.half_ref), channel_id=1, source_target_pairs={{0,16},{8,24},{16,0},{24,8},{1,17},{9,25},{17,1},{25,9},{2,18},{10... | collective-permute-start | bytes 221192 | tf_op jit(solution)/shard_map/ppermute | solution.py:426
  37.0 7.4 %all_to_all.37.recv_ref = f32[8,8,256]{2,1,0:T(8,128)S(1)} all-to-all(f32[8,8,256]{2,1,0:T(8,128)S(1)} %get-tuple-element.40), channel_id=1, replica_groups=mesh['wide'=4,'narrow'=8] {'narrow'}, dimensions={0} | all-to-all | bytes 131072 | tf_op jit(solution)/shard_map/all_to_all | solution.py:429
  44.4 9.2 %shard_map.97 = (f32[16,1024]{1,0:T(8,128)S(1)}, f32[16,1152]{1,0:T(8,128)S(1)}, f32[8,8,256]{2,1,0:T(8,128)S(1)}, f32[8,128]{1,0:T(8,128)}) custom-call(f32[8,8,256]{2,1,0:T(8,128)S(1)} %all_to_all.37.recv_ref, f32[16,1152]{1,0:T(8,128)S(1)} %get-tuple-element.41.half_ref, f32[16,1152]{1,0:T(8,128)S(1)} %collective-permute-done.1.other_ref, ...), custom_call_target="tpu_custom_call" | custom-call | tf_op jit(solution)/shard_map/pallas_call | solution.py:510
  54.1 7.4 %all_to_all.38.recv_ref = f32[8,8,256]{2,1,0:T(8,128)S(1)} all-to-all(f32[8,8,256]{2,1,0:T(8,128)S(1)} %get-tuple-element.44), channel_id=1, replica_groups=mesh['wide'=4,'narrow'=8] {'narrow'}, dimensions={0} | all-to-all | bytes 131072 | tf_op jit(solution)/shard_map/all_to_all | solution.py:429
  61.5 1.6 %shard_map.98 = (f32[8,2048]{1,0:T(8,128)S(1)}, f32[8,8,256]{2,1,0:T(8,128)S(1)}, f32[16,1152]{1,0:T(8,128)S(1)}, f32[8,128]{1,0:T(8,128)S(1)}) custom-call(f32[8,8,256]{2,1,0:T(8,128)S(1)} %all_to_all.38.recv_ref, f32[16,1152]{1,0:T(8,128)S(1)} %get-tuple-element.45.half_ref, f32[16,1152]{1,0:T(8,128)S(1)} %collective-permute-done.2.other_ref, ...), custom_call_target="tpu_custom_call" | custom-call | tf_op jit(solution)/shard_map/pallas_call | solution.py:491
  63.4 7.4 %all_to_all.39.recv_ref = f32[8,8,256]{2,1,0:T(8,128)S(1)} all-to-all(f32[8,8,256]{2,1,0:T(8,128)S(1)} %get-tuple-element.48), channel_id=1, replica_groups=mesh['wide'=4,'narrow'=8] {'narrow'}, dimensions={0} | all-to-all | bytes 131072 | tf_op jit(solution)/shard_map/all_to_all | solution.py:429
  70.8 9.2 %shard_map.99 = (f32[16,1024]{1,0:T(8,128)S(1)}, f32[16,1152]{1,0:T(8,128)S(1)}, f32[8,8,256]{2,1,0:T(8,128)S(1)}, f32[8,128]{1,0:T(8,128)S(1)}) custom-call(f32[8,8,256]{2,1,0:T(8,128)S(1)} %all_to_all.39.recv_ref, f32[16,1152]{1,0:T(8,128)S(1)} %get-tuple-element.49.half_ref, f32[16,1152]{1,0:T(8,128)S(1)} %collective-permute-done.3.other_ref, ...), custom_call_target="tpu_custom_call" | custom-call | tf_op jit(solution)/shard_map/pallas_call | solution.py:510
  80.0 1.6 %collective-permute-start.4 = (f32[16,1152]{1,0:T(8,128)S(1)}, f32[16,1152]{1,0:T(8,128)S(1)}, u32[]{:S(2)}, u32[]{:S(2)}) collective-permute-start(f32[16,1152]{1,0:T(8,128)S(1)} %get-tuple-element.52.refs_1_), channel_id=1, source_target_pairs={{0,8},{8,0},{16,24},{24,16},{1,9},{9,1},{17,25},{25,17},{2,10},{10... | collective-permute-start | bytes 221192 | tf_op jit(solution)/shard_map/ppermute | solution.py:426
  81.6 7.4 %all_to_all.40.refs_0_ = f32[8,8,256]{2,1,0:T(8,128)S(1)} all-to-all(f32[8,8,256]{2,1,0:T(8,128)S(1)} %get-tuple-element.51), channel_id=1, replica_groups=mesh['wide'=4,'narrow'=8] {'narrow'}, dimensions={0} | all-to-all | bytes 131072 | tf_op jit(solution)/shard_map/all_to_all | solution.py:429
  89.0 1.4 %shard_map.100 = (f32[8,2048]{1,0:T(8,128)S(1)}, f32[16,1152]{1,0:T(8,128)S(1)}, f32[8,128]{1,0:T(8,128)}) custom-call(f32[8,8,256]{2,1,0:T(8,128)S(1)} %all_to_all.40.refs_0_, f32[16,1152]{1,0:T(8,128)S(1)} %get-tuple-element.52.refs_1_, f32[16,1152]{1,0:T(8,128)S(1)} %collective-permute-done.4.refs_2_, s32[16,128]{1,0:T(8,128)S(1)} %get-tuple-element.46.given_ref.refs_3_), custom_call_target="tpu_custom_call" | custom-call | tf_op jit(solution)/shard_map/pallas_call | solution.py:491
  90.4 2.6 %collective-permute-start.5 = (f32[16,1152]{1,0:T(8,128)S(1)}, f32[16,1152]{1,0:T(8,128)S(1)}, u32[]{:S(2)}, u32[]{:S(2)}) collective-permute-start(f32[16,1152]{1,0:T(8,128)S(1)} %get-tuple-element.56.att2a), channel_id=1, source_target_pairs={{0,16},{8,24},{16,0},{24,8},{1,17},{9,25},{17,1},{25,9},{2,18},{10... | collective-permute-start | bytes 221192 | tf_op jit(solution)/shard_map/ppermute | solution.py:426
  93.0 3.6 %collective-permute-done.5.att2b = f32[16,1152]{1,0:T(8,128)S(1)} collective-permute-done((f32[16,1152]{1,0:T(8,128)S(1)}, f32[16,1152]{1,0:T(8,128)S(1)}, u32[]{:S(2)}, u32[]{:S(2)}) %collective-permute-start.5) | collective-permute-done | bytes 73760 | tf_op jit(solution)/shard_map/ppermute | solution.py:426
  96.9 10.4 %all_to_all.41 = f32[32,1,128]{2,1,0:T(1,128)S(1)} all-to-all(f32[32,1,128]{2,1,0:T(1,128)S(1)} %bitcast.18), channel_id=1, replica_groups=mesh['wide'=4,'narrow'=8] {'wide','narrow'}, dimensions={0} | all-to-all | bytes 32768 | tf_op jit(solution)/shard_map/all_to_all | solution.py:531
  107.3 0.9 shard_map.102
  (18 shorter events, 2.6 us)
Async XLA Ops:
  0.6 0.7 copy-start.3
  1.3 0.7 copy-start.4
  3.0 3.4 %copy-start = (f32[16,131072]{1,0:T(8,128)S(1)}, f32[16,131072]{1,0:T(8,128)}, u32[]{:S(2)}) copy-start(f32[16,131072]{1,0:T(8,128)} %param.7) | copy-start | bytes 25165828
  6.3 2.2 %copy-start.1 = (f32[5,131072]{1,0:T(8,128)S(1)}, f32[5,131072]{1,0:T(8,128)}, u32[]{:S(2)}) copy-start(f32[5,131072]{1,0:T(8,128)} %param.6) | copy-start | bytes 7864324
  8.5 1.0 copy-start.2
  9.6 0.7 copy-start.5
  21.1 11.6 %collective-permute-start = (f32[16,1152]{1,0:T(8,128)S(1)}, f32[16,1152]{1,0:T(8,128)S(1)}, u32[]{:S(2)}, u32[]{:S(2)}) collective-permute-start(f32[16,1152]{1,0:T(8,128)S(1)} %get-tuple-element.38.half_ref), channel_id=1, source_target_pairs={{0,8},{8,0},{16,24},{24,16},{1,9},{9,1},{17,25},{25,17},{2,10},{10... | collective-permute-start | bytes 221192 | tf_op jit(solution)/shard_map/ppermute | solution.py:426
  34.3 10.0 %collective-permute-start.1 = (f32[16,1152]{1,0:T(8,128)S(1)}, f32[16,1152]{1,0:T(8,128)S(1)}, u32[]{:S(2)}, u32[]{:S(2)}) collective-permute-start(f32[16,1152]{1,0:T(8,128)S(1)} %get-tuple-element.41.half_ref), channel_id=1, source_target_pairs={{0,16},{8,24},{16,0},{24,8},{1,17},{9,25},{17,1},{25,9},{2,18},{10... | collective-permute-start | bytes 221192 | tf_op jit(solution)/shard_map/ppermute | solution.py:426
  53.6 7.9 %collective-permute-start.2 = (f32[16,1152]{1,0:T(8,128)S(1)}, f32[16,1152]{1,0:T(8,128)S(1)}, u32[]{:S(2)}, u32[]{:S(2)}) collective-permute-start(f32[16,1152]{1,0:T(8,128)S(1)} %get-tuple-element.45.half_ref), channel_id=1, source_target_pairs={{0,8},{8,0},{16,24},{24,16},{1,9},{9,1},{17,25},{25,17},{2,10},{10... | collective-permute-start | bytes 221192 | tf_op jit(solution)/shard_map/ppermute | solution.py:426
  63.0 7.8 %collective-permute-start.3 = (f32[16,1152]{1,0:T(8,128)S(1)}, f32[16,1152]{1,0:T(8,128)S(1)}, u32[]{:S(2)}, u32[]{:S(2)}) collective-permute-start(f32[16,1152]{1,0:T(8,128)S(1)} %get-tuple-element.49.half_ref), channel_id=1, source_target_pairs={{0,16},{8,24},{16,0},{24,8},{1,17},{9,25},{17,1},{25,9},{2,18},{10... | collective-permute-start | bytes 221192 | tf_op jit(solution)/shard_map/ppermute | solution.py:426
  80.0 9.0 %collective-permute-start.4 = (f32[16,1152]{1,0:T(8,128)S(1)}, f32[16,1152]{1,0:T(8,128)S(1)}, u32[]{:S(2)}, u32[]{:S(2)}) collective-permute-start(f32[16,1152]{1,0:T(8,128)S(1)} %get-tuple-element.52.refs_1_), channel_id=1, source_target_pairs={{0,8},{8,0},{16,24},{24,16},{1,9},{9,1},{17,25},{25,17},{2,10},{10... | collective-permute-start | bytes 221192 | tf_op jit(solution)/shard_map/ppermute | solution.py:426
  90.4 6.2 %collective-permute-start.5 = (f32[16,1152]{1,0:T(8,128)S(1)}, f32[16,1152]{1,0:T(8,128)S(1)}, u32[]{:S(2)}, u32[]{:S(2)}) collective-permute-start(f32[16,1152]{1,0:T(8,128)S(1)} %get-tuple-element.56.att2a), channel_id=1, source_target_pairs={{0,16},{8,24},{16,0},{24,8},{1,17},{9,25},{17,1},{25,9},{2,18},{10... | collective-permute-start | bytes 221192 | tf_op jit(solution)/shard_map/ppermute | solution.py:426

commit v2 on v1

--- a/solution.py
+++ b/solution.py
@@ -60,7 +60,7 @@
             store[pl.ds(at, rows), pl.ds(column, LANE)] = kept.astype(BF16)
 
 
-def index_kernel(narrow, source_ref, segment_ref, pos_ref, seg_ref, order_ref, ids_ref, left, right):
+def rank_blocks(narrow, source_ref, segment_ref, pos_ref, seg_ref, order_ref, ids_ref, left, right):
     tiles = source_ref.shape[0]
     cap = tiles * LANE // narrow
     local = to_tiles(source_ref[...]) & (SRC_DEV * narrow - 1)
@@ -101,7 +101,7 @@
         right[:, t * LANE : (t + 1) * LANE] = jnp.where(high_at == here % HIGH, 1.0, 0.0).astype(
             BF16
         )
-    found = dot_lanes(left[...], right[...])
+    found = dot_lanes(left[0 : 4 * levels, :], right[...])
     tile_at, lane_at = found[:levels], found[levels : 2 * levels]
     order = (tile_at * LANE + lane_at).astype(I32)
     ids = found[2 * levels : 3 * levels] * LANE + found[3 * levels :]
@@ -159,45 +159,76 @@
     return ref[t // per, :, (t % per) * LANE : (t % per + 1) * LANE]
 
 
-def start_kernel(att_ref, src_ref, rhs_ref, count_ref, table_ref, first_ref, square_ref, counts):
-    step = pl.program_id(0)
-
-    @pl.when(step == 0)
-    def _():
-        counts[...] = to_tiles(count_ref[...])
-        square_ref[...] = jnp.zeros_like(square_ref)
-
-    wide_rhs = rhs_ref[...].T
-    place = row_iota(64)
-    live, obs = [], []
-    for half in range(2):
-        alive = place < counts[pl.ds(step * 2 + half, 1), :]
-        live.append(alive)
-        part = jnp.where(alive, wide_rhs[half * 64 : half * 64 + 64], 0.0)
-        obs.append(part)
-        square = part * part
-        total = square[0:8]
-        for at in range(8, 64, 8):
-            total = total + square[at : at + 8]
-        square_ref[...] += total
-    att_rows = 16
-    for i in range(att_rows + src_ref.shape[1]):
-        if i < att_rows:
-            values = att_ref[i // 8, :, i % 8, :]
-        else:
-            values = src_ref[:, i - att_rows, :]
-        turned = values.T
+def start_kernel(
+    narrow,
+    att_hbm, src_hbm, rhs_hbm, source_hbm, segment_hbm, count_hbm,
+    table_ref, square_ref, pos_ref, seg_ref, order_ref, att_ref, send_ref,
+    att_in, src_in, rhs_in, source_in, segment_in, count_in, blocks, ids, left, right, sems, int_sems,
+):
+    groups = att_in.shape[0]
+    att_rows, src_rows = att_in.shape[1] * att_in.shape[3], src_in.shape[2]
+    obs = table_ref.shape[2]
+
+    def ints():
+        pairs = ((source_hbm, source_in), (segment_hbm, segment_in), (count_hbm, count_in))
+        return [
+            pltpu.make_async_copy(one, two, int_sems.at[at]) for at, (one, two) in enumerate(pairs)
+        ]
+
+    def loads(g):
+        cut = pl.ds(g * LANE, LANE)
+        return [
+            pltpu.make_async_copy(att_hbm.at[:, cut], att_in.at[g], sems.at[0, g]),
+            pltpu.make_async_copy(src_hbm.at[cut], src_in.at[g], sems.at[1, g]),
+            pltpu.make_async_copy(rhs_hbm.at[cut], rhs_in.at[g], sems.at[2, g]),
+        ]
+
+    def begin(g, carry):
+        for one in loads(g):
+            one.start()
+        return carry
+
+    for one in ints():
+        one.start()
+    lax.fori_loop(0, groups, begin, 0)
+    for one in ints():
+        one.wait()
+    count_in[...] = to_tiles(count_in[...])
+    square_ref[...] = jnp.zeros_like(square_ref)
+    rank_blocks(narrow, source_in, segment_in, pos_ref, seg_ref, order_ref, ids, left, right)
+    place = row_iota(obs)
+
+    def turn(g, carry):
+        for one in loads(g):
+            one.wait()
+        wide_rhs = rhs_in[g].T
+        live, rhs = [], []
         for half in range(2):
-            part = jnp.where(live[half], turned[half * 64 : half * 64 + 64], 0.0)
-            table_ref[half, i] = part
-            first_ref[half, i : i + 1, :] = jnp.sum(part * obs[half], axis=0, keepdims=True)
-    for half in range(2):
-        first_ref[half, 21:24, :] = jnp.zeros((3, LANE), F32)
-
-
-def first_send_kernel(
-    narrow, blocks, seg_ref, order_ref, ids_ref, square_ref, att_ref, send_ref, left, right
-):
+            alive = place < count_in[pl.ds(g * 2 + half, 1), :]
+            live.append(alive)
+            part = jnp.where(alive, wide_rhs[half * obs : half * obs + obs], 0.0)
+            rhs.append(part)
+            square = part * part
+            total = square[0:8]
+            for at in range(8, obs, 8):
+                total = total + square[at : at + 8]
+            square_ref[...] += total
+        for i in range(att_rows + src_rows):
+            if i < att_rows:
+                values = att_in[g, i // 8, :, i % 8, :]
+            else:
+                values = src_in[g, :, i - att_rows, :]
+            turned = values.T
+            for half in range(2):
+                part = jnp.where(live[half], turned[half * obs : half * obs + obs], 0.0)
+                table_ref[g * 2 + half, i] = part
+                blocks[g * 2 + half, i : i + 1, :] = jnp.sum(part * rhs[half], axis=0, keepdims=True)
+        for half in range(2):
+            rest = 24 - att_rows - src_rows
+            blocks[g * 2 + half, 24 - rest : 24, :] = jnp.zeros((rest, LANE), F32)
+        return carry
+
+    lax.fori_loop(0, groups, turn, 0)
     scatter_att(blocks, seg_ref, att_ref, left, right)
     lane = lane_iota(16)
     att_ref[:, SEG_DEV:] = jnp.where(lane == 0, jnp.sum(square_ref[...]), 0.0)
@@ -206,7 +237,7 @@
         narrow,
         blocks,
         order_ref,
-        lambda t: jnp.where(row == 5, ids_ref[t : t + 1, :], 0.0),
+        lambda t: jnp.where(row == 5, ids[t : t + 1, :], 0.0),
         send_ref,
     )
 
@@ -263,20 +294,12 @@
 
 def product_kernel(
     narrow, first, recv_ref, half_ref, other_ref, known_ref, pos_ref, seg_ref, order_ref, table_ref,
-    full_ref, att_ref, send_ref, scale_ref, vec, blocks, left, right, held, sems,
+    full_ref, att_ref, send_ref, scale_ref, vec, blocks, left, right,
 ):
-    tiles, rows = pos_ref.shape[0], held.shape[1]
+    tiles, rows = pos_ref.shape[0], table_ref.shape[1]
     cap = recv_ref.shape[2]
     per = cap // LANE
 
-    def copy(t):
-        return pltpu.make_async_copy(table_ref.at[t], held.at[t], sems.at[t])
-
-    def begin(t, carry):
-        copy(t).start()
-        return carry
-
-    lax.fori_loop(0, tiles, begin, 0)
     full = half_ref[...] + other_ref[...]
     full_ref[...] = full[:, :SEG_DEV]
     notes = full[0:1, SEG_DEV:]
@@ -318,12 +341,11 @@
     lax.fori_loop(0, tiles, gather, 0)
 
     def multiply(t, carry):
-        copy(t).wait()
-        image = held[t, 0] * vec[t, 0:1, :]
+        image = table_ref[t, 0] * vec[t, 0:1, :]
         for i in range(1, rows):
-            image = image + held[t, i] * vec[t, i : i + 1, :]
+            image = image + table_ref[t, i] * vec[t, i : i + 1, :]
         for i in range(rows):
-            blocks[t, i : i + 1, :] = jnp.sum(held[t, i] * image, axis=0, keepdims=True)
+            blocks[t, i : i + 1, :] = jnp.sum(table_ref[t, i] * image, axis=0, keepdims=True)
         blocks[t, rows:24, :] = jnp.zeros((24 - rows, LANE), F32)
         return carry
 
@@ -400,6 +422,10 @@
     return jax.ShapeDtypeStruct(shape, dtype)
 
 
+def in_hbm(values):
+    return pltpu.with_memory_space_constraint(values, pltpu.HBM)
+
+
 def call(kernel, outs, scratch=(), limit=24, **more):
     return pl.pallas_call(
         kernel,
@@ -432,44 +458,54 @@
     att_view = att_design.reshape(att_rows // 8, 8, columns, LANE).transpose(0, 2, 1, 3)
     src_view = src_design.reshape(src_rows, columns, LANE).transpose(1, 0, 2)
 
-    table, first, square = call(
-        start_kernel,
-        (sds((tiles, rows, obs, LANE)), sds((tiles, 24, LANE)), sds((8, LANE))),
-        [pltpu.VMEM((tiles, LANE), I32)],
-        grid=(groups,),
-        in_specs=[
-            pl.BlockSpec((att_rows // 8, LANE, 8, LANE), lambda g: (0, g, 0, 0)),
-            pl.BlockSpec((LANE, src_rows, LANE), lambda g: (g, 0, 0)),
-            pl.BlockSpec((LANE, LANE), lambda g: (g, 0)),
-            pl.BlockSpec((tiles, LANE), lambda g: (0, 0)),
-        ],
-        out_specs=(
-            pl.BlockSpec((2, rows, obs, LANE), lambda g: (g, 0, 0, 0)),
-            pl.BlockSpec((2, 24, LANE), lambda g: (g, 0, 0)),
-            pl.BlockSpec((8, LANE), lambda g: (0, 0)),
-        ),
-    )(att_view, src_view, right_side.reshape(columns, LANE), tile_rows(block_count))
-
     right_store = pltpu.VMEM((HIGH, blocks), BF16)
     att_left = pltpu.VMEM((3 * 16 * SEG_DEV // HIGH, blocks), BF16)
     src_left = pltpu.VMEM((3 * 8 * SRC_DEV // HIGH, blocks), BF16)
     tile_int = sds((tiles, LANE), I32)
-    pos, seg, order, ids = call(
-        functools.partial(index_kernel, narrow),
-        (tile_int, tile_int, tile_int, sds((tiles, LANE))),
-        [pltpu.VMEM((4 * blocks // HIGH, blocks), BF16), right_store],
-    )(tile_rows(block_source), tile_rows(block_segment))
-
     send_shape = sds((narrow, 8, cap))
     att_shape = sds((16, SEG_DEV + LANE))
     src_shape = sds((8, SRC_DEV))
-    part, send = call(
-        functools.partial(first_send_kernel, narrow),
-        (att_shape, send_shape),
-        [att_left, right_store],
-    )(first, seg, order, ids, square)
-
-    given = ids_known = None
+    table, square, pos, seg, order, part, send = call(
+        functools.partial(start_kernel, narrow),
+        (
+            sds((tiles, rows, obs, LANE)),
+            sds((8, LANE)),
+            tile_int,
+            tile_int,
+            tile_int,
+            att_shape,
+            send_shape,
+        ),
+        [
+            pltpu.VMEM((groups, att_rows // 8, LANE, 8, LANE), F32),
+            pltpu.VMEM((groups, LANE, src_rows, LANE), F32),
+            pltpu.VMEM((groups, LANE, LANE), F32),
+            pltpu.VMEM((tiles, LANE), I32),
+            pltpu.VMEM((tiles, LANE), I32),
+            pltpu.VMEM((tiles, LANE), I32),
+            pltpu.VMEM((tiles, 24, LANE), F32),
+            pltpu.VMEM((tiles, LANE), F32),
+            att_left,
+            right_store,
+            pltpu.SemaphoreType.DMA((3, groups)),
+            pltpu.SemaphoreType.DMA((3,)),
+        ],
+        in_specs=[pl.BlockSpec(memory_space=pltpu.HBM)] * 6,
+    )(
+        *map(
+            in_hbm,
+            (
+                att_view,
+                src_view,
+                right_side.reshape(columns, LANE),
+                tile_rows(block_source),
+                tile_rows(block_segment),
+                tile_rows(block_count),
+            ),
+        )
+    )
+
+    given = None
     results = []
     scale = None
     for step in range(3):
@@ -515,11 +551,7 @@
                 pltpu.VMEM((tiles, 24, LANE), F32),
                 att_left,
                 right_store,
-                pltpu.VMEM((tiles, rows, obs, LANE), F32),
-                pltpu.SemaphoreType.DMA((tiles,)),
             ],
-            in_specs=[pl.BlockSpec(memory_space=pltpu.VMEM)] * 7
-            + [pl.BlockSpec(memory_space=pl.ANY)],
         )(back, total, later, note, pos, seg, order, table)
         results.append((src_sum, att_sum))
 

time: 109 us -> 92.1 us (0.84)
  local copies, waits for them, and re-layouts: 8.69 us -> 0.01 us
  Pallas kernels: 35.8 us -> 28.1 us
    unnamed x12 -> x0, local copies, waits for them, and re-layouts: 8.69 us -> none
    pallas_call x2, Pallas kernels: 18.4 us -> 9.95 us  [on_device(): call(functools.partial(product_kernel, narrow, first_time), (sds((16, SEG...]
    pallas_call x3 -> x1, Pallas kernels: 11.7 us -> 12.4 us  [on_device(): call(functools.partial(start_kernel, narrow), (sds((tiles, rows, obs, LAN...]
where the time goes in v2:
time: 92.1 us; the launch traced here: 91.8 us
  blocking collectives  48.5 us (53%)
  Pallas kernels  28.1 us (31%)
  starting transfers between devices  10.9 us (12%)
  waiting for transfers between devices  3.61 us (4%)
    all_to_all x5, blocking collectives, exchange(): return lax.all_to_all(values, 'narrow', 0, 0)  38.1 us
    pallas_call x1, Pallas kernels, on_device(): call(functools.partial(start_kernel, narrow), (sds((tiles, rows, obs, LAN...  12.4 us
    ppermute x6, starting transfers between devices, across(): return lax.ppermute(values, 'wide', [(i, i ^ step) for i in range(wide)])  10.9 us
    all_to_all x1, blocking collectives, on_device(): dots = lax.all_to_all(dots, ('wide', 'narrow'), 0, 0, tiled=True)  10.4 us
    pallas_call x2, Pallas kernels, on_device(): call(functools.partial(product_kernel, narrow, first_time), (sds((16, SEG...  9.95 us
    pallas_call x3, Pallas kernels, on_device(): call(whole, tuple(outs), [src_left, right_store])  4.56 us
    ppermute x6, waiting for transfers between devices, across(): return lax.ppermute(values, 'wide', [(i, i ^ step) for i in range(wide)])  3.61 us
  transfers between devices with their start and end apart: 6, of which 1 were waited for; matrix products, arithmetic and copies ran while one was open for 0% of the time, Pallas kernels for 0%

profile of v2, /device:TPU:0, one launch (start us, length us, event | category | flops | bytes accessed | tf_op | source)
XLA Modules:
  0.0 91.8 jit_solution(9307590847143430038)
XLA Ops:
  0.6 12.4 %shard_map.93 = (f32[16,21,64,128]{3,2,1,0:T(8,128)S(1)}, f32[8,128]{1,0:T(8,128)S(1)}, s32[16,128]{1,0:T(8,128)S(1)}, s32[16,128]{1,0:T(8,128)S(1)}, s32[16,128...) custom-call(f32[2,1024,8,128]{3,2,1,0:T(8,128)} %bitcast.16, f32[1024,5,128]{2,1,0:T(8,128)} %bitcast.17, ...), custom_call_target="tpu_custom_call" | custom-call | tf_op jit(solution)/shard_map/pallas_call | solution.py:468
  13.1 3.1 %collective-permute-start = (f32[16,1152]{1,0:T(8,128)S(1)}, f32[16,1152]{1,0:T(8,128)S(1)}, u32[]{:S(2)}, u32[]{:S(2)}) collective-permute-start(f32[16,1152]{1,0:T(8,128)S(1)} %get-tuple-element.31.half_ref), channel_id=1, source_target_pairs={{0,8},{8,0},{16,24},{24,16},{1,9},{9,1},{17,25},{25,17},{2,10},{10... | collective-permute-start | bytes 221192 | tf_op jit(solution)/shard_map/ppermute | solution.py:452
  16.2 8.5 %all_to_all.36.recv_ref = f32[8,8,256]{2,1,0:T(8,128)S(1)} all-to-all(f32[8,8,256]{2,1,0:T(8,128)S(1)} %get-tuple-element.30), channel_id=1, replica_groups=mesh['wide'=4,'narrow'=8] {'narrow'}, dimensions={0} | all-to-all | bytes 131072 | tf_op jit(solution)/shard_map/all_to_all | solution.py:455
  24.7 0.0 collective-permute-done.other_ref
  24.7 1.6 %shard_map.94 = (f32[8,2048]{1,0:T(8,128)S(1)}, f32[8,8,256]{2,1,0:T(8,128)S(1)}, f32[16,1152]{1,0:T(8,128)S(1)}, s32[16,128]{1,0:T(8,128)S(1)}) custom-call(f32[8,8,256]{2,1,0:T(8,128)S(1)} %all_to_all.36.recv_ref, f32[16,1152]{1,0:T(8,128)S(1)} %get-tuple-element.31.half_ref, f32[16,1152]{1,0:T(8,128)S(1)} %collective-permute-done.other_ref, ...), custom_call_target="tpu_custom_call" | custom-call | tf_op jit(solution)/shard_map/pallas_call | solution.py:527
  26.3 2.6 %collective-permute-start.1 = (f32[16,1152]{1,0:T(8,128)S(1)}, f32[16,1152]{1,0:T(8,128)S(1)}, u32[]{:S(2)}, u32[]{:S(2)}) collective-permute-start(f32[16,1152]{1,0:T(8,128)S(1)} %get-tuple-element.35.half_ref), channel_id=1, source_target_pairs={{0,16},{8,24},{16,0},{24,8},{1,17},{9,25},{17,1},{25,9},{2,18},{10... | collective-permute-start | bytes 221192 | tf_op jit(solution)/shard_map/ppermute | solution.py:452
  29.0 7.4 %all_to_all.37.recv_ref = f32[8,8,256]{2,1,0:T(8,128)S(1)} all-to-all(f32[8,8,256]{2,1,0:T(8,128)S(1)} %get-tuple-element.34), channel_id=1, replica_groups=mesh['wide'=4,'narrow'=8] {'narrow'}, dimensions={0} | all-to-all | bytes 131072 | tf_op jit(solution)/shard_map/all_to_all | solution.py:455
  36.4 0.0 collective-permute-done.1.other_ref
  36.4 5.0 %shard_map.95 = (f32[16,1024]{1,0:T(8,128)S(1)}, f32[16,1152]{1,0:T(8,128)S(1)}, f32[8,8,256]{2,1,0:T(8,128)S(1)}, f32[8,128]{1,0:T(8,128)}) custom-call(f32[8,8,256]{2,1,0:T(8,128)S(1)} %all_to_all.37.recv_ref, f32[16,1152]{1,0:T(8,128)S(1)} %get-tuple-element.35.half_ref, f32[16,1152]{1,0:T(8,128)S(1)} %collective-permute-done.1.other_ref, ...), custom_call_target="tpu_custom_call" | custom-call | tf_op jit(solution)/shard_map/pallas_call | solution.py:546
  41.4 0.5 collective-permute-start.2
  41.8 7.4 %all_to_all.38.recv_ref = f32[8,8,256]{2,1,0:T(8,128)S(1)} all-to-all(f32[8,8,256]{2,1,0:T(8,128)S(1)} %get-tuple-element.39), channel_id=1, replica_groups=mesh['wide'=4,'narrow'=8] {'narrow'}, dimensions={0} | all-to-all | bytes 131072 | tf_op jit(solution)/shard_map/all_to_all | solution.py:455
  49.2 0.0 collective-permute-done.2.other_ref
  49.2 1.6 %shard_map.96 = (f32[8,2048]{1,0:T(8,128)S(1)}, f32[8,8,256]{2,1,0:T(8,128)S(1)}, f32[16,1152]{1,0:T(8,128)S(1)}, f32[8,128]{1,0:T(8,128)S(1)}) custom-call(f32[8,8,256]{2,1,0:T(8,128)S(1)} %all_to_all.38.recv_ref, f32[16,1152]{1,0:T(8,128)S(1)} %get-tuple-element.40.half_ref, f32[16,1152]{1,0:T(8,128)S(1)} %collective-permute-done.2.other_ref, ...), custom_call_target="tpu_custom_call" | custom-call | tf_op jit(solution)/shard_map/pallas_call | solution.py:527
  50.8 0.4 collective-permute-start.3
  51.2 7.4 %all_to_all.39.recv_ref = f32[8,8,256]{2,1,0:T(8,128)S(1)} all-to-all(f32[8,8,256]{2,1,0:T(8,128)S(1)} %get-tuple-element.43), channel_id=1, replica_groups=mesh['wide'=4,'narrow'=8] {'narrow'}, dimensions={0} | all-to-all | bytes 131072 | tf_op jit(solution)/shard_map/all_to_all | solution.py:455
  58.6 5.0 %shard_map.97 = (f32[16,1024]{1,0:T(8,128)S(1)}, f32[16,1152]{1,0:T(8,128)S(1)}, f32[8,8,256]{2,1,0:T(8,128)S(1)}, f32[8,128]{1,0:T(8,128)S(1)}) custom-call(f32[8,8,256]{2,1,0:T(8,128)S(1)} %all_to_all.39.recv_ref, f32[16,1152]{1,0:T(8,128)S(1)} %get-tuple-element.44.half_ref, f32[16,1152]{1,0:T(8,128)S(1)} %collective-permute-done.3.other_ref, ...), custom_call_target="tpu_custom_call" | custom-call | tf_op jit(solution)/shard_map/pallas_call | solution.py:546
  63.5 1.6 %collective-permute-start.4 = (f32[16,1152]{1,0:T(8,128)S(1)}, f32[16,1152]{1,0:T(8,128)S(1)}, u32[]{:S(2)}, u32[]{:S(2)}) collective-permute-start(f32[16,1152]{1,0:T(8,128)S(1)} %get-tuple-element.47.refs_1_), channel_id=1, source_target_pairs={{0,8},{8,0},{16,24},{24,16},{1,9},{9,1},{17,25},{25,17},{2,10},{10... | collective-permute-start | bytes 221192 | tf_op jit(solution)/shard_map/ppermute | solution.py:452
  65.2 7.4 %all_to_all.40.refs_0_ = f32[8,8,256]{2,1,0:T(8,128)S(1)} all-to-all(f32[8,8,256]{2,1,0:T(8,128)S(1)} %get-tuple-element.46), channel_id=1, replica_groups=mesh['wide'=4,'narrow'=8] {'narrow'}, dimensions={0} | all-to-all | bytes 131072 | tf_op jit(solution)/shard_map/all_to_all | solution.py:455
  72.6 1.4 %shard_map.98 = (f32[8,2048]{1,0:T(8,128)S(1)}, f32[16,1152]{1,0:T(8,128)S(1)}, f32[8,128]{1,0:T(8,128)}) custom-call(f32[8,8,256]{2,1,0:T(8,128)S(1)} %all_to_all.40.refs_0_, f32[16,1152]{1,0:T(8,128)S(1)} %get-tuple-element.47.refs_1_, f32[16,1152]{1,0:T(8,128)S(1)} %collective-permute-done.4.refs_2_, s32[16,128]{1,0:T(8,128)S(1)} %get-tuple-element.41.given_ref.refs_3_), custom_call_target="tpu_custom_call" | custom-call | tf_op jit(solution)/shard_map/pallas_call | solution.py:527
  74.0 2.6 %collective-permute-start.5 = (f32[16,1152]{1,0:T(8,128)S(1)}, f32[16,1152]{1,0:T(8,128)S(1)}, u32[]{:S(2)}, u32[]{:S(2)}) collective-permute-start(f32[16,1152]{1,0:T(8,128)S(1)} %get-tuple-element.51.att2a), channel_id=1, source_target_pairs={{0,16},{8,24},{16,0},{24,8},{1,17},{9,25},{17,1},{25,9},{2,18},{10... | collective-permute-start | bytes 221192 | tf_op jit(solution)/shard_map/ppermute | solution.py:452
  76.5 3.6 %collective-permute-done.5.att2b = f32[16,1152]{1,0:T(8,128)S(1)} collective-permute-done((f32[16,1152]{1,0:T(8,128)S(1)}, f32[16,1152]{1,0:T(8,128)S(1)}, u32[]{:S(2)}, u32[]{:S(2)}) %collective-permute-start.5) | collective-permute-done | bytes 73760 | tf_op jit(solution)/shard_map/ppermute | solution.py:452
  80.1 0.3 shard_map.99
  80.4 10.4 %all_to_all.41 = f32[32,1,128]{2,1,0:T(1,128)S(1)} all-to-all(f32[32,1,128]{2,1,0:T(1,128)S(1)} %bitcast.15), channel_id=1, replica_groups=mesh['wide'=4,'narrow'=8] {'wide','narrow'}, dimensions={0} | all-to-all | bytes 32768 | tf_op jit(solution)/shard_map/all_to_all | solution.py:563
  90.9 0.9 shard_map.100
  (4 shorter events, 0.0 us)
Async XLA Ops:
  13.1 11.6 %collective-permute-start = (f32[16,1152]{1,0:T(8,128)S(1)}, f32[16,1152]{1,0:T(8,128)S(1)}, u32[]{:S(2)}, u32[]{:S(2)}) collective-permute-start(f32[16,1152]{1,0:T(8,128)S(1)} %get-tuple-element.31.half_ref), channel_id=1, source_target_pairs={{0,8},{8,0},{16,24},{24,16},{1,9},{9,1},{17,25},{25,17},{2,10},{10... | collective-permute-start | bytes 221192 | tf_op jit(solution)/shard_map/ppermute | solution.py:452
  26.3 10.0 %collective-permute-start.1 = (f32[16,1152]{1,0:T(8,128)S(1)}, f32[16,1152]{1,0:T(8,128)S(1)}, u32[]{:S(2)}, u32[]{:S(2)}) collective-permute-start(f32[16,1152]{1,0:T(8,128)S(1)} %get-tuple-element.35.half_ref), channel_id=1, source_target_pairs={{0,16},{8,24},{16,0},{24,8},{1,17},{9,25},{17,1},{25,9},{2,18},{10... | collective-permute-start | bytes 221192 | tf_op jit(solution)/shard_map/ppermute | solution.py:452
  41.4 7.9 %collective-permute-start.2 = (f32[16,1152]{1,0:T(8,128)S(1)}, f32[16,1152]{1,0:T(8,128)S(1)}, u32[]{:S(2)}, u32[]{:S(2)}) collective-permute-start(f32[16,1152]{1,0:T(8,128)S(1)} %get-tuple-element.40.half_ref), channel_id=1, source_target_pairs={{0,8},{8,0},{16,24},{24,16},{1,9},{9,1},{17,25},{25,17},{2,10},{10... | collective-permute-start | bytes 221192 | tf_op jit(solution)/shard_map/ppermute | solution.py:452
  50.8 7.8 %collective-permute-start.3 = (f32[16,1152]{1,0:T(8,128)S(1)}, f32[16,1152]{1,0:T(8,128)S(1)}, u32[]{:S(2)}, u32[]{:S(2)}) collective-permute-start(f32[16,1152]{1,0:T(8,128)S(1)} %get-tuple-element.44.half_ref), channel_id=1, source_target_pairs={{0,16},{8,24},{16,0},{24,8},{1,17},{9,25},{17,1},{25,9},{2,18},{10... | collective-permute-start | bytes 221192 | tf_op jit(solution)/shard_map/ppermute | solution.py:452
  63.5 9.0 %collective-permute-start.4 = (f32[16,1152]{1,0:T(8,128)S(1)}, f32[16,1152]{1,0:T(8,128)S(1)}, u32[]{:S(2)}, u32[]{:S(2)}) collective-permute-start(f32[16,1152]{1,0:T(8,128)S(1)} %get-tuple-element.47.refs_1_), channel_id=1, source_target_pairs={{0,8},{8,0},{16,24},{24,16},{1,9},{9,1},{17,25},{25,17},{2,10},{10... | collective-permute-start | bytes 221192 | tf_op jit(solution)/shard_map/ppermute | solution.py:452
  74.0 6.2 %collective-permute-start.5 = (f32[16,1152]{1,0:T(8,128)S(1)}, f32[16,1152]{1,0:T(8,128)S(1)}, u32[]{:S(2)}, u32[]{:S(2)}) collective-permute-start(f32[16,1152]{1,0:T(8,128)S(1)} %get-tuple-element.51.att2a), channel_id=1, source_target_pairs={{0,16},{8,24},{16,0},{24,8},{1,17},{9,25},{17,1},{25,9},{2,18},{10... | collective-permute-start | bytes 221192 | tf_op jit(solution)/shard_map/ppermute | solution.py:452

commit v3 on v2

--- a/solution.py
+++ b/solution.py
@@ -165,8 +165,10 @@
     table_ref, square_ref, pos_ref, seg_ref, order_ref, att_ref, send_ref,
     att_in, src_in, rhs_in, source_in, segment_in, count_in, blocks, ids, left, right, sems, int_sems,
 ):
-    groups = att_in.shape[0]
-    att_rows, src_rows = att_in.shape[1] * att_in.shape[3], src_in.shape[2]
+    groups, att_sets = att_in.shape[0], att_in.shape[1]
+    att_rows, src_rows = att_sets * 8, src_hbm.shape[1]
+    att_flat = att_in.reshape(groups * att_sets * LANE * 8, LANE)
+    src_flat = src_in.reshape(groups * LANE * 8, LANE)
     obs = table_ref.shape[2]
 
     def ints():
@@ -179,7 +181,7 @@
         cut = pl.ds(g * LANE, LANE)
         return [
             pltpu.make_async_copy(att_hbm.at[:, cut], att_in.at[g], sems.at[0, g]),
-            pltpu.make_async_copy(src_hbm.at[cut], src_in.at[g], sems.at[1, g]),
+            pltpu.make_async_copy(src_hbm.at[cut], src_in.at[g, :, 0:src_rows], sems.at[1, g]),
             pltpu.make_async_copy(rhs_hbm.at[cut], rhs_in.at[g], sems.at[2, g]),
         ]
 
@@ -215,9 +217,11 @@
             square_ref[...] += total
         for i in range(att_rows + src_rows):
             if i < att_rows:
-                values = att_in[g, i // 8, :, i % 8, :]
+                base = pl.multiple_of((g * att_sets + i // 8) * (LANE * 8), LANE * 8)
+                values = att_flat[pl.ds(base + i % 8, LANE, stride=8), :]
             else:
-                values = src_in[g, :, i - att_rows, :]
+                base = pl.multiple_of(g * (LANE * 8), LANE * 8)
+                values = src_flat[pl.ds(base + i - att_rows, LANE, stride=8), :]
             turned = values.T
             for half in range(2):
                 part = jnp.where(live[half], turned[half * obs : half * obs + obs], 0.0)
@@ -478,7 +482,7 @@
         ),
         [
             pltpu.VMEM((groups, att_rows // 8, LANE, 8, LANE), F32),
-            pltpu.VMEM((groups, LANE, src_rows, LANE), F32),
+            pltpu.VMEM((groups, LANE, 8, LANE), F32),
             pltpu.VMEM((groups, LANE, LANE), F32),
             pltpu.VMEM((tiles, LANE), I32),
             pltpu.VMEM((tiles, LANE), I32),

time: 92.1 us -> 86.9 us (0.944)
  Pallas kernels: 28.1 us -> 22.8 us
    pallas_call x1, Pallas kernels: 12.4 us -> 7.15 us  [on_device(): call(functools.partial(start_kernel, narrow), (sds((tiles, rows, obs, LAN...]
where the time goes in v3:
time: 86.9 us; the launch traced here: 86.5 us
  blocking collectives  48.5 us (56%)
  Pallas kernels  22.8 us (26%)
  starting transfers between devices  10.9 us (13%)
  waiting for transfers between devices  3.61 us (4%)
    all_to_all x5, blocking collectives, exchange(): return lax.all_to_all(values, 'narrow', 0, 0)  38.1 us
    ppermute x6, starting transfers between devices, across(): return lax.ppermute(values, 'wide', [(i, i ^ step) for i in range(wide)])  10.9 us
    all_to_all x1, blocking collectives, on_device(): dots = lax.all_to_all(dots, ('wide', 'narrow'), 0, 0, tiled=True)  10.4 us
    pallas_call x2, Pallas kernels, on_device(): call(functools.partial(product_kernel, narrow, first_time), (sds((16, SEG...  9.94 us
    pallas_call x1, Pallas kernels, on_device(): call(functools.partial(start_kernel, narrow), (sds((tiles, rows, obs, LAN...  7.15 us
    pallas_call x3, Pallas kernels, on_device(): call(whole, tuple(outs), [src_left, right_store])  4.56 us
    ppermute x6, waiting for transfers between devices, across(): return lax.ppermute(values, 'wide', [(i, i ^ step) for i in range(wide)])  3.61 us
  transfers between devices with their start and end apart: 6, of which 1 were waited for; matrix products, arithmetic and copies ran while one was open for 0% of the time, Pallas kernels for 0%

profile of v3, /device:TPU:0, one launch (start us, length us, event | category | flops | bytes accessed | tf_op | source)
XLA Modules:
  0.0 86.5 jit_solution(18069204009645288910)
XLA Ops:
  0.6 7.1 %shard_map.93 = (f32[16,21,64,128]{3,2,1,0:T(8,128)S(1)}, f32[8,128]{1,0:T(8,128)S(1)}, s32[16,128]{1,0:T(8,128)S(1)}, s32[16,128]{1,0:T(8,128)S(1)}, s32[16,128...) custom-call(f32[2,1024,8,128]{3,2,1,0:T(8,128)} %bitcast.16, f32[1024,5,128]{2,1,0:T(8,128)} %bitcast.17, ...), custom_call_target="tpu_custom_call" | custom-call | tf_op jit(solution)/shard_map/pallas_call | solution.py:472
  7.8 3.1 %collective-permute-start = (f32[16,1152]{1,0:T(8,128)S(1)}, f32[16,1152]{1,0:T(8,128)S(1)}, u32[]{:S(2)}, u32[]{:S(2)}) collective-permute-start(f32[16,1152]{1,0:T(8,128)S(1)} %get-tuple-element.31.half_ref), channel_id=1, source_target_pairs={{0,8},{8,0},{16,24},{24,16},{1,9},{9,1},{17,25},{25,17},{2,10},{10... | collective-permute-start | bytes 221192 | tf_op jit(solution)/shard_map/ppermute | solution.py:456
  10.9 8.5 %all_to_all.36.recv_ref = f32[8,8,256]{2,1,0:T(8,128)S(1)} all-to-all(f32[8,8,256]{2,1,0:T(8,128)S(1)} %get-tuple-element.30), channel_id=1, replica_groups=mesh['wide'=4,'narrow'=8] {'narrow'}, dimensions={0} | all-to-all | bytes 131072 | tf_op jit(solution)/shard_map/all_to_all | solution.py:459
  19.4 0.0 collective-permute-done.other_ref
  19.4 1.6 %shard_map.94 = (f32[8,2048]{1,0:T(8,128)S(1)}, f32[8,8,256]{2,1,0:T(8,128)S(1)}, f32[16,1152]{1,0:T(8,128)S(1)}, s32[16,128]{1,0:T(8,128)S(1)}) custom-call(f32[8,8,256]{2,1,0:T(8,128)S(1)} %all_to_all.36.recv_ref, f32[16,1152]{1,0:T(8,128)S(1)} %get-tuple-element.31.half_ref, f32[16,1152]{1,0:T(8,128)S(1)} %collective-permute-done.other_ref, ...), custom_call_target="tpu_custom_call" | custom-call | tf_op jit(solution)/shard_map/pallas_call | solution.py:531
  21.0 2.7 %collective-permute-start.1 = (f32[16,1152]{1,0:T(8,128)S(1)}, f32[16,1152]{1,0:T(8,128)S(1)}, u32[]{:S(2)}, u32[]{:S(2)}) collective-permute-start(f32[16,1152]{1,0:T(8,128)S(1)} %get-tuple-element.35.half_ref), channel_id=1, source_target_pairs={{0,16},{8,24},{16,0},{24,8},{1,17},{9,25},{17,1},{25,9},{2,18},{10... | collective-permute-start | bytes 221192 | tf_op jit(solution)/shard_map/ppermute | solution.py:456
  23.7 7.4 %all_to_all.37.recv_ref = f32[8,8,256]{2,1,0:T(8,128)S(1)} all-to-all(f32[8,8,256]{2,1,0:T(8,128)S(1)} %get-tuple-element.34), channel_id=1, replica_groups=mesh['wide'=4,'narrow'=8] {'narrow'}, dimensions={0} | all-to-all | bytes 131072 | tf_op jit(solution)/shard_map/all_to_all | solution.py:459
  31.1 0.0 collective-permute-done.1.other_ref
  31.1 5.0 %shard_map.95 = (f32[16,1024]{1,0:T(8,128)S(1)}, f32[16,1152]{1,0:T(8,128)S(1)}, f32[8,8,256]{2,1,0:T(8,128)S(1)}, f32[8,128]{1,0:T(8,128)}) custom-call(f32[8,8,256]{2,1,0:T(8,128)S(1)} %all_to_all.37.recv_ref, f32[16,1152]{1,0:T(8,128)S(1)} %get-tuple-element.35.half_ref, f32[16,1152]{1,0:T(8,128)S(1)} %collective-permute-done.1.other_ref, ...), custom_call_target="tpu_custom_call" | custom-call | tf_op jit(solution)/shard_map/pallas_call | solution.py:550
  36.1 0.5 collective-permute-start.2
  36.6 7.4 %all_to_all.38.recv_ref = f32[8,8,256]{2,1,0:T(8,128)S(1)} all-to-all(f32[8,8,256]{2,1,0:T(8,128)S(1)} %get-tuple-element.39), channel_id=1, replica_groups=mesh['wide'=4,'narrow'=8] {'narrow'}, dimensions={0} | all-to-all | bytes 131072 | tf_op jit(solution)/shard_map/all_to_all | solution.py:459
  44.0 1.6 %shard_map.96 = (f32[8,2048]{1,0:T(8,128)S(1)}, f32[8,8,256]{2,1,0:T(8,128)S(1)}, f32[16,1152]{1,0:T(8,128)S(1)}, f32[8,128]{1,0:T(8,128)S(1)}) custom-call(f32[8,8,256]{2,1,0:T(8,128)S(1)} %all_to_all.38.recv_ref, f32[16,1152]{1,0:T(8,128)S(1)} %get-tuple-element.40.half_ref, f32[16,1152]{1,0:T(8,128)S(1)} %collective-permute-done.2.other_ref, ...), custom_call_target="tpu_custom_call" | custom-call | tf_op jit(solution)/shard_map/pallas_call | solution.py:531
  45.5 0.4 collective-permute-start.3
  45.9 7.4 %all_to_all.39.recv_ref = f32[8,8,256]{2,1,0:T(8,128)S(1)} all-to-all(f32[8,8,256]{2,1,0:T(8,128)S(1)} %get-tuple-element.43), channel_id=1, replica_groups=mesh['wide'=4,'narrow'=8] {'narrow'}, dimensions={0} | all-to-all | bytes 131072 | tf_op jit(solution)/shard_map/all_to_all | solution.py:459
  53.3 0.0 collective-permute-done.3.other_ref
  53.3 4.9 %shard_map.97 = (f32[16,1024]{1,0:T(8,128)S(1)}, f32[16,1152]{1,0:T(8,128)S(1)}, f32[8,8,256]{2,1,0:T(8,128)S(1)}, f32[8,128]{1,0:T(8,128)S(1)}) custom-call(f32[8,8,256]{2,1,0:T(8,128)S(1)} %all_to_all.39.recv_ref, f32[16,1152]{1,0:T(8,128)S(1)} %get-tuple-element.44.half_ref, f32[16,1152]{1,0:T(8,128)S(1)} %collective-permute-done.3.other_ref, ...), custom_call_target="tpu_custom_call" | custom-call | tf_op jit(solution)/shard_map/pallas_call | solution.py:550
  58.3 1.6 %collective-permute-start.4 = (f32[16,1152]{1,0:T(8,128)S(1)}, f32[16,1152]{1,0:T(8,128)S(1)}, u32[]{:S(2)}, u32[]{:S(2)}) collective-permute-start(f32[16,1152]{1,0:T(8,128)S(1)} %get-tuple-element.47.refs_1_), channel_id=1, source_target_pairs={{0,8},{8,0},{16,24},{24,16},{1,9},{9,1},{17,25},{25,17},{2,10},{10... | collective-permute-start | bytes 221192 | tf_op jit(solution)/shard_map/ppermute | solution.py:456
  59.9 7.4 %all_to_all.40.refs_0_ = f32[8,8,256]{2,1,0:T(8,128)S(1)} all-to-all(f32[8,8,256]{2,1,0:T(8,128)S(1)} %get-tuple-element.46), channel_id=1, replica_groups=mesh['wide'=4,'narrow'=8] {'narrow'}, dimensions={0} | all-to-all | bytes 131072 | tf_op jit(solution)/shard_map/all_to_all | solution.py:459
  67.3 1.4 %shard_map.98 = (f32[8,2048]{1,0:T(8,128)S(1)}, f32[16,1152]{1,0:T(8,128)S(1)}, f32[8,128]{1,0:T(8,128)}) custom-call(f32[8,8,256]{2,1,0:T(8,128)S(1)} %all_to_all.40.refs_0_, f32[16,1152]{1,0:T(8,128)S(1)} %get-tuple-element.47.refs_1_, f32[16,1152]{1,0:T(8,128)S(1)} %collective-permute-done.4.refs_2_, s32[16,128]{1,0:T(8,128)S(1)} %get-tuple-element.41.given_ref.refs_3_), custom_call_target="tpu_custom_call" | custom-call | tf_op jit(solution)/shard_map/pallas_call | solution.py:531
  68.7 2.6 %collective-permute-start.5 = (f32[16,1152]{1,0:T(8,128)S(1)}, f32[16,1152]{1,0:T(8,128)S(1)}, u32[]{:S(2)}, u32[]{:S(2)}) collective-permute-start(f32[16,1152]{1,0:T(8,128)S(1)} %get-tuple-element.51.att2a), channel_id=1, source_target_pairs={{0,16},{8,24},{16,0},{24,8},{1,17},{9,25},{17,1},{25,9},{2,18},{10... | collective-permute-start | bytes 221192 | tf_op jit(solution)/shard_map/ppermute | solution.py:456
  71.3 3.6 %collective-permute-done.5.att2b = f32[16,1152]{1,0:T(8,128)S(1)} collective-permute-done((f32[16,1152]{1,0:T(8,128)S(1)}, f32[16,1152]{1,0:T(8,128)S(1)}, u32[]{:S(2)}, u32[]{:S(2)}) %collective-permute-start.5) | collective-permute-done | bytes 73760 | tf_op jit(solution)/shard_map/ppermute | solution.py:456
  74.9 0.3 shard_map.99
  75.2 10.4 %all_to_all.41 = f32[32,1,128]{2,1,0:T(1,128)S(1)} all-to-all(f32[32,1,128]{2,1,0:T(1,128)S(1)} %bitcast.15), channel_id=1, replica_groups=mesh['wide'=4,'narrow'=8] {'wide','narrow'}, dimensions={0} | all-to-all | bytes 32768 | tf_op jit(solution)/shard_map/all_to_all | solution.py:567
  85.6 0.9 %shard_map.100 = (f32[5,2048]{1,0:T(8,128)}, f32[16,1024]{1,0:T(8,128)}, f32[5,2048]{1,0:T(8,128)}, f32[16,1024]{1,0:T(8,128)}) custom-call(f32[32,128]{1,0:T(8,128)S(1)} %bitcast.14, f32[8,128]{1,0:T(8,128)S(1)} %get-tuple-element.53.scale_ref, f32[8,2048]{1,0:T(8,128)S(1)} %get-tuple-element.33.src0, f32[8,2048]{1,0:T(8,128)S(1)} %get-tuple-element.42.src1, ...), custom_call_target="tpu_custom_call" | custom-call | tf_op jit(solution)/shard_map/pallas_call | solution.py:568
  (4 shorter events, 0.0 us)
Async XLA Ops:
  7.8 11.6 %collective-permute-start = (f32[16,1152]{1,0:T(8,128)S(1)}, f32[16,1152]{1,0:T(8,128)S(1)}, u32[]{:S(2)}, u32[]{:S(2)}) collective-permute-start(f32[16,1152]{1,0:T(8,128)S(1)} %get-tuple-element.31.half_ref), channel_id=1, source_target_pairs={{0,8},{8,0},{16,24},{24,16},{1,9},{9,1},{17,25},{25,17},{2,10},{10... | collective-permute-start | bytes 221192 | tf_op jit(solution)/shard_map/ppermute | solution.py:456
  21.0 10.0 %collective-permute-start.1 = (f32[16,1152]{1,0:T(8,128)S(1)}, f32[16,1152]{1,0:T(8,128)S(1)}, u32[]{:S(2)}, u32[]{:S(2)}) collective-permute-start(f32[16,1152]{1,0:T(8,128)S(1)} %get-tuple-element.35.half_ref), channel_id=1, source_target_pairs={{0,16},{8,24},{16,0},{24,8},{1,17},{9,25},{17,1},{25,9},{2,18},{10... | collective-permute-start | bytes 221192 | tf_op jit(solution)/shard_map/ppermute | solution.py:456
  36.1 7.9 %collective-permute-start.2 = (f32[16,1152]{1,0:T(8,128)S(1)}, f32[16,1152]{1,0:T(8,128)S(1)}, u32[]{:S(2)}, u32[]{:S(2)}) collective-permute-start(f32[16,1152]{1,0:T(8,128)S(1)} %get-tuple-element.40.half_ref), channel_id=1, source_target_pairs={{0,8},{8,0},{16,24},{24,16},{1,9},{9,1},{17,25},{25,17},{2,10},{10... | collective-permute-start | bytes 221192 | tf_op jit(solution)/shard_map/ppermute | solution.py:456
  45.5 7.8 %collective-permute-start.3 = (f32[16,1152]{1,0:T(8,128)S(1)}, f32[16,1152]{1,0:T(8,128)S(1)}, u32[]{:S(2)}, u32[]{:S(2)}) collective-permute-start(f32[16,1152]{1,0:T(8,128)S(1)} %get-tuple-element.44.half_ref), channel_id=1, source_target_pairs={{0,16},{8,24},{16,0},{24,8},{1,17},{9,25},{17,1},{25,9},{2,18},{10... | collective-permute-start | bytes 221192 | tf_op jit(solution)/shard_map/ppermute | solution.py:456
  58.3 9.0 %collective-permute-start.4 = (f32[16,1152]{1,0:T(8,128)S(1)}, f32[16,1152]{1,0:T(8,128)S(1)}, u32[]{:S(2)}, u32[]{:S(2)}) collective-permute-start(f32[16,1152]{1,0:T(8,128)S(1)} %get-tuple-element.47.refs_1_), channel_id=1, source_target_pairs={{0,8},{8,0},{16,24},{24,16},{1,9},{9,1},{17,25},{25,17},{2,10},{10... | collective-permute-start | bytes 221192 | tf_op jit(solution)/shard_map/ppermute | solution.py:456
  68.7 6.2 %collective-permute-start.5 = (f32[16,1152]{1,0:T(8,128)S(1)}, f32[16,1152]{1,0:T(8,128)S(1)}, u32[]{:S(2)}, u32[]{:S(2)}) collective-permute-start(f32[16,1152]{1,0:T(8,128)S(1)} %get-tuple-element.51.att2a), channel_id=1, source_target_pairs={{0,16},{8,24},{16,0},{24,8},{1,17},{9,25},{17,1},{25,9},{2,18},{10... | collective-permute-start | bytes 221192 | tf_op jit(solution)/shard_map/ppermute | solution.py:456

commit v4 on v3

--- a/solution.py
+++ b/solution.py
@@ -6,6 +6,7 @@
 from jax.experimental import pallas as pl
 from jax.experimental.pallas import tpu as pltpu
 from jax.sharding import PartitionSpec as P
+
 
 SRC_DEV = 2048
 SEG_DEV = 1024
@@ -82,7 +83,6 @@
         pos = jnp.where(owner == m, m * cap + rank[m * tiles : (m + 1) * tiles], pos)
     pos_ref[...] = pos
     levels = tiles * LANE // HIGH
-    high_at = row_iota(HIGH)
     lane = lane_iota(1).astype(F32)
     for t in range(tiles):
         here = pos[t : t + 1]
@@ -98,9 +98,7 @@
             left[part * levels : (part + 1) * levels, t * LANE : (t + 1) * LANE] = jnp.where(
                 level, piece, 0.0
             ).astype(BF16)
-        right[:, t * LANE : (t + 1) * LANE] = jnp.where(high_at == here % HIGH, 1.0, 0.0).astype(
-            BF16
-        )
+    mark_high(right, lambda t: pos[t : t + 1], tiles)
     found = dot_lanes(left[0 : 4 * levels, :], right[...])
     tile_at, lane_at = found[:levels], found[levels : 2 * levels]
     order = (tile_at * LANE + lane_at).astype(I32)
@@ -113,16 +111,21 @@
             ids_ref[row : row + 1, :] = ids[level : level + 1, cut]
 
 
+def mark_high(right, rows_of, tiles):
+    high_at = row_iota(HIGH)
+    for t in range(tiles):
+        here = rows_of(t) & (HIGH - 1)
+        right[:, t * LANE : (t + 1) * LANE] = jnp.where(high_at == here, 1.0, 0.0).astype(BF16)
+
+
 def scatter_att(blocks, seg_ref, out_ref, left, right):
     tiles = seg_ref.shape[0]
     levels = SEG_DEV // HIGH
-    high_at = row_iota(HIGH)
 
     def fill(t, carry):
         here = seg_ref[pl.ds(t, 1), :]
         column = pl.multiple_of(t * LANE, LANE)
         spread_rows(left, blocks[t, 0:16, :], here // HIGH, column, levels)
-        right[:, pl.ds(column, LANE)] = jnp.where(high_at == here % HIGH, 1.0, 0.0).astype(BF16)
         return carry
 
     lax.fori_loop(0, tiles, fill, 0)
@@ -162,8 +165,9 @@
 def start_kernel(
     narrow,
     att_hbm, src_hbm, rhs_hbm, source_hbm, segment_hbm, count_hbm,
-    table_ref, square_ref, pos_ref, seg_ref, order_ref, att_ref, send_ref,
-    att_in, src_in, rhs_in, source_in, segment_in, count_in, blocks, ids, left, right, sems, int_sems,
+    table_hbm, square_ref, pos_ref, seg_ref, order_ref, right, att_ref, send_ref,
+    table_ref, att_in, src_in, rhs_in, source_in, segment_in, count_in, blocks, ids, left, sems, int_sems,
+    out_sems,
 ):
     groups, att_sets = att_in.shape[0], att_in.shape[1]
     att_rows, src_rows = att_sets * 8, src_hbm.shape[1]
@@ -184,6 +188,14 @@
             pltpu.make_async_copy(src_hbm.at[cut], src_in.at[g, :, 0:src_rows], sems.at[1, g]),
             pltpu.make_async_copy(rhs_hbm.at[cut], rhs_in.at[g], sems.at[2, g]),
         ]
+
+    def store(g):
+        cut = pl.ds(g * 2, 2)
+        return pltpu.make_async_copy(table_ref.at[cut], table_hbm.at[cut], out_sems.at[g])
+
+    def finish(g, carry):
+        store(g).wait()
+        return carry
 
     def begin(g, carry):
         for one in loads(g):
@@ -198,6 +210,7 @@
     count_in[...] = to_tiles(count_in[...])
     square_ref[...] = jnp.zeros_like(square_ref)
     rank_blocks(narrow, source_in, segment_in, pos_ref, seg_ref, order_ref, ids, left, right)
+    mark_high(right, lambda t: seg_ref[t : t + 1, :], seg_ref.shape[0])
     place = row_iota(obs)
 
     def turn(g, carry):
@@ -230,6 +243,7 @@
         for half in range(2):
             rest = 24 - att_rows - src_rows
             blocks[g * 2 + half, 24 - rest : 24, :] = jnp.zeros((rest, LANE), F32)
+        store(g).start()
         return carry
 
     lax.fori_loop(0, groups, turn, 0)
@@ -244,41 +258,39 @@
         lambda t: jnp.where(row == 5, ids[t : t + 1, :], 0.0),
         send_ref,
     )
-
-
-def owner_kernel(
-    narrow, first, recv_ref, half_ref, other_ref, given_ref, src_ref, back_ref, att_ref, out_ref,
-    left, right,
-):
-    tiles, cap = given_ref.shape[0], recv_ref.shape[2]
+    lax.fori_loop(0, groups, finish, 0)
+
+
+def owner_kernel(narrow, first, last, *refs):
+    if first:
+        recv_ref, src_ref, back_ref, index_ref, right, left = refs
+    elif last:
+        recv_ref, index_ref, right, src_ref, left = refs
+    else:
+        recv_ref, index_ref, right, src_ref, back_ref, known_ref, left = refs
+    tiles, cap = index_ref.shape[0], recv_ref.shape[2]
     per = cap // LANE
     levels = SRC_DEV // HIGH
-    high_at = row_iota(HIGH)
     keep = row_iota(8) < 5
-    att_ref[...] = half_ref[...] + other_ref[...]
     if first:
         for t in range(tiles):
-            out_ref[t : t + 1, :] = entry(recv_ref, per, t)[5:6].astype(I32)
-        index_ref = out_ref
-    else:
-        index_ref = given_ref
+            index_ref[t : t + 1, :] = entry(recv_ref, per, t)[5:6].astype(I32)
+        mark_high(right, lambda t: index_ref[t : t + 1, :], tiles)
+    elif not last:
         known = recv_ref[0, :, 0:LANE]
         for n in range(1, narrow):
             known = known + recv_ref[n, :, 0:LANE]
-        out_ref[...] = known
+        known_ref[...] = known
     for t in range(tiles):
         here = index_ref[t : t + 1, :]
         values = jnp.where(keep, entry(recv_ref, per, t), 0.0)
         spread_rows(left, values, here // HIGH, t * LANE, levels)
-        right[:, t * LANE : (t + 1) * LANE] = jnp.where(high_at == here % HIGH, 1.0, 0.0).astype(
-            BF16
-        )
     sums = dot_lanes(left[...], right[...])
     size = 8 * levels
     sums = sums[:size] + (sums[size : 2 * size] + sums[2 * size :])
     for level in range(levels):
         src_ref[:, level * HIGH : (level + 1) * HIGH] = sums[level * 8 : (level + 1) * 8]
-    if back_ref is None:
+    if last:
         return
     square = jnp.sum(src_ref[...] * src_ref[...]) if first else 0.0
     mark = jnp.where((row_iota(8) == 6) & (lane_iota(8) == 0), square, 0.0)
@@ -297,57 +309,66 @@
 
 
 def product_kernel(
-    narrow, first, recv_ref, half_ref, other_ref, known_ref, pos_ref, seg_ref, order_ref, table_ref,
-    full_ref, att_ref, send_ref, scale_ref, vec, blocks, left, right,
+    narrow, first, recv_ref, half_ref, later_ref, known_ref, pos_ref, seg_ref, order_ref, right,
+    table_hbm, full_ref, att_ref, send_ref, scale_ref, vec, blocks, left, table_ref, sems,
 ):
     tiles, rows = pos_ref.shape[0], table_ref.shape[1]
+
+    def load(t):
+        return pltpu.make_async_copy(table_hbm.at[t], table_ref.at[t], sems.at[t])
+
+    def begin(t, carry):
+        load(t).start()
+        return carry
+
+    lax.fori_loop(0, tiles, begin, 0)
     cap = recv_ref.shape[2]
     per = cap // LANE
-
-    full = half_ref[...] + other_ref[...]
+    full = half_ref[...] + later_ref[...]
     full_ref[...] = full[:, :SEG_DEV]
     notes = full[0:1, SEG_DEV:]
+    lane, row = lane_iota(8), row_iota(8)
+    send_note = jnp.zeros((8, LANE), F32)
+    att_note = jnp.zeros((16, LANE), F32)
     if first:
         scale = jnp.ones((1, 1), F32)
         square_src = recv_ref[0, 6:7, 0:LANE]
         for n in range(1, narrow):
             square_src = square_src + recv_ref[n, 6:7, 0:LANE]
-        square_src = lane_value(square_src, 0)
+        att_note = jnp.where(lane_iota(16) == 1, lane_value(square_src, 0), 0.0)
         square_att = jnp.sum(full[:, :SEG_DEV] * full[:, :SEG_DEV], keepdims=True)
-        rhs_square = lane_value(notes, 0)
-        att_note = jnp.where(lane_iota(16) == 1, square_src, 0.0)
-        send_note = jnp.where(
-            row_iota(8) == 6,
-            jnp.where(lane_iota(8) == 0, rhs_square, jnp.where(lane_iota(8) == 1, square_att, 0.0)),
-            0.0,
-        )
+        send_note = jnp.where(lane == 0, lane_value(notes, 0), 0.0)
+        send_note = jnp.where(lane == 1, square_att, send_note)
+        send_note = jnp.where(row == 6, send_note, 0.0)
     else:
         known = known_ref[6:7, :]
         square = lane_value(notes, 1) + lane_value(known, 1)
         scale = lane_value(known, 0) / square
-        att_note = jnp.zeros((16, LANE), F32)
-        send_note = jnp.zeros((8, LANE), F32)
     scale_ref[...] = jnp.broadcast_to(scale, (8, LANE))
+    att_ref[:, SEG_DEV:] = att_note
 
     def gather(t, carry):
-        where_src = pos_ref[pl.ds(t, 1), :]
         where_att = seg_ref[pl.ds(t, 1), :]
-        for top in range(0, 16, 8):
-            picked = pick(
-                lambda c: full_ref[top : top + 8, c * LANE : (c + 1) * LANE],
-                SEG_DEV // LANE,
-                where_att,
-            )
-            vec[t, top : top + 8, :] = picked * scale
-        vec[t, 16:24, :] = pick(lambda c: entry(recv_ref, per, c), tiles, where_src) * scale
+        for top in range(0, 24, 8):
+            if top < 16:
+                picked = pick(
+                    lambda c: full_ref[top : top + 8, c * LANE : (c + 1) * LANE],
+                    SEG_DEV // LANE,
+                    where_att,
+                )
+            else:
+                picked = pick(lambda c: entry(recv_ref, per, c), tiles, pos_ref[pl.ds(t, 1), :])
+            vec[t, top : top + 8, :] = picked if first else picked * scale
         return carry
 
     lax.fori_loop(0, tiles, gather, 0)
 
     def multiply(t, carry):
-        image = table_ref[t, 0] * vec[t, 0:1, :]
-        for i in range(1, rows):
-            image = image + table_ref[t, i] * vec[t, i : i + 1, :]
+        load(t).wait()
+        image = None
+        for i in range(rows):
+            part = table_ref[t, i] * vec[t, i : i + 1, :]
+            image = part if image is None else image + part
         for i in range(rows):
             blocks[t, i : i + 1, :] = jnp.sum(table_ref[t, i] * image, axis=0, keepdims=True)
         blocks[t, rows:24, :] = jnp.zeros((24 - rows, LANE), F32)
@@ -355,7 +376,6 @@
 
     lax.fori_loop(0, tiles, multiply, 0)
     scatter_att(blocks, seg_ref, att_ref, left, right)
-    att_ref[:, SEG_DEV:] = att_note
     send_sorted(narrow, blocks, order_ref, lambda t: send_note, send_ref)
 
 
@@ -430,7 +450,7 @@
     return pltpu.with_memory_space_constraint(values, pltpu.HBM)
 
 
-def call(kernel, outs, scratch=(), limit=24, **more):
+def call(kernel, outs, scratch=(), limit=8, **more):
     return pl.pallas_call(
         kernel,
         out_shape=outs,
@@ -462,25 +482,28 @@
     att_view = att_design.reshape(att_rows // 8, 8, columns, LANE).transpose(0, 2, 1, 3)
     src_view = src_design.reshape(src_rows, columns, LANE).transpose(1, 0, 2)
 
-    right_store = pltpu.VMEM((HIGH, blocks), BF16)
+    right_shape = sds((HIGH, blocks), BF16)
     att_left = pltpu.VMEM((3 * 16 * SEG_DEV // HIGH, blocks), BF16)
     src_left = pltpu.VMEM((3 * 8 * SRC_DEV // HIGH, blocks), BF16)
     tile_int = sds((tiles, LANE), I32)
     send_shape = sds((narrow, 8, cap))
     att_shape = sds((16, SEG_DEV + LANE))
     src_shape = sds((8, SRC_DEV))
-    table, square, pos, seg, order, part, send = call(
+    table_shape = (tiles, rows, obs, LANE)
+    table, square, pos, seg, order, att_right, part, send = call(
         functools.partial(start_kernel, narrow),
         (
-            sds((tiles, rows, obs, LANE)),
+            pltpu.HBM(table_shape, F32),
             sds((8, LANE)),
             tile_int,
             tile_int,
             tile_int,
+            right_shape,
             att_shape,
             send_shape,
         ),
         [
+            pltpu.VMEM(table_shape, F32),
             pltpu.VMEM((groups, att_rows // 8, LANE, 8, LANE), F32),
             pltpu.VMEM((groups, LANE, 8, LANE), F32),
             pltpu.VMEM((groups, LANE, LANE), F32),
@@ -490,11 +513,14 @@
             pltpu.VMEM((tiles, 24, LANE), F32),
             pltpu.VMEM((tiles, LANE), F32),
             att_left,
-            right_store,
             pltpu.SemaphoreType.DMA((3, groups)),
             pltpu.SemaphoreType.DMA((3,)),
+            pltpu.SemaphoreType.DMA((groups,)),
         ],
         in_specs=[pl.BlockSpec(memory_space=pltpu.HBM)] * 6,
+        out_specs=(pl.BlockSpec(memory_space=pltpu.HBM),)
+        + (pl.BlockSpec(memory_space=pltpu.VMEM),) * 7,
+        limit=32,
     )(
         *map(
             in_hbm,
@@ -509,33 +535,15 @@
         )
     )
 
-    given = None
     results = []
-    scale = None
+    note = jnp.zeros((8, LANE), F32)
+    owners = None
     for step in range(3):
+        first_time, last_time = step == 0, step == 2
         other = across(part, 1)
         arrived = exchange(send)
-        first_time = step == 0
-        last_time = step == 2
-        outs = [src_shape]
-        if not last_time:
-            outs.append(send_shape)
-        outs.append(att_shape)
-        outs.append(tile_int if first_time else sds((8, LANE)))
-        kernel = functools.partial(owner_kernel, narrow, first_time)
-        if last_time:
-            whole = lambda *refs, k=kernel: k(*refs[:5], None, *refs[5:])
-        else:
-            whole = kernel
-        given_in = seg if first_time else given
-        made = call(whole, tuple(outs), [src_left, right_store])(arrived, part, other, given_in)
-        src_sum, half, note = made[0], made[-2], made[-1]
-        if first_time:
-            given = note
-            note = jnp.zeros((8, LANE), F32)
+        total, jump = part + other, 2
         later = None
-        total = half
-        jump = 2
         while jump < wide:
             if later is not None:
                 total = total + later
@@ -543,10 +551,20 @@
             jump *= 2
         if later is None:
             later = jnp.zeros_like(total)
-        if last_time:
+        kernel = functools.partial(owner_kernel, narrow, first_time, last_time)
+        if first_time:
+            src_sum, back, *owners = call(
+                kernel, (src_shape, send_shape, tile_int, right_shape), [src_left]
+            )(arrived)
+        elif last_time:
+            src_sum = call(kernel, src_shape, [src_left])(arrived, *owners)
             results.append((src_sum, total, later))
             break
-        back = exchange(made[1])
+        else:
+            src_sum, back, note = call(
+                kernel, (src_shape, send_shape, sds((8, LANE))), [src_left]
+            )(arrived, *owners)
+        back = exchange(back)
         att_sum, part, send, scale = call(
             functools.partial(product_kernel, narrow, first_time),
             (sds((16, SEG_DEV)), att_shape, send_shape, sds((8, LANE))),
@@ -554,11 +572,14 @@
                 pltpu.VMEM((tiles, 24, LANE), F32),
                 pltpu.VMEM((tiles, 24, LANE), F32),
                 att_left,
-                right_store,
+                pltpu.VMEM(table_shape, F32),
+                pltpu.SemaphoreType.DMA((tiles,)),
             ],
-        )(back, total, later, note, pos, seg, order, table)
+            in_specs=[pl.BlockSpec(memory_space=pltpu.VMEM)] * 8
+            + [pl.BlockSpec(memory_space=pltpu.HBM)],
+            limit=20,
+        )(back, total, later, note, pos, seg, order, att_right, in_hbm(table))
         results.append((src_sum, att_sum))
-
     weight = jnp.where(lax.axis_index("wide") == 0, 1.0, 0.0).astype(F32) * jnp.ones((8, LANE), F32)
     (src0, att0), (src1, att1), (src2, att2a, att2b) = results
     dots, att2 = call(dots_kernel, (sds((devices, LANE)), sds((16, SEG_DEV))))(
@@ -581,6 +602,7 @@
     both = ("wide", "narrow")
     in_specs = (P(None, both), P(None, both), P(both), P(both), P(both), P(both))
     out_specs = (P(None, both), P(None, "narrow"), P(None, both), P(None, "narrow"))
+
     return jax.shard_map(
         on_device, mesh=mesh, in_specs=in_specs, out_specs=out_specs, check_vma=False
     )

time: 86.9 us -> 86.3 us (level)
  blocking collectives: 48.5 us -> 23.7 us
  starting transfers between devices: 10.9 us -> 23.6 us
  waiting for transfers between devices: 3.61 us -> 12.3 us
  Pallas kernels: 22.8 us -> 25.3 us
    all_to_all x5 -> x2, blocking collectives: 38.1 us -> 14.8 us  [exchange(): return lax.all_to_all(values, 'narrow', 0, 0)]
    all_to_all x0 -> x3, starting transfers between devices: none -> 10.4 us  [exchange(): return lax.all_to_all(values, 'narrow', 0, 0)]
    all_to_all x0 -> x3, waiting for transfers between devices: none -> 9.02 us  [exchange(): return lax.all_to_all(values, 'narrow', 0, 0)]
    ppermute x6, starting transfers between devices: 10.9 us -> 13.2 us  [across(): return lax.ppermute(values, 'wide', [(i, i ^ step) for i in range(wide)])]
    pallas_call x2, Pallas kernels: 9.94 us -> 11.7 us  [on_device(): call(functools.partial(product_kernel, narrow, first_time), (sds((16, SEG...]
    all_to_all x1, blocking collectives: 10.4 us -> 8.92 us  [on_device(): dots = lax.all_to_all(dots, ('wide', 'narrow'), 0, 0, tiled=True)]
  transfers between devices with their start and end apart: 6 -> 9, of which waited for: 1 -> 5; matrix products, arithmetic and copies ran while one was open for 0% -> 0% of each run, Pallas kernels for 0% -> 4%
where the time goes in v4:
time: 86.3 us; the launch traced here: 85.8 us
  Pallas kernels  25.3 us (29%)
  blocking collectives  23.7 us (27%)
  starting transfers between devices  23.6 us (27%)
  waiting for transfers between devices  12.3 us (14%)
    all_to_all x2, blocking collectives, exchange(): return lax.all_to_all(values, 'narrow', 0, 0)  14.8 us
    ppermute x6, starting transfers between devices, across(): return lax.ppermute(values, 'wide', [(i, i ^ step) for i in range(wide)])  13.2 us
    pallas_call x2, Pallas kernels, on_device(): call(functools.partial(product_kernel, narrow, first_time), (sds((16, SEG...  11.7 us
    all_to_all x3, starting transfers between devices, exchange(): return lax.all_to_all(values, 'narrow', 0, 0)  10.4 us
    all_to_all x3, waiting for transfers between devices, exchange(): return lax.all_to_all(values, 'narrow', 0, 0)  9.02 us
    pallas_call x1, Pallas kernels, on_device(): call(functools.partial(start_kernel, narrow), (pltpu.HBM(table_shape, F32...  8.95 us
    all_to_all x1, blocking collectives, on_device(): dots = lax.all_to_all(dots, ('wide', 'narrow'), 0, 0, tiled=True)  8.92 us
    ppermute x6, waiting for transfers between devices, across(): return lax.ppermute(values, 'wide', [(i, i ^ step) for i in range(wide)])  3.33 us
  transfers between devices with their start and end apart: 9, of which 5 were waited for; matrix products, arithmetic and copies ran while one was open for 0% of the time, Pallas kernels for 4%

profile of v4, /device:TPU:0, one launch (start us, length us, event | category | flops | bytes accessed | tf_op | source)
XLA Modules:
  0.0 85.8 jit_solution(6437062330981411034)
XLA Ops:
  0.6 9.0 %shard_map.93 = (f32[16,21,64,128]{3,2,1,0:T(8,128)}, f32[8,128]{1,0:T(8,128)S(1)}, s32[16,128]{1,0:T(8,128)S(1)}, s32[16,128]{1,0:T(8,128)S(1)}, s32[16,128]{1,...) custom-call(f32[2,1024,8,128]{3,2,1,0:T(8,128)} %bitcast.16, ...), custom_call_target="tpu_custom_call" | custom-call | tf_op jit(solution)/shard_map/pallas_call | solution.py:493
  9.6 3.1 %collective-permute-start = (f32[16,1152]{1,0:T(8,128)S(1)}, f32[16,1152]{1,0:T(8,128)S(1)}, u32[]{:S(2)}, u32[]{:S(2)}) collective-permute-start(f32[16,1152]{1,0:T(8,128)S(1)} %get-tuple-element.31), channel_id=1, source_target_pairs={{0,8},{8,0},{16,24},{24,16},{1,9},{9,1},{17,25},{25,17},{2,10},{10... | collective-permute-start | bytes 221192 | tf_op jit(solution)/shard_map/ppermute | solution.py:476
  12.7 3.7 %all-to-all-start = ((f32[8,8,256]{2,1,0:T(8,128)}), f32[8,8,256]{2,1,0:T(8,128)S(1)}, u32[]{:S(2)}, u32[]{:S(2)}) async-start(f32[8,8,256]{2,1,0:T(8,128)} %get-tuple-element.28), calls=%async_computation | async-start | bytes 131072 | tf_op jit(solution)/shard_map/all_to_all | solution.py:479
  16.4 2.7 %collective-permute-start.1 = (f32[16,1152]{1,0:T(8,128)S(1)}, f32[16,1152]{1,0:T(8,128)S(1)}, u32[]{:S(2)}, u32[]{:S(2)}) collective-permute-start(f32[16,1152]{1,0:T(8,128)S(1)} %add.9.half_ref), channel_id=1, source_target_pairs={{0,16},{8,24},{16,0},{24,8},{1,17},{9,25},{17,1},{25,9},{2,18},{10... | collective-permute-start | bytes 221192 | tf_op jit(solution)/shard_map/ppermute | solution.py:476
  19.1 2.3 %all-to-all-done.refs_0_ = f32[8,8,256]{2,1,0:T(8,128)S(1)} async-done(((f32[8,8,256]{2,1,0:T(8,128)}), f32[8,8,256]{2,1,0:T(8,128)S(1)}, u32[]{:S(2)}, u32[]{:S(2)}) %all-to-all-start) | async-done | bytes 65568 | tf_op jit(solution)/shard_map/all_to_all | solution.py:479
  21.4 1.6 %shard_map.94 = (f32[8,2048]{1,0:T(8,128)S(1)}, f32[8,8,256]{2,1,0:T(8,128)S(1)}, s32[16,128]{1,0:T(8,128)S(1)}, bf16[256,2048]{1,0:T(8,128)(2,1)S(1)}) custom-call(f32[8,8,256]{2,1,0:T(8,128)S(1)} %all-to-all-done.refs_0_), custom_call_target="tpu_custom_call" | custom-call | tf_op jit(solution)/shard_map/pallas_call | solution.py:556
  23.0 7.4 %all_to_all.36.recv_ref = f32[8,8,256]{2,1,0:T(8,128)S(1)} all-to-all(f32[8,8,256]{2,1,0:T(8,128)S(1)} %get-tuple-element.30), channel_id=1, replica_groups=mesh['wide'=4,'narrow'=8] {'narrow'}, dimensions={0} | all-to-all | bytes 131072 | tf_op jit(solution)/shard_map/all_to_all | solution.py:479
  30.4 5.9 %shard_map.95 = (f32[16,1024]{1,0:T(8,128)S(1)}, f32[16,1152]{1,0:T(8,128)S(1)}, f32[8,8,256]{2,1,0:T(8,128)}, f32[8,128]{1,0:T(8,128)}) custom-call(f32[8,8,256]{2,1,0:T(8,128)S(1)} %all_to_all.36.recv_ref, f32[16,1152]{1,0:T(8,128)S(1)} %add.9.half_ref, f32[16,1152]{1,0:T(8,128)S(1)} %collective-permute-done.1.later_ref, ...), custom_call_target="tpu_custom_call" | custom-call | tf_op jit(solution)/shard_map/pallas_call | solution.py:568
  36.3 0.5 collective-permute-start.2
  36.8 3.4 %all-to-all-start.2 = ((f32[8,8,256]{2,1,0:T(8,128)}), f32[8,8,256]{2,1,0:T(8,128)S(1)}, u32[]{:S(2)}, u32[]{:S(2)}) async-start(f32[8,8,256]{2,1,0:T(8,128)} %get-tuple-element.37), calls=%async_computation.2 | async-start | bytes 131072 | tf_op jit(solution)/shard_map/all_to_all | solution.py:479
  40.2 0.5 collective-permute-done.2
  40.7 2.7 %collective-permute-start.3 = (f32[16,1152]{1,0:T(8,128)S(1)}, f32[16,1152]{1,0:T(8,128)S(1)}, u32[]{:S(2)}, u32[]{:S(2)}) collective-permute-start(f32[16,1152]{1,0:T(8,128)S(1)} %add.10.half_ref), channel_id=1, source_target_pairs={{0,16},{8,24},{16,0},{24,8},{1,17},{9,25},{17,1},{25,9},{2,18},{10... | collective-permute-start | bytes 221192 | tf_op jit(solution)/shard_map/ppermute | solution.py:476
  43.4 1.7 %all-to-all-done.2.refs_0_ = f32[8,8,256]{2,1,0:T(8,128)S(1)} async-done(((f32[8,8,256]{2,1,0:T(8,128)}), f32[8,8,256]{2,1,0:T(8,128)S(1)}, u32[]{:S(2)}, u32[]{:S(2)}) %all-to-all-start.2) | async-done | bytes 65568 | tf_op jit(solution)/shard_map/all_to_all | solution.py:479
  45.1 1.2 %shard_map.96 = (f32[8,2048]{1,0:T(8,128)S(1)}, f32[8,8,256]{2,1,0:T(8,128)S(1)}, f32[8,128]{1,0:T(8,128)S(1)}) custom-call(f32[8,8,256]{2,1,0:T(8,128)S(1)} %all-to-all-done.2.refs_0_, s32[16,128]{1,0:T(8,128)S(1)} %get-tuple-element.38.refs_1_, bf16[256,2048]{1,0:T(8,128)(2,1)S(1)} %get-tuple-element.39.refs_2_), custom_call_target="tpu_custom_call" | custom-call | tf_op jit(solution)/shard_map/pallas_call | solution.py:564
  46.3 7.4 %all_to_all.37.recv_ref = f32[8,8,256]{2,1,0:T(8,128)S(1)} all-to-all(f32[8,8,256]{2,1,0:T(8,128)S(1)} %get-tuple-element.41), channel_id=1, replica_groups=mesh['wide'=4,'narrow'=8] {'narrow'}, dimensions={0} | all-to-all | bytes 131072 | tf_op jit(solution)/shard_map/all_to_all | solution.py:479
  53.7 5.9 %shard_map.97 = (f32[16,1024]{1,0:T(8,128)S(1)}, f32[16,1152]{1,0:T(8,128)S(1)}, f32[8,8,256]{2,1,0:T(8,128)}, f32[8,128]{1,0:T(8,128)S(1)}) custom-call(f32[8,8,256]{2,1,0:T(8,128)S(1)} %all_to_all.37.recv_ref, f32[16,1152]{1,0:T(8,128)S(1)} %add.10.half_ref, f32[16,1152]{1,0:T(8,128)S(1)} %collective-permute-done.3.later_ref, ...), custom_call_target="tpu_custom_call" | custom-call | tf_op jit(solution)/shard_map/pallas_call | solution.py:568
  59.6 1.6 %collective-permute-start.4 = (f32[16,1152]{1,0:T(8,128)S(1)}, f32[16,1152]{1,0:T(8,128)S(1)}, u32[]{:S(2)}, u32[]{:S(2)}) collective-permute-start(f32[16,1152]{1,0:T(8,128)S(1)} %get-tuple-element.47), channel_id=1, source_target_pairs={{0,8},{8,0},{16,24},{24,16},{1,9},{9,1},{17,25},{25,17},{2,10},{10... | collective-permute-start | bytes 221192 | tf_op jit(solution)/shard_map/ppermute | solution.py:476
  61.3 2.8 %collective-permute-done.4 = f32[16,1152]{1,0:T(8,128)S(1)} collective-permute-done((f32[16,1152]{1,0:T(8,128)S(1)}, f32[16,1152]{1,0:T(8,128)S(1)}, u32[]{:S(2)}, u32[]{:S(2)}) %collective-permute-start.4) | collective-permute-done | bytes 73760 | tf_op jit(solution)/shard_map/ppermute | solution.py:476
  64.0 2.7 %collective-permute-start.5 = (f32[16,1152]{1,0:T(8,128)S(1)}, f32[16,1152]{1,0:T(8,128)S(1)}, u32[]{:S(2)}, u32[]{:S(2)}) collective-permute-start(f32[16,1152]{1,0:T(8,128)S(1)} %add.11.att2a), channel_id=1, source_target_pairs={{0,16},{8,24},{16,0},{24,8},{1,17},{9,25},{17,1},{25,9},{2,18},{10... | collective-permute-start | bytes 221192 | tf_op jit(solution)/shard_map/ppermute | solution.py:476
  66.7 3.4 %all-to-all-start.4 = ((f32[8,8,256]{2,1,0:T(8,128)}), f32[8,8,256]{2,1,0:T(8,128)S(1)}, u32[]{:S(2)}, u32[]{:S(2)}) async-start(f32[8,8,256]{2,1,0:T(8,128)} %get-tuple-element.44), calls=%async_computation.4 | async-start | bytes 131072 | tf_op jit(solution)/shard_map/all_to_all | solution.py:479
  70.1 4.9 %all-to-all-done.4.refs_0_ = f32[8,8,256]{2,1,0:T(8,128)S(1)} async-done(((f32[8,8,256]{2,1,0:T(8,128)}), f32[8,8,256]{2,1,0:T(8,128)S(1)}, u32[]{:S(2)}, u32[]{:S(2)}) %all-to-all-start.4) | async-done | bytes 65568 | tf_op jit(solution)/shard_map/all_to_all | solution.py:479
  75.0 0.6 shard_map.98.src2
  75.9 8.9 %all_to_all.38 = f32[32,1,128]{2,1,0:T(1,128)S(1)} all-to-all(f32[32,1,128]{2,1,0:T(1,128)S(1)} %bitcast.15), channel_id=1, replica_groups=mesh['wide'=4,'narrow'=8] {'wide','narrow'}, dimensions={0} | all-to-all | bytes 32768 | tf_op jit(solution)/shard_map/all_to_all | solution.py:588
  84.9 0.9 %shard_map.100 = (f32[5,2048]{1,0:T(8,128)}, f32[16,1024]{1,0:T(8,128)}, f32[5,2048]{1,0:T(8,128)}, f32[16,1024]{1,0:T(8,128)}) custom-call(f32[32,128]{1,0:T(8,128)S(1)} %bitcast.14, f32[8,128]{1,0:T(8,128)S(1)} %get-tuple-element.49.scale_ref, f32[8,2048]{1,0:T(8,128)S(1)} %get-tuple-element.29.src0, f32[8,2048]{1,0:T(8,128)S(1)} %get-tuple-element.40.src1, ...), custom_call_target="tpu_custom_call" | custom-call | tf_op jit(solution)/shard_map/pallas_call | solution.py:589
  (10 shorter events, 0.3 us)
Async XLA Ops:
  9.6 6.8 %collective-permute-start = (f32[16,1152]{1,0:T(8,128)S(1)}, f32[16,1152]{1,0:T(8,128)S(1)}, u32[]{:S(2)}, u32[]{:S(2)}) collective-permute-start(f32[16,1152]{1,0:T(8,128)S(1)} %get-tuple-element.31), channel_id=1, source_target_pairs={{0,8},{8,0},{16,24},{24,16},{1,9},{9,1},{17,25},{25,17},{2,10},{10... | collective-permute-start | bytes 221192 | tf_op jit(solution)/shard_map/ppermute | solution.py:476
  12.7 8.7 %all-to-all-start = ((f32[8,8,256]{2,1,0:T(8,128)}), f32[8,8,256]{2,1,0:T(8,128)S(1)}, u32[]{:S(2)}, u32[]{:S(2)}) async-start(f32[8,8,256]{2,1,0:T(8,128)} %get-tuple-element.28), calls=%async_computation | async-start | bytes 131072 | tf_op jit(solution)/shard_map/all_to_all | solution.py:479
  16.4 14.0 %collective-permute-start.1 = (f32[16,1152]{1,0:T(8,128)S(1)}, f32[16,1152]{1,0:T(8,128)S(1)}, u32[]{:S(2)}, u32[]{:S(2)}) collective-permute-start(f32[16,1152]{1,0:T(8,128)S(1)} %add.9.half_ref), channel_id=1, source_target_pairs={{0,16},{8,24},{16,0},{24,8},{1,17},{9,25},{17,1},{25,9},{2,18},{10... | collective-permute-start | bytes 221192 | tf_op jit(solution)/shard_map/ppermute | solution.py:476
  36.3 4.4 %collective-permute-start.2 = (f32[16,1152]{1,0:T(8,128)S(1)}, f32[16,1152]{1,0:T(8,128)S(1)}, u32[]{:S(2)}, u32[]{:S(2)}) collective-permute-start(f32[16,1152]{1,0:T(8,128)S(1)} %get-tuple-element.42), channel_id=1, source_target_pairs={{0,8},{8,0},{16,24},{24,16},{1,9},{9,1},{17,25},{25,17},{2,10},{10... | collective-permute-start | bytes 221192 | tf_op jit(solution)/shard_map/ppermute | solution.py:476
  36.8 8.3 %all-to-all-start.2 = ((f32[8,8,256]{2,1,0:T(8,128)}), f32[8,8,256]{2,1,0:T(8,128)S(1)}, u32[]{:S(2)}, u32[]{:S(2)}) async-start(f32[8,8,256]{2,1,0:T(8,128)} %get-tuple-element.37), calls=%async_computation.2 | async-start | bytes 131072 | tf_op jit(solution)/shard_map/all_to_all | solution.py:479
  40.7 13.0 %collective-permute-start.3 = (f32[16,1152]{1,0:T(8,128)S(1)}, f32[16,1152]{1,0:T(8,128)S(1)}, u32[]{:S(2)}, u32[]{:S(2)}) collective-permute-start(f32[16,1152]{1,0:T(8,128)S(1)} %add.10.half_ref), channel_id=1, source_target_pairs={{0,16},{8,24},{16,0},{24,8},{1,17},{9,25},{17,1},{25,9},{2,18},{10... | collective-permute-start | bytes 221192 | tf_op jit(solution)/shard_map/ppermute | solution.py:476
  59.6 4.4 %collective-permute-start.4 = (f32[16,1152]{1,0:T(8,128)S(1)}, f32[16,1152]{1,0:T(8,128)S(1)}, u32[]{:S(2)}, u32[]{:S(2)}) collective-permute-start(f32[16,1152]{1,0:T(8,128)S(1)} %get-tuple-element.47), channel_id=1, source_target_pairs={{0,8},{8,0},{16,24},{24,16},{1,9},{9,1},{17,25},{25,17},{2,10},{10... | collective-permute-start | bytes 221192 | tf_op jit(solution)/shard_map/ppermute | solution.py:476
  64.0 11.6 %collective-permute-start.5 = (f32[16,1152]{1,0:T(8,128)S(1)}, f32[16,1152]{1,0:T(8,128)S(1)}, u32[]{:S(2)}, u32[]{:S(2)}) collective-permute-start(f32[16,1152]{1,0:T(8,128)S(1)} %add.11.att2a), channel_id=1, source_target_pairs={{0,16},{8,24},{16,0},{24,8},{1,17},{9,25},{17,1},{25,9},{2,18},{10... | collective-permute-start | bytes 221192 | tf_op jit(solution)/shard_map/ppermute | solution.py:476
  66.7 8.3 %all-to-all-start.4 = ((f32[8,8,256]{2,1,0:T(8,128)}), f32[8,8,256]{2,1,0:T(8,128)S(1)}, u32[]{:S(2)}, u32[]{:S(2)}) async-start(f32[8,8,256]{2,1,0:T(8,128)} %get-tuple-element.44), calls=%async_computation.4 | async-start | bytes 131072 | tf_op jit(solution)/shard_map/all_to_all | solution.py:479

commit v5 on v4

--- a/solution.py
+++ b/solution.py
@@ -165,9 +165,8 @@
 def start_kernel(
     narrow,
     att_hbm, src_hbm, rhs_hbm, source_hbm, segment_hbm, count_hbm,
-    table_hbm, square_ref, pos_ref, seg_ref, order_ref, right, att_ref, send_ref,
-    table_ref, att_in, src_in, rhs_in, source_in, segment_in, count_in, blocks, ids, left, sems, int_sems,
-    out_sems,
+    table_ref, square_ref, pos_ref, seg_ref, order_ref, right, att_ref, send_ref,
+    att_in, src_in, rhs_in, source_in, segment_in, count_in, blocks, ids, left, sems, int_sems,
 ):
     groups, att_sets = att_in.shape[0], att_in.shape[1]
     att_rows, src_rows = att_sets * 8, src_hbm.shape[1]
@@ -188,14 +187,6 @@
             pltpu.make_async_copy(src_hbm.at[cut], src_in.at[g, :, 0:src_rows], sems.at[1, g]),
             pltpu.make_async_copy(rhs_hbm.at[cut], rhs_in.at[g], sems.at[2, g]),
         ]
-
-    def store(g):
-        cut = pl.ds(g * 2, 2)
-        return pltpu.make_async_copy(table_ref.at[cut], table_hbm.at[cut], out_sems.at[g])
-
-    def finish(g, carry):
-        store(g).wait()
-        return carry
 
     def begin(g, carry):
         for one in loads(g):
@@ -243,7 +234,6 @@
         for half in range(2):
             rest = 24 - att_rows - src_rows
             blocks[g * 2 + half, 24 - rest : 24, :] = jnp.zeros((rest, LANE), F32)
-        store(g).start()
         return carry
 
     lax.fori_loop(0, groups, turn, 0)
@@ -258,16 +248,18 @@
         lambda t: jnp.where(row == 5, ids[t : t + 1, :], 0.0),
         send_ref,
     )
-    lax.fori_loop(0, groups, finish, 0)
 
 
 def owner_kernel(narrow, first, last, *refs):
     if first:
-        recv_ref, src_ref, back_ref, index_ref, right, left = refs
+        recv_ref, part_ref, other_ref, src_ref, back_ref, half_ref, index_ref, right, left = refs
     elif last:
         recv_ref, index_ref, right, src_ref, left = refs
     else:
-        recv_ref, index_ref, right, src_ref, back_ref, known_ref, left = refs
+        recv_ref, part_ref, other_ref, index_ref, right = refs[:5]
+        src_ref, back_ref, half_ref, known_ref, left = refs[5:]
+    if not last:
+        half_ref[...] = part_ref[...] + other_ref[...]
     tiles, cap = index_ref.shape[0], recv_ref.shape[2]
     per = cap // LANE
     levels = SRC_DEV // HIGH
@@ -310,20 +302,10 @@
 
 def product_kernel(
     narrow, first, recv_ref, half_ref, later_ref, known_ref, pos_ref, seg_ref, order_ref, right,
-    table_hbm, full_ref, att_ref, send_ref, scale_ref, vec, blocks, left, table_ref, sems,
+    table_ref, full_ref, att_ref, send_ref, scale_ref, vec, blocks, left,
 ):
     tiles, rows = pos_ref.shape[0], table_ref.shape[1]
-
-    def load(t):
-        return pltpu.make_async_copy(table_hbm.at[t], table_ref.at[t], sems.at[t])
-
-    def begin(t, carry):
-        load(t).start()
-        return carry
-
-    lax.fori_loop(0, tiles, begin, 0)
-    cap = recv_ref.shape[2]
-    per = cap // LANE
+    per = recv_ref.shape[2] // LANE
     full = half_ref[...] + later_ref[...]
     full_ref[...] = full[:, :SEG_DEV]
     notes = full[0:1, SEG_DEV:]
@@ -364,7 +346,6 @@
     lax.fori_loop(0, tiles, gather, 0)
 
     def multiply(t, carry):
-        load(t).wait()
         image = None
         for i in range(rows):
             part = table_ref[t, i] * vec[t, i : i + 1, :]
@@ -478,6 +459,15 @@
     def exchange(values):
         return lax.all_to_all(values, "narrow", 0, 0)
 
+    def far_sums(total):
+        later, jump = None, 2
+        while jump < wide:
+            if later is not None:
+                total = total + later
+            later = across(total, jump)
+            jump *= 2
+        return total, jnp.zeros_like(total) if later is None else later
+
     tile_rows = lambda values: values.reshape(tiles, LANE)
     att_view = att_design.reshape(att_rows // 8, 8, columns, LANE).transpose(0, 2, 1, 3)
     src_view = src_design.reshape(src_rows, columns, LANE).transpose(1, 0, 2)
@@ -493,7 +483,7 @@
     table, square, pos, seg, order, att_right, part, send = call(
         functools.partial(start_kernel, narrow),
         (
-            pltpu.HBM(table_shape, F32),
+            sds(table_shape),
             sds((8, LANE)),
             tile_int,
             tile_int,
@@ -503,7 +493,6 @@
             send_shape,
         ),
         [
-            pltpu.VMEM(table_shape, F32),
             pltpu.VMEM((groups, att_rows // 8, LANE, 8, LANE), F32),
             pltpu.VMEM((groups, LANE, 8, LANE), F32),
             pltpu.VMEM((groups, LANE, LANE), F32),
@@ -515,12 +504,9 @@
             att_left,
             pltpu.SemaphoreType.DMA((3, groups)),
             pltpu.SemaphoreType.DMA((3,)),
-            pltpu.SemaphoreType.DMA((groups,)),
         ],
         in_specs=[pl.BlockSpec(memory_space=pltpu.HBM)] * 6,
-        out_specs=(pl.BlockSpec(memory_space=pltpu.HBM),)
-        + (pl.BlockSpec(memory_space=pltpu.VMEM),) * 7,
-        limit=32,
+        limit=20,
     )(
         *map(
             in_hbm,
@@ -542,28 +528,22 @@
         first_time, last_time = step == 0, step == 2
         other = across(part, 1)
         arrived = exchange(send)
-        total, jump = part + other, 2
-        later = None
-        while jump < wide:
-            if later is not None:
-                total = total + later
-            later = across(total, jump)
-            jump *= 2
-        if later is None:
-            later = jnp.zeros_like(total)
         kernel = functools.partial(owner_kernel, narrow, first_time, last_time)
-        if first_time:
-            src_sum, back, *owners = call(
-                kernel, (src_shape, send_shape, tile_int, right_shape), [src_left]
-            )(arrived)
-        elif last_time:
+        if last_time:
+            total, later = far_sums(part + other)
             src_sum = call(kernel, src_shape, [src_left])(arrived, *owners)
             results.append((src_sum, total, later))
             break
+        outs = (src_shape, send_shape, att_shape)
+        if first_time:
+            src_sum, back, half, *owners = call(
+                kernel, outs + (tile_int, right_shape), [src_left]
+            )(arrived, part, other)
         else:
-            src_sum, back, note = call(
-                kernel, (src_shape, send_shape, sds((8, LANE))), [src_left]
-            )(arrived, *owners)
+            src_sum, back, half, note = call(kernel, outs + (sds((8, LANE)),), [src_left])(
+                arrived, part, other, *owners
+            )
+        total, later = far_sums(half)
         back = exchange(back)
         att_sum, part, send, scale = call(
             functools.partial(product_kernel, narrow, first_time),
@@ -572,13 +552,8 @@
                 pltpu.VMEM((tiles, 24, LANE), F32),
                 pltpu.VMEM((tiles, 24, LANE), F32),
                 att_left,
-                pltpu.VMEM(table_shape, F32),
-                pltpu.SemaphoreType.DMA((tiles,)),
             ],
-            in_specs=[pl.BlockSpec(memory_space=pltpu.VMEM)] * 8
-            + [pl.BlockSpec(memory_space=pltpu.HBM)],
-            limit=20,
-        )(back, total, later, note, pos, seg, order, att_right, in_hbm(table))
+        )(back, total, later, note, pos, seg, order, att_right, table)
         results.append((src_sum, att_sum))
     weight = jnp.where(lax.axis_index("wide") == 0, 1.0, 0.0).astype(F32) * jnp.ones((8, LANE), F32)
     (src0, att0), (src1, att1), (src2, att2a, att2b) = results

time: 86.3 us -> 84.4 us (0.978)
  blocking collectives: 23.7 us -> 39.6 us
  starting transfers between devices: 23.6 us -> 14.3 us
  waiting for transfers between devices: 12.3 us -> 7.74 us
  Pallas kernels: 25.3 us -> 21.7 us
    all_to_all x2 -> x4, blocking collectives: 14.8 us -> 30.7 us  [exchange(): return lax.all_to_all(values, 'narrow', 0, 0)]
    all_to_all x3 -> x1, starting transfers between devices: 10.4 us -> 3.35 us  [exchange(): return lax.all_to_all(values, 'narrow', 0, 0)]
    all_to_all x3 -> x1, waiting for transfers between devices: 9.02 us -> 4.94 us  [exchange(): return lax.all_to_all(values, 'narrow', 0, 0)]
    ppermute x6, starting transfers between devices: 13.2 us -> 10.9 us  [across(): return lax.ppermute(values, 'wide', [(i, i ^ step) for i in range(wide)])]
    pallas_call x3, Pallas kernels: 11.8 us -> 9.9 us  [the longest x1 7.06 us: on_device(): call(functools.partial(start_kernel, narrow), (sds(table_shape), sds((8,...]
    pallas_call x2, Pallas kernels: 11.7 us -> 9.99 us  [on_device(): call(functools.partial(product_kernel, narrow, first_time), (sds((16, SEG...]
  transfers between devices with their start and end apart: 9 -> 7, of which waited for: 5 -> 2; matrix products, arithmetic and copies ran while one was open for 0% -> 0% of each run, Pallas kernels for 4% -> 1%
where the time goes in v5:
time: 84.4 us; the launch traced here: 84 us
  blocking collectives  39.6 us (47%)
  Pallas kernels  21.7 us (26%)
  starting transfers between devices  14.3 us (17%)
  waiting for transfers between devices  7.74 us (9%)
    all_to_all x4, blocking collectives, exchange(): return lax.all_to_all(values, 'narrow', 0, 0)  30.7 us
    ppermute x6, starting transfers between devices, across(): return lax.ppermute(values, 'wide', [(i, i ^ step) for i in range(wide)])  10.9 us
    pallas_call x2, Pallas kernels, on_device(): call(functools.partial(product_kernel, narrow, first_time), (sds((16, SEG...  9.99 us
    all_to_all x1, blocking collectives, on_device(): dots = lax.all_to_all(dots, ('wide', 'narrow'), 0, 0, tiled=True)  8.91 us
    pallas_call x1, Pallas kernels, on_device(): call(functools.partial(start_kernel, narrow), (sds(table_shape), sds((8,...  7.06 us
    all_to_all x1, waiting for transfers between devices, exchange(): return lax.all_to_all(values, 'narrow', 0, 0)  4.94 us
    all_to_all x1, starting transfers between devices, exchange(): return lax.all_to_all(values, 'narrow', 0, 0)  3.35 us
    ppermute x6, waiting for transfers between devices, across(): return lax.ppermute(values, 'wide', [(i, i ^ step) for i in range(wide)])  2.8 us
  transfers between devices with their start and end apart: 7, of which 2 were waited for; matrix products, arithmetic and copies ran while one was open for 0% of the time, Pallas kernels for 1%

profile of v5, /device:TPU:0, one launch (start us, length us, event | category | flops | bytes accessed | tf_op | source)
XLA Modules:
  0.0 84.0 jit_solution(786465156169679408)
XLA Ops:
  0.6 7.1 %shard_map.93 = (f32[16,21,64,128]{3,2,1,0:T(8,128)S(1)}, f32[8,128]{1,0:T(8,128)S(1)}, s32[16,128]{1,0:T(8,128)S(1)}, s32[16,128]{1,0:T(8,128)S(1)}, s32[16,128...) custom-call(f32[2,1024,8,128]{3,2,1,0:T(8,128)} %bitcast.16, ...), custom_call_target="tpu_custom_call" | custom-call | tf_op jit(solution)/shard_map/pallas_call | solution.py:483
  7.7 3.1 %collective-permute-start = (f32[16,1152]{1,0:T(8,128)S(1)}, f32[16,1152]{1,0:T(8,128)S(1)}, u32[]{:S(2)}, u32[]{:S(2)}) collective-permute-start(f32[16,1152]{1,0:T(8,128)S(1)} %get-tuple-element.31.refs_1_), channel_id=1, source_target_pairs={{0,8},{8,0},{16,24},{24,16},{1,9},{9,1},{17,25},{25,17},{2,10},{10... | collective-permute-start | bytes 221192 | tf_op jit(solution)/shard_map/ppermute | solution.py:457
  10.8 8.5 %all_to_all.36.refs_0_ = f32[8,8,256]{2,1,0:T(8,128)S(1)} all-to-all(f32[8,8,256]{2,1,0:T(8,128)S(1)} %get-tuple-element.30), channel_id=1, replica_groups=mesh['wide'=4,'narrow'=8] {'narrow'}, dimensions={0} | all-to-all | bytes 131072 | tf_op jit(solution)/shard_map/all_to_all | solution.py:460
  19.3 0.0 collective-permute-done.refs_2_
  19.4 1.6 %shard_map.94 = (f32[8,2048]{1,0:T(8,128)S(1)}, f32[8,8,256]{2,1,0:T(8,128)S(1)}, f32[16,1152]{1,0:T(8,128)S(1)}, s32[16,128]{1,0:T(8,128)S(1)}, bf16[256,2048]{1,0:T(8,128)(2,1)S(1)}) custom-call(f32[8,8,256]{2,1,0:T(8,128)S(1)} %all_to_all.36.refs_0_, f32[16,1152]{1,0:T(8,128)S(1)} %get-tuple-element.31.refs_1_, f32[16,1152]{1,0:T(8,128)S(1)} %collective-permute-done.refs_2_), custom_call_target="tpu_custom_call" | custom-call | tf_op jit(solution)/shard_map/pallas_call | solution.py:539
  20.9 2.6 %collective-permute-start.1 = (f32[16,1152]{1,0:T(8,128)S(1)}, f32[16,1152]{1,0:T(8,128)S(1)}, u32[]{:S(2)}, u32[]{:S(2)}) collective-permute-start(f32[16,1152]{1,0:T(8,128)S(1)} %get-tuple-element.34.half_ref), channel_id=1, source_target_pairs={{0,16},{8,24},{16,0},{24,8},{1,17},{9,25},{17,1},{25,9},{2,18},{10... | collective-permute-start | bytes 221192 | tf_op jit(solution)/shard_map/ppermute | solution.py:457
  23.6 7.4 %all_to_all.37.recv_ref = f32[8,8,256]{2,1,0:T(8,128)S(1)} all-to-all(f32[8,8,256]{2,1,0:T(8,128)S(1)} %get-tuple-element.33), channel_id=1, replica_groups=mesh['wide'=4,'narrow'=8] {'narrow'}, dimensions={0} | all-to-all | bytes 131072 | tf_op jit(solution)/shard_map/all_to_all | solution.py:460
  31.0 0.0 collective-permute-done.1.later_ref
  31.0 4.7 %shard_map.95 = (f32[16,1024]{1,0:T(8,128)S(1)}, f32[16,1152]{1,0:T(8,128)S(1)}, f32[8,8,256]{2,1,0:T(8,128)S(1)}, f32[8,128]{1,0:T(8,128)}) custom-call(f32[8,8,256]{2,1,0:T(8,128)S(1)} %all_to_all.37.recv_ref, f32[16,1152]{1,0:T(8,128)S(1)} %get-tuple-element.34.half_ref, f32[16,1152]{1,0:T(8,128)S(1)} %collective-permute-done.1.later_ref, ...), custom_call_target="tpu_custom_call" | custom-call | tf_op jit(solution)/shard_map/pallas_call | solution.py:548
  35.7 0.5 collective-permute-start.2
  36.2 7.4 %all_to_all.38.refs_0_ = f32[8,8,256]{2,1,0:T(8,128)S(1)} all-to-all(f32[8,8,256]{2,1,0:T(8,128)S(1)} %get-tuple-element.40), channel_id=1, replica_groups=mesh['wide'=4,'narrow'=8] {'narrow'}, dimensions={0} | all-to-all | bytes 131072 | tf_op jit(solution)/shard_map/all_to_all | solution.py:460
  43.6 1.2 %shard_map.96 = (f32[8,2048]{1,0:T(8,128)S(1)}, f32[8,8,256]{2,1,0:T(8,128)S(1)}, f32[16,1152]{1,0:T(8,128)S(1)}, f32[8,128]{1,0:T(8,128)S(1)}) custom-call(f32[8,8,256]{2,1,0:T(8,128)S(1)} %all_to_all.38.refs_0_, f32[16,1152]{1,0:T(8,128)S(1)} %get-tuple-element.41.refs_1_, f32[16,1152]{1,0:T(8,128)S(1)} %collective-permute-done.2.refs_2_, ...), custom_call_target="tpu_custom_call" | custom-call | tf_op jit(solution)/shard_map/pallas_call | solution.py:543
  44.8 0.4 collective-permute-start.3
  45.2 7.4 %all_to_all.39.recv_ref = f32[8,8,256]{2,1,0:T(8,128)S(1)} all-to-all(f32[8,8,256]{2,1,0:T(8,128)S(1)} %get-tuple-element.45), channel_id=1, replica_groups=mesh['wide'=4,'narrow'=8] {'narrow'}, dimensions={0} | all-to-all | bytes 131072 | tf_op jit(solution)/shard_map/all_to_all | solution.py:460
  52.6 5.3 %shard_map.97 = (f32[16,1024]{1,0:T(8,128)S(1)}, f32[16,1152]{1,0:T(8,128)S(1)}, f32[8,8,256]{2,1,0:T(8,128)}, f32[8,128]{1,0:T(8,128)S(1)}) custom-call(f32[8,8,256]{2,1,0:T(8,128)S(1)} %all_to_all.39.recv_ref, f32[16,1152]{1,0:T(8,128)S(1)} %get-tuple-element.46.half_ref, f32[16,1152]{1,0:T(8,128)S(1)} %collective-permute-done.3.later_ref, ...), custom_call_target="tpu_custom_call" | custom-call | tf_op jit(solution)/shard_map/pallas_call | solution.py:548
  57.9 1.6 %collective-permute-start.4 = (f32[16,1152]{1,0:T(8,128)S(1)}, f32[16,1152]{1,0:T(8,128)S(1)}, u32[]{:S(2)}, u32[]{:S(2)}) collective-permute-start(f32[16,1152]{1,0:T(8,128)S(1)} %get-tuple-element.51), channel_id=1, source_target_pairs={{0,8},{8,0},{16,24},{24,16},{1,9},{9,1},{17,25},{25,17},{2,10},{10... | collective-permute-start | bytes 221192 | tf_op jit(solution)/shard_map/ppermute | solution.py:457
  59.5 2.8 %collective-permute-done.4 = f32[16,1152]{1,0:T(8,128)S(1)} collective-permute-done((f32[16,1152]{1,0:T(8,128)S(1)}, f32[16,1152]{1,0:T(8,128)S(1)}, u32[]{:S(2)}, u32[]{:S(2)}) %collective-permute-start.4) | collective-permute-done | bytes 73760 | tf_op jit(solution)/shard_map/ppermute | solution.py:457
  62.3 2.7 %collective-permute-start.5 = (f32[16,1152]{1,0:T(8,128)S(1)}, f32[16,1152]{1,0:T(8,128)S(1)}, u32[]{:S(2)}, u32[]{:S(2)}) collective-permute-start(f32[16,1152]{1,0:T(8,128)S(1)} %add.3.att2a), channel_id=1, source_target_pairs={{0,16},{8,24},{16,0},{24,8},{1,17},{9,25},{17,1},{25,9},{2,18},{10... | collective-permute-start | bytes 221192 | tf_op jit(solution)/shard_map/ppermute | solution.py:457
  64.9 3.4 %all-to-all-start.4 = ((f32[8,8,256]{2,1,0:T(8,128)}), f32[8,8,256]{2,1,0:T(8,128)S(1)}, u32[]{:S(2)}, u32[]{:S(2)}) async-start(f32[8,8,256]{2,1,0:T(8,128)} %get-tuple-element.48), calls=%async_computation.4 | async-start | bytes 131072 | tf_op jit(solution)/shard_map/all_to_all | solution.py:460
  68.3 4.9 %all-to-all-done.4.refs_0_ = f32[8,8,256]{2,1,0:T(8,128)S(1)} async-done(((f32[8,8,256]{2,1,0:T(8,128)}), f32[8,8,256]{2,1,0:T(8,128)S(1)}, u32[]{:S(2)}, u32[]{:S(2)}) %all-to-all-start.4) | async-done | bytes 65568 | tf_op jit(solution)/shard_map/all_to_all | solution.py:460
  73.3 0.6 shard_map.98.src2
  73.9 0.3 shard_map.99
  74.2 8.9 %all_to_all.40 = f32[32,1,128]{2,1,0:T(1,128)S(1)} all-to-all(f32[32,1,128]{2,1,0:T(1,128)S(1)} %bitcast.15), channel_id=1, replica_groups=mesh['wide'=4,'narrow'=8] {'wide','narrow'}, dimensions={0} | all-to-all | bytes 32768 | tf_op jit(solution)/shard_map/all_to_all | solution.py:563
  83.1 0.9 %shard_map.100 = (f32[5,2048]{1,0:T(8,128)}, f32[16,1024]{1,0:T(8,128)}, f32[5,2048]{1,0:T(8,128)}, f32[16,1024]{1,0:T(8,128)}) custom-call(f32[32,128]{1,0:T(8,128)S(1)} %bitcast.14, f32[8,128]{1,0:T(8,128)S(1)} %get-tuple-element.53.scale_ref, f32[8,2048]{1,0:T(8,128)S(1)} %get-tuple-element.32.src0, f32[8,2048]{1,0:T(8,128)S(1)} %get-tuple-element.44.src1, ...), custom_call_target="tpu_custom_call" | custom-call | tf_op jit(solution)/shard_map/pallas_call | solution.py:564
  (6 shorter events, 0.0 us)
Async XLA Ops:
  7.7 11.6 %collective-permute-start = (f32[16,1152]{1,0:T(8,128)S(1)}, f32[16,1152]{1,0:T(8,128)S(1)}, u32[]{:S(2)}, u32[]{:S(2)}) collective-permute-start(f32[16,1152]{1,0:T(8,128)S(1)} %get-tuple-element.31.refs_1_), channel_id=1, source_target_pairs={{0,8},{8,0},{16,24},{24,16},{1,9},{9,1},{17,25},{25,17},{2,10},{10... | collective-permute-start | bytes 221192 | tf_op jit(solution)/shard_map/ppermute | solution.py:457
  20.9 10.0 %collective-permute-start.1 = (f32[16,1152]{1,0:T(8,128)S(1)}, f32[16,1152]{1,0:T(8,128)S(1)}, u32[]{:S(2)}, u32[]{:S(2)}) collective-permute-start(f32[16,1152]{1,0:T(8,128)S(1)} %get-tuple-element.34.half_ref), channel_id=1, source_target_pairs={{0,16},{8,24},{16,0},{24,8},{1,17},{9,25},{17,1},{25,9},{2,18},{10... | collective-permute-start | bytes 221192 | tf_op jit(solution)/shard_map/ppermute | solution.py:457
  35.7 7.9 %collective-permute-start.2 = (f32[16,1152]{1,0:T(8,128)S(1)}, f32[16,1152]{1,0:T(8,128)S(1)}, u32[]{:S(2)}, u32[]{:S(2)}) collective-permute-start(f32[16,1152]{1,0:T(8,128)S(1)} %get-tuple-element.41.refs_1_), channel_id=1, source_target_pairs={{0,8},{8,0},{16,24},{24,16},{1,9},{9,1},{17,25},{25,17},{2,10},{10... | collective-permute-start | bytes 221192 | tf_op jit(solution)/shard_map/ppermute | solution.py:457
  44.8 7.8 %collective-permute-start.3 = (f32[16,1152]{1,0:T(8,128)S(1)}, f32[16,1152]{1,0:T(8,128)S(1)}, u32[]{:S(2)}, u32[]{:S(2)}) collective-permute-start(f32[16,1152]{1,0:T(8,128)S(1)} %get-tuple-element.46.half_ref), channel_id=1, source_target_pairs={{0,16},{8,24},{16,0},{24,8},{1,17},{9,25},{17,1},{25,9},{2,18},{10... | collective-permute-start | bytes 221192 | tf_op jit(solution)/shard_map/ppermute | solution.py:457
  57.9 4.4 %collective-permute-start.4 = (f32[16,1152]{1,0:T(8,128)S(1)}, f32[16,1152]{1,0:T(8,128)S(1)}, u32[]{:S(2)}, u32[]{:S(2)}) collective-permute-start(f32[16,1152]{1,0:T(8,128)S(1)} %get-tuple-element.51), channel_id=1, source_target_pairs={{0,8},{8,0},{16,24},{24,16},{1,9},{9,1},{17,25},{25,17},{2,10},{10... | collective-permute-start | bytes 221192 | tf_op jit(solution)/shard_map/ppermute | solution.py:457
  62.3 11.6 %collective-permute-start.5 = (f32[16,1152]{1,0:T(8,128)S(1)}, f32[16,1152]{1,0:T(8,128)S(1)}, u32[]{:S(2)}, u32[]{:S(2)}) collective-permute-start(f32[16,1152]{1,0:T(8,128)S(1)} %add.3.att2a), channel_id=1, source_target_pairs={{0,16},{8,24},{16,0},{24,8},{1,17},{9,25},{17,1},{25,9},{2,18},{10... | collective-permute-start | bytes 221192 | tf_op jit(solution)/shard_map/ppermute | solution.py:457
  64.9 8.3 %all-to-all-start.4 = ((f32[8,8,256]{2,1,0:T(8,128)}), f32[8,8,256]{2,1,0:T(8,128)S(1)}, u32[]{:S(2)}, u32[]{:S(2)}) async-start(f32[8,8,256]{2,1,0:T(8,128)} %get-tuple-element.48), calls=%async_computation.4 | async-start | bytes 131072 | tf_op jit(solution)/shard_map/all_to_all | solution.py:460

commit v6 on v5

--- a/solution.py
+++ b/solution.py
@@ -48,17 +48,14 @@
     return top, middle, rest - middle
 
 
-def dot_lanes(left, right):
-    return lax.dot_general(left, right, (((1,), (1,)), ((), ())), preferred_element_type=F32)
-
-
 def spread_rows(store, picked, row, column, levels):
     rows = picked.shape[0]
+    size = levels * rows
+    mask = jnp.where(row_iota(size) // rows == row, 1.0, 0.0).astype(BF16)
     for part, piece in enumerate(split_three(picked)):
-        for level in range(levels):
-            at = (part * levels + level) * rows
-            kept = jnp.where(row == level, piece, 0.0)
-            store[pl.ds(at, rows), pl.ds(column, LANE)] = kept.astype(BF16)
+        whole = jnp.concatenate([piece] * (16 // rows), axis=0).astype(BF16)
+        whole = jnp.concatenate([whole] * (size // 16), axis=0)
+        store[pl.ds(part * size, size), pl.ds(column, LANE)] = whole * mask
 
 
 def rank_blocks(narrow, source_ref, segment_ref, pos_ref, seg_ref, order_ref, ids_ref, left, right):
@@ -98,8 +95,8 @@
             left[part * levels : (part + 1) * levels, t * LANE : (t + 1) * LANE] = jnp.where(
                 level, piece, 0.0
             ).astype(BF16)
-    mark_high(right, lambda t: pos[t : t + 1], tiles)
-    found = dot_lanes(left[0 : 4 * levels, :], right[...])
+    mark_high(right, pos)
+    found = jnp.dot(left[0 : 4 * levels, :], right[...], preferred_element_type=F32)
     tile_at, lane_at = found[:levels], found[levels : 2 * levels]
     order = (tile_at * LANE + lane_at).astype(I32)
     ids = found[2 * levels : 3 * levels] * LANE + found[3 * levels :]
@@ -111,25 +108,24 @@
             ids_ref[row : row + 1, :] = ids[level : level + 1, cut]
 
 
-def mark_high(right, rows_of, tiles):
-    high_at = row_iota(HIGH)
-    for t in range(tiles):
-        here = rows_of(t) & (HIGH - 1)
-        right[:, t * LANE : (t + 1) * LANE] = jnp.where(high_at == here, 1.0, 0.0).astype(BF16)
-
-
-def scatter_att(blocks, seg_ref, out_ref, left, right):
-    tiles = seg_ref.shape[0]
+def mark_high(right, index):
+    columns = (index & (HIGH - 1)).astype(F32).T
+    high_at = lane_iota(LANE, HIGH).astype(F32).astype(BF16)
+    one, zero = jnp.ones((), BF16), jnp.zeros((), BF16)
+    for t in range(index.shape[0]):
+        here = jnp.broadcast_to(columns[:, t : t + 1], (LANE, HIGH)).astype(BF16)
+        right[t * LANE : (t + 1) * LANE, :] = jnp.where(high_at == here, one, zero)
+
+
+def fill_att(blocks, seg_ref, left, t):
+    here = seg_ref[pl.ds(t, 1), :]
+    column = pl.multiple_of(t * LANE, LANE)
+    spread_rows(left, blocks[t, 0:16, :], here // HIGH, column, SEG_DEV // HIGH)
+
+
+def scatter_att(out_ref, left, right):
     levels = SEG_DEV // HIGH
-
-    def fill(t, carry):
-        here = seg_ref[pl.ds(t, 1), :]
-        column = pl.multiple_of(t * LANE, LANE)
-        spread_rows(left, blocks[t, 0:16, :], here // HIGH, column, levels)
-        return carry
-
-    lax.fori_loop(0, tiles, fill, 0)
-    sums = dot_lanes(left[...], right[...])
+    sums = jnp.dot(left[...], right[...], preferred_element_type=F32)
     size = 16 * levels
     sums = sums[:size] + (sums[size : 2 * size] + sums[2 * size :])
     for level in range(levels):
@@ -201,10 +197,12 @@
     count_in[...] = to_tiles(count_in[...])
     square_ref[...] = jnp.zeros_like(square_ref)
     rank_blocks(narrow, source_in, segment_in, pos_ref, seg_ref, order_ref, ids, left, right)
-    mark_high(right, lambda t: seg_ref[t : t + 1, :], seg_ref.shape[0])
+    mark_high(right, seg_ref[...])
     place = row_iota(obs)
 
     def turn(g, carry):
+        for half in range(2):
+            fill_att(blocks, seg_ref, left, jnp.maximum(g * 2 - 2 + half, half))
         for one in loads(g):
             one.wait()
         wide_rhs = rhs_in[g].T
@@ -237,7 +235,9 @@
         return carry
 
     lax.fori_loop(0, groups, turn, 0)
-    scatter_att(blocks, seg_ref, att_ref, left, right)
+    for half in range(2):
+        fill_att(blocks, seg_ref, left, groups * 2 - 2 + half)
+    scatter_att(att_ref, left, right)
     lane = lane_iota(16)
     att_ref[:, SEG_DEV:] = jnp.where(lane == 0, jnp.sum(square_ref[...]), 0.0)
     row = row_iota(8)
@@ -267,7 +267,7 @@
     if first:
         for t in range(tiles):
             index_ref[t : t + 1, :] = entry(recv_ref, per, t)[5:6].astype(I32)
-        mark_high(right, lambda t: index_ref[t : t + 1, :], tiles)
+        mark_high(right, index_ref[...])
     elif not last:
         known = recv_ref[0, :, 0:LANE]
         for n in range(1, narrow):
@@ -277,7 +277,7 @@
         here = index_ref[t : t + 1, :]
         values = jnp.where(keep, entry(recv_ref, per, t), 0.0)
         spread_rows(left, values, here // HIGH, t * LANE, levels)
-    sums = dot_lanes(left[...], right[...])
+    sums = jnp.dot(left[...], right[...], preferred_element_type=F32)
     size = 8 * levels
     sums = sums[:size] + (sums[size : 2 * size] + sums[2 * size :])
     for level in range(levels):
@@ -329,7 +329,7 @@
     scale_ref[...] = jnp.broadcast_to(scale, (8, LANE))
     att_ref[:, SEG_DEV:] = att_note
 
-    def gather(t, carry):
+    def gather(t):
         where_att = seg_ref[pl.ds(t, 1), :]
         for top in range(0, 24, 8):
             if top < 16:
@@ -341,11 +341,9 @@
             else:
                 picked = pick(lambda c: entry(recv_ref, per, c), tiles, pos_ref[pl.ds(t, 1), :])
             vec[t, top : top + 8, :] = picked if first else picked * scale
-        return carry
-
-    lax.fori_loop(0, tiles, gather, 0)
 
     def multiply(t, carry):
+        fill_att(blocks, seg_ref, left, jnp.maximum(t - 1, 0))
         image = None
         for i in range(rows):
             part = table_ref[t, i] * vec[t, i : i + 1, :]
@@ -353,10 +351,13 @@
         for i in range(rows):
             blocks[t, i : i + 1, :] = jnp.sum(table_ref[t, i] * image, axis=0, keepdims=True)
         blocks[t, rows:24, :] = jnp.zeros((24 - rows, LANE), F32)
+        gather(jnp.minimum(t + 1, tiles - 1))
         return carry
 
+    gather(0)
     lax.fori_loop(0, tiles, multiply, 0)
-    scatter_att(blocks, seg_ref, att_ref, left, right)
+    fill_att(blocks, seg_ref, left, tiles - 1)
+    scatter_att(att_ref, left, right)
     send_sorted(narrow, blocks, order_ref, lambda t: send_note, send_ref)
 
 
@@ -472,7 +473,7 @@
     att_view = att_design.reshape(att_rows // 8, 8, columns, LANE).transpose(0, 2, 1, 3)
     src_view = src_design.reshape(src_rows, columns, LANE).transpose(1, 0, 2)
 
-    right_shape = sds((HIGH, blocks), BF16)
+    right_shape = sds((blocks, HIGH), BF16)
     att_left = pltpu.VMEM((3 * 16 * SEG_DEV // HIGH, blocks), BF16)
     src_left = pltpu.VMEM((3 * 8 * SRC_DEV // HIGH, blocks), BF16)
     tile_int = sds((tiles, LANE), I32)

time: 84.4 us -> 82.2 us (0.974)
  Pallas kernels: 21.7 us -> 19.4 us
    pallas_call x2, Pallas kernels: 9.99 us -> 8.88 us  [on_device(): call(functools.partial(product_kernel, narrow, first_time), (sds((16, SEG...]
where the time goes in v6:
time: 82.2 us; the launch traced here: 81.8 us
  blocking collectives  39.6 us (48%)
  Pallas kernels  19.4 us (24%)
  starting transfers between devices  14.3 us (17%)
  waiting for transfers between devices  7.73 us (9%)
    all_to_all x4, blocking collectives, exchange(): return lax.all_to_all(values, 'narrow', 0, 0)  30.7 us
    ppermute x6, starting transfers between devices, across(): return lax.ppermute(values, 'wide', [(i, i ^ step) for i in range(wide)])  10.9 us
    all_to_all x1, blocking collectives, on_device(): dots = lax.all_to_all(dots, ('wide', 'narrow'), 0, 0, tiled=True)  8.92 us
    pallas_call x2, Pallas kernels, on_device(): call(functools.partial(product_kernel, narrow, first_time), (sds((16, SEG...  8.88 us
    pallas_call x1, Pallas kernels, on_device(): call(functools.partial(start_kernel, narrow), (sds(table_shape), sds((8,...  6.45 us
    all_to_all x1, waiting for transfers between devices, exchange(): return lax.all_to_all(values, 'narrow', 0, 0)  4.94 us
    all_to_all x1, starting transfers between devices, exchange(): return lax.all_to_all(values, 'narrow', 0, 0)  3.35 us
    ppermute x6, waiting for transfers between devices, across(): return lax.ppermute(values, 'wide', [(i, i ^ step) for i in range(wide)])  2.79 us
  transfers between devices with their start and end apart: 7, of which 2 were waited for; matrix products, arithmetic and copies ran while one was open for 0% of the time, Pallas kernels for 1%

profile of v6, /device:TPU:0, one launch (start us, length us, event | category | flops | bytes accessed | tf_op | source)
XLA Modules:
  0.0 81.8 jit_solution(18129782594602312222)
XLA Ops:
  0.6 6.4 %shard_map.93 = (f32[16,21,64,128]{3,2,1,0:T(8,128)S(1)}, f32[8,128]{1,0:T(8,128)S(1)}, s32[16,128]{1,0:T(8,128)S(1)}, s32[16,128]{1,0:T(8,128)S(1)}, s32[16,128...) custom-call(f32[2,1024,8,128]{3,2,1,0:T(8,128)} %bitcast.16, ...), custom_call_target="tpu_custom_call" | custom-call | tf_op jit(solution)/shard_map/pallas_call | solution.py:484
  7.1 3.1 %collective-permute-start = (f32[16,1152]{1,0:T(8,128)S(1)}, f32[16,1152]{1,0:T(8,128)S(1)}, u32[]{:S(2)}, u32[]{:S(2)}) collective-permute-start(f32[16,1152]{1,0:T(8,128)S(1)} %get-tuple-element.31.refs_1_), channel_id=1, source_target_pairs={{0,8},{8,0},{16,24},{24,16},{1,9},{9,1},{17,25},{25,17},{2,10},{10... | collective-permute-start | bytes 221192 | tf_op jit(solution)/shard_map/ppermute | solution.py:458
  10.2 8.5 %all_to_all.36.refs_0_ = f32[8,8,256]{2,1,0:T(8,128)S(1)} all-to-all(f32[8,8,256]{2,1,0:T(8,128)S(1)} %get-tuple-element.30), channel_id=1, replica_groups=mesh['wide'=4,'narrow'=8] {'narrow'}, dimensions={0} | all-to-all | bytes 131072 | tf_op jit(solution)/shard_map/all_to_all | solution.py:461
  18.7 1.4 %shard_map.94 = (f32[8,2048]{1,0:T(8,128)S(1)}, f32[8,8,256]{2,1,0:T(8,128)S(1)}, f32[16,1152]{1,0:T(8,128)S(1)}, s32[16,128]{1,0:T(8,128)S(1)}, bf16[2048,256]{1,0:T(8,128)(2,1)S(1)}) custom-call(f32[8,8,256]{2,1,0:T(8,128)S(1)} %all_to_all.36.refs_0_, f32[16,1152]{1,0:T(8,128)S(1)} %get-tuple-element.31.refs_1_, f32[16,1152]{1,0:T(8,128)S(1)} %collective-permute-done.refs_2_), custom_call_target="tpu_custom_call" | custom-call | tf_op jit(solution)/shard_map/pallas_call | solution.py:540
  20.1 2.7 %collective-permute-start.1 = (f32[16,1152]{1,0:T(8,128)S(1)}, f32[16,1152]{1,0:T(8,128)S(1)}, u32[]{:S(2)}, u32[]{:S(2)}) collective-permute-start(f32[16,1152]{1,0:T(8,128)S(1)} %get-tuple-element.34.half_ref), channel_id=1, source_target_pairs={{0,16},{8,24},{16,0},{24,8},{1,17},{9,25},{17,1},{25,9},{2,18},{10... | collective-permute-start | bytes 221192 | tf_op jit(solution)/shard_map/ppermute | solution.py:458
  22.8 7.4 %all_to_all.37.recv_ref = f32[8,8,256]{2,1,0:T(8,128)S(1)} all-to-all(f32[8,8,256]{2,1,0:T(8,128)S(1)} %get-tuple-element.33), channel_id=1, replica_groups=mesh['wide'=4,'narrow'=8] {'narrow'}, dimensions={0} | all-to-all | bytes 131072 | tf_op jit(solution)/shard_map/all_to_all | solution.py:461
  30.2 0.0 collective-permute-done.1.later_ref
  30.2 4.1 %shard_map.95 = (f32[16,1024]{1,0:T(8,128)S(1)}, f32[16,1152]{1,0:T(8,128)S(1)}, f32[8,8,256]{2,1,0:T(8,128)S(1)}, f32[8,128]{1,0:T(8,128)}) custom-call(f32[8,8,256]{2,1,0:T(8,128)S(1)} %all_to_all.37.recv_ref, f32[16,1152]{1,0:T(8,128)S(1)} %get-tuple-element.34.half_ref, f32[16,1152]{1,0:T(8,128)S(1)} %collective-permute-done.1.later_ref, ...), custom_call_target="tpu_custom_call" | custom-call | tf_op jit(solution)/shard_map/pallas_call | solution.py:549
  34.3 0.5 collective-permute-start.2
  34.8 7.4 %all_to_all.38.refs_0_ = f32[8,8,256]{2,1,0:T(8,128)S(1)} all-to-all(f32[8,8,256]{2,1,0:T(8,128)S(1)} %get-tuple-element.40), channel_id=1, replica_groups=mesh['wide'=4,'narrow'=8] {'narrow'}, dimensions={0} | all-to-all | bytes 131072 | tf_op jit(solution)/shard_map/all_to_all | solution.py:461
  42.2 0.0 collective-permute-done.2.refs_2_
  42.2 1.1 %shard_map.96 = (f32[8,2048]{1,0:T(8,128)S(1)}, f32[8,8,256]{2,1,0:T(8,128)S(1)}, f32[16,1152]{1,0:T(8,128)S(1)}, f32[8,128]{1,0:T(8,128)S(1)}) custom-call(f32[8,8,256]{2,1,0:T(8,128)S(1)} %all_to_all.38.refs_0_, f32[16,1152]{1,0:T(8,128)S(1)} %get-tuple-element.41.refs_1_, f32[16,1152]{1,0:T(8,128)S(1)} %collective-permute-done.2.refs_2_, ...), custom_call_target="tpu_custom_call" | custom-call | tf_op jit(solution)/shard_map/pallas_call | solution.py:544
  43.3 0.4 collective-permute-start.3
  43.7 7.4 %all_to_all.39.recv_ref = f32[8,8,256]{2,1,0:T(8,128)S(1)} all-to-all(f32[8,8,256]{2,1,0:T(8,128)S(1)} %get-tuple-element.45), channel_id=1, replica_groups=mesh['wide'=4,'narrow'=8] {'narrow'}, dimensions={0} | all-to-all | bytes 131072 | tf_op jit(solution)/shard_map/all_to_all | solution.py:461
  51.1 4.8 %shard_map.97 = (f32[16,1024]{1,0:T(8,128)S(1)}, f32[16,1152]{1,0:T(8,128)S(1)}, f32[8,8,256]{2,1,0:T(8,128)}, f32[8,128]{1,0:T(8,128)S(1)}) custom-call(f32[8,8,256]{2,1,0:T(8,128)S(1)} %all_to_all.39.recv_ref, f32[16,1152]{1,0:T(8,128)S(1)} %get-tuple-element.46.half_ref, f32[16,1152]{1,0:T(8,128)S(1)} %collective-permute-done.3.later_ref, ...), custom_call_target="tpu_custom_call" | custom-call | tf_op jit(solution)/shard_map/pallas_call | solution.py:549
  55.8 1.6 %collective-permute-start.4 = (f32[16,1152]{1,0:T(8,128)S(1)}, f32[16,1152]{1,0:T(8,128)S(1)}, u32[]{:S(2)}, u32[]{:S(2)}) collective-permute-start(f32[16,1152]{1,0:T(8,128)S(1)} %get-tuple-element.51), channel_id=1, source_target_pairs={{0,8},{8,0},{16,24},{24,16},{1,9},{9,1},{17,25},{25,17},{2,10},{10... | collective-permute-start | bytes 221192 | tf_op jit(solution)/shard_map/ppermute | solution.py:458
  57.4 2.8 %collective-permute-done.4 = f32[16,1152]{1,0:T(8,128)S(1)} collective-permute-done((f32[16,1152]{1,0:T(8,128)S(1)}, f32[16,1152]{1,0:T(8,128)S(1)}, u32[]{:S(2)}, u32[]{:S(2)}) %collective-permute-start.4) | collective-permute-done | bytes 73760 | tf_op jit(solution)/shard_map/ppermute | solution.py:458
  60.2 2.7 %collective-permute-start.5 = (f32[16,1152]{1,0:T(8,128)S(1)}, f32[16,1152]{1,0:T(8,128)S(1)}, u32[]{:S(2)}, u32[]{:S(2)}) collective-permute-start(f32[16,1152]{1,0:T(8,128)S(1)} %add.3.att2a), channel_id=1, source_target_pairs={{0,16},{8,24},{16,0},{24,8},{1,17},{9,25},{17,1},{25,9},{2,18},{10... | collective-permute-start | bytes 221192 | tf_op jit(solution)/shard_map/ppermute | solution.py:458
  62.9 3.4 %all-to-all-start.4 = ((f32[8,8,256]{2,1,0:T(8,128)}), f32[8,8,256]{2,1,0:T(8,128)S(1)}, u32[]{:S(2)}, u32[]{:S(2)}) async-start(f32[8,8,256]{2,1,0:T(8,128)} %get-tuple-element.48), calls=%async_computation.4 | async-start | bytes 131072 | tf_op jit(solution)/shard_map/all_to_all | solution.py:461
  66.2 4.9 %all-to-all-done.4.refs_0_ = f32[8,8,256]{2,1,0:T(8,128)S(1)} async-done(((f32[8,8,256]{2,1,0:T(8,128)}), f32[8,8,256]{2,1,0:T(8,128)S(1)}, u32[]{:S(2)}, u32[]{:S(2)}) %all-to-all-start.4) | async-done | bytes 65568 | tf_op jit(solution)/shard_map/all_to_all | solution.py:461
  71.2 0.4 shard_map.98.src2
  71.6 0.3 shard_map.99
  71.9 8.9 %all_to_all.40 = f32[32,1,128]{2,1,0:T(1,128)S(1)} all-to-all(f32[32,1,128]{2,1,0:T(1,128)S(1)} %bitcast.15), channel_id=1, replica_groups=mesh['wide'=4,'narrow'=8] {'wide','narrow'}, dimensions={0} | all-to-all | bytes 32768 | tf_op jit(solution)/shard_map/all_to_all | solution.py:564
  80.9 0.9 %shard_map.100 = (f32[5,2048]{1,0:T(8,128)}, f32[16,1024]{1,0:T(8,128)}, f32[5,2048]{1,0:T(8,128)}, f32[16,1024]{1,0:T(8,128)}) custom-call(f32[32,128]{1,0:T(8,128)S(1)} %bitcast.14, f32[8,128]{1,0:T(8,128)S(1)} %get-tuple-element.53.scale_ref, f32[8,2048]{1,0:T(8,128)S(1)} %get-tuple-element.32.src0, f32[8,2048]{1,0:T(8,128)S(1)} %get-tuple-element.44.src1, ...), custom_call_target="tpu_custom_call" | custom-call | tf_op jit(solution)/shard_map/pallas_call | solution.py:565
  (6 shorter events, 0.0 us)
Async XLA Ops:
  7.1 11.6 %collective-permute-start = (f32[16,1152]{1,0:T(8,128)S(1)}, f32[16,1152]{1,0:T(8,128)S(1)}, u32[]{:S(2)}, u32[]{:S(2)}) collective-permute-start(f32[16,1152]{1,0:T(8,128)S(1)} %get-tuple-element.31.refs_1_), channel_id=1, source_target_pairs={{0,8},{8,0},{16,24},{24,16},{1,9},{9,1},{17,25},{25,17},{2,10},{10... | collective-permute-start | bytes 221192 | tf_op jit(solution)/shard_map/ppermute | solution.py:458
  20.1 10.0 %collective-permute-start.1 = (f32[16,1152]{1,0:T(8,128)S(1)}, f32[16,1152]{1,0:T(8,128)S(1)}, u32[]{:S(2)}, u32[]{:S(2)}) collective-permute-start(f32[16,1152]{1,0:T(8,128)S(1)} %get-tuple-element.34.half_ref), channel_id=1, source_target_pairs={{0,16},{8,24},{16,0},{24,8},{1,17},{9,25},{17,1},{25,9},{2,18},{10... | collective-permute-start | bytes 221192 | tf_op jit(solution)/shard_map/ppermute | solution.py:458
  34.3 7.9 %collective-permute-start.2 = (f32[16,1152]{1,0:T(8,128)S(1)}, f32[16,1152]{1,0:T(8,128)S(1)}, u32[]{:S(2)}, u32[]{:S(2)}) collective-permute-start(f32[16,1152]{1,0:T(8,128)S(1)} %get-tuple-element.41.refs_1_), channel_id=1, source_target_pairs={{0,8},{8,0},{16,24},{24,16},{1,9},{9,1},{17,25},{25,17},{2,10},{10... | collective-permute-start | bytes 221192 | tf_op jit(solution)/shard_map/ppermute | solution.py:458
  43.3 7.8 %collective-permute-start.3 = (f32[16,1152]{1,0:T(8,128)S(1)}, f32[16,1152]{1,0:T(8,128)S(1)}, u32[]{:S(2)}, u32[]{:S(2)}) collective-permute-start(f32[16,1152]{1,0:T(8,128)S(1)} %get-tuple-element.46.half_ref), channel_id=1, source_target_pairs={{0,16},{8,24},{16,0},{24,8},{1,17},{9,25},{17,1},{25,9},{2,18},{10... | collective-permute-start | bytes 221192 | tf_op jit(solution)/shard_map/ppermute | solution.py:458
  55.8 4.4 %collective-permute-start.4 = (f32[16,1152]{1,0:T(8,128)S(1)}, f32[16,1152]{1,0:T(8,128)S(1)}, u32[]{:S(2)}, u32[]{:S(2)}) collective-permute-start(f32[16,1152]{1,0:T(8,128)S(1)} %get-tuple-element.51), channel_id=1, source_target_pairs={{0,8},{8,0},{16,24},{24,16},{1,9},{9,1},{17,25},{25,17},{2,10},{10... | collective-permute-start | bytes 221192 | tf_op jit(solution)/shard_map/ppermute | solution.py:458
  60.2 11.4 %collective-permute-start.5 = (f32[16,1152]{1,0:T(8,128)S(1)}, f32[16,1152]{1,0:T(8,128)S(1)}, u32[]{:S(2)}, u32[]{:S(2)}) collective-permute-start(f32[16,1152]{1,0:T(8,128)S(1)} %add.3.att2a), channel_id=1, source_target_pairs={{0,16},{8,24},{16,0},{24,8},{1,17},{9,25},{17,1},{25,9},{2,18},{10... | collective-permute-start | bytes 221192 | tf_op jit(solution)/shard_map/ppermute | solution.py:458
  62.9 8.3 %all-to-all-start.4 = ((f32[8,8,256]{2,1,0:T(8,128)}), f32[8,8,256]{2,1,0:T(8,128)S(1)}, u32[]{:S(2)}, u32[]{:S(2)}) async-start(f32[8,8,256]{2,1,0:T(8,128)} %get-tuple-element.48), calls=%async_computation.4 | async-start | bytes 131072 | tf_op jit(solution)/shard_map/all_to_all | solution.py:461

commit v7 on v6

--- a/solution.py
+++ b/solution.py
@@ -56,6 +56,21 @@
         whole = jnp.concatenate([piece] * (16 // rows), axis=0).astype(BF16)
         whole = jnp.concatenate([whole] * (size // 16), axis=0)
         store[pl.ds(part * size, size), pl.ds(column, LANE)] = whole * mask
+
+
+def fold_rows(values):
+    total = values[0:8]
+    for at in range(8, values.shape[0], 8):
+        total = total + values[at : at + 8]
+    return total
+
+
+def row_sums(sums):
+    rows = sums.shape[0] // 8
+    total = sums[pl.ds(0, rows, stride=8), :]
+    for at in range(1, 8):
+        total = total + sums[pl.ds(at, rows, stride=8), :]
+    return total
 
 
 def rank_blocks(narrow, source_ref, segment_ref, pos_ref, seg_ref, order_ref, ids_ref, left, right):
@@ -162,7 +177,7 @@
     narrow,
     att_hbm, src_hbm, rhs_hbm, source_hbm, segment_hbm, count_hbm,
     table_ref, square_ref, pos_ref, seg_ref, order_ref, right, att_ref, send_ref,
-    att_in, src_in, rhs_in, source_in, segment_in, count_in, blocks, ids, left, sems, int_sems,
+    att_in, src_in, rhs_in, source_in, segment_in, count_in, blocks, ids, sums, left, sems, int_sems,
 ):
     groups, att_sets = att_in.shape[0], att_in.shape[1]
     att_rows, src_rows = att_sets * 8, src_hbm.shape[1]
@@ -196,6 +211,7 @@
         one.wait()
     count_in[...] = to_tiles(count_in[...])
     square_ref[...] = jnp.zeros_like(square_ref)
+    sums[...] = jnp.zeros_like(sums)
     rank_blocks(narrow, source_in, segment_in, pos_ref, seg_ref, order_ref, ids, left, right)
     mark_high(right, seg_ref[...])
     place = row_iota(obs)
@@ -212,11 +228,7 @@
             live.append(alive)
             part = jnp.where(alive, wide_rhs[half * obs : half * obs + obs], 0.0)
             rhs.append(part)
-            square = part * part
-            total = square[0:8]
-            for at in range(8, obs, 8):
-                total = total + square[at : at + 8]
-            square_ref[...] += total
+            square_ref[...] += fold_rows(part * part)
         for i in range(att_rows + src_rows):
             if i < att_rows:
                 base = pl.multiple_of((g * att_sets + i // 8) * (LANE * 8), LANE * 8)
@@ -228,10 +240,9 @@
             for half in range(2):
                 part = jnp.where(live[half], turned[half * obs : half * obs + obs], 0.0)
                 table_ref[g * 2 + half, i] = part
-                blocks[g * 2 + half, i : i + 1, :] = jnp.sum(part * rhs[half], axis=0, keepdims=True)
+                sums[half, i * 8 : i * 8 + 8, :] = fold_rows(part * rhs[half])
         for half in range(2):
-            rest = 24 - att_rows - src_rows
-            blocks[g * 2 + half, 24 - rest : 24, :] = jnp.zeros((rest, LANE), F32)
+            blocks[g * 2 + half] = row_sums(sums.at[half])
         return carry
 
     lax.fori_loop(0, groups, turn, 0)
@@ -302,8 +313,9 @@
 
 def product_kernel(
     narrow, first, recv_ref, half_ref, later_ref, known_ref, pos_ref, seg_ref, order_ref, right,
-    table_ref, full_ref, att_ref, send_ref, scale_ref, vec, blocks, left,
+    table_ref, full_ref, att_ref, sent_ref, scale_ref, vec, blocks, sums, left, *own,
 ):
+    send_ref = sent_ref if first else own[0]
     tiles, rows = pos_ref.shape[0], table_ref.shape[1]
     per = recv_ref.shape[2] // LANE
     full = half_ref[...] + later_ref[...]
@@ -349,26 +361,37 @@
             part = table_ref[t, i] * vec[t, i : i + 1, :]
             image = part if image is None else image + part
         for i in range(rows):
-            blocks[t, i : i + 1, :] = jnp.sum(table_ref[t, i] * image, axis=0, keepdims=True)
-        blocks[t, rows:24, :] = jnp.zeros((24 - rows, LANE), F32)
+            sums[i * 8 : i * 8 + 8, :] = fold_rows(table_ref[t, i] * image)
+        blocks[t] = row_sums(sums)
         gather(jnp.minimum(t + 1, tiles - 1))
         return carry
 
+    sums[...] = jnp.zeros_like(sums)
     gather(0)
     lax.fori_loop(0, tiles, multiply, 0)
+    send_sorted(narrow, blocks, order_ref, lambda t: send_note, send_ref)
+    if not first:
+        sending = pltpu.make_async_copy(send_ref, sent_ref, own[1])
+        sending.start()
     fill_att(blocks, seg_ref, left, tiles - 1)
     scatter_att(att_ref, left, right)
-    send_sorted(narrow, blocks, order_ref, lambda t: send_note, send_ref)
+    if not first:
+        sending.wait()
 
 
 def dots_kernel(
-    src0, src1, src2, att0, att1, att2a, att2b, square_ref, scale_ref, weight_ref, out_ref, att2
+    src0, src1, src2, att0, att1, mine, later, square_ref, scale_ref, side_ref, out_ref, kept_ref
 ):
-    att2[...] = (att2a[...] + att2b[...])[:, :SEG_DEV]
+    kept_ref[...] = mine[...] + later[...]
     scale = scale_ref[0:1, 0:1]
-    weight = weight_ref[0:1, 0:1]
+    upper, weight = side_ref[0:1, 0:1] > 0.5, side_ref[1:2, 0:1]
+    half = kept_ref.shape[1]
+
+    def own_half(ref):
+        return jnp.where(upper, ref[:, half:], ref[:, :half])
+
     src = (src0[...], src1[...] * scale, src2[...] * scale)
-    att = (att0[...], att1[...] * scale, att2[...] * scale)
+    att = (own_half(att0), own_half(att1) * scale, kept_ref[...] * scale)
     out = jnp.where(lane_iota(1) == 0, jnp.sum(square_ref[...], keepdims=True), 0.0)
     for at, (one, two) in enumerate(((0, 0), (0, 1), (1, 1), (1, 2), (2, 2))):
         total = jnp.sum(src[one] * src[two], keepdims=True)
@@ -378,8 +401,13 @@
 
 
 def finish_kernel(
-    dots_ref, scale_ref, src0, src1, src2, att0, att1, att2, sol_src, sol_att, dir_src, dir_att
+    dots_ref, scale_ref, side_ref, src0, src1, src2, att0, att1, kept, back,
+    sol_src, sol_att, dir_src, dir_att, att2,
 ):
+    upper = side_ref[0:1, 0:1] > 0.5
+    half = kept.shape[1]
+    att2[:, :half] = jnp.where(upper, back[...], kept[...])
+    att2[:, half:] = jnp.where(upper, kept[...], back[...])
     sums = jnp.sum(dots_ref[...], axis=0, keepdims=True)
     rhs_square, m0, m1, m2, m3, m4 = [lane_value(sums, at) for at in range(6)]
     scale = scale_ref[0:1, 0:1]
@@ -460,14 +488,16 @@
     def exchange(values):
         return lax.all_to_all(values, "narrow", 0, 0)
 
-    def far_sums(total):
+    def far_sums(total, end):
         later, jump = None, 2
-        while jump < wide:
+        while jump < end:
             if later is not None:
                 total = total + later
             later = across(total, jump)
             jump *= 2
-        return total, jnp.zeros_like(total) if later is None else later
+        return total, later
+
+    upper = lax.axis_index("wide") >= wide // 2
 
     tile_rows = lambda values: values.reshape(tiles, LANE)
     att_view = att_design.reshape(att_rows // 8, 8, columns, LANE).transpose(0, 2, 1, 3)
@@ -502,6 +532,7 @@
             pltpu.VMEM((tiles, LANE), I32),
             pltpu.VMEM((tiles, 24, LANE), F32),
             pltpu.VMEM((tiles, LANE), F32),
+            pltpu.VMEM((2, 24 * 8, LANE), F32),
             att_left,
             pltpu.SemaphoreType.DMA((3, groups)),
             pltpu.SemaphoreType.DMA((3,)),
@@ -531,9 +562,14 @@
         arrived = exchange(send)
         kernel = functools.partial(owner_kernel, narrow, first_time, last_time)
         if last_time:
-            total, later = far_sums(part + other)
+            total, later = far_sums(part + other, wide // 2)
+            if later is not None:
+                total = total + later
+            low, high = total[:, : SEG_DEV // 2], total[:, SEG_DEV // 2 : SEG_DEV]
+            mine, other = jnp.where(upper, high, low), jnp.where(upper, low, high)
+            later = across(other, wide // 2)
             src_sum = call(kernel, src_shape, [src_left])(arrived, *owners)
-            results.append((src_sum, total, later))
+            results.append((src_sum, mine, later))
             break
         outs = (src_shape, send_shape, att_shape)
         if first_time:
@@ -544,24 +580,41 @@
             src_sum, back, half, note = call(kernel, outs + (sds((8, LANE)),), [src_left])(
                 arrived, part, other, *owners
             )
-        total, later = far_sums(half)
+        total, later = far_sums(half, wide)
         back = exchange(back)
+        own, specs = [], {}
+        if not first_time:
+            in_vmem = pl.BlockSpec(memory_space=pltpu.VMEM)
+            own = [pltpu.VMEM(send_shape.shape, F32), pltpu.SemaphoreType.DMA(())]
+            specs = dict(
+                out_specs=(in_vmem, in_vmem, pl.BlockSpec(memory_space=pltpu.HBM), in_vmem)
+            )
         att_sum, part, send, scale = call(
             functools.partial(product_kernel, narrow, first_time),
-            (sds((16, SEG_DEV)), att_shape, send_shape, sds((8, LANE))),
+            (
+                sds((16, SEG_DEV)),
+                att_shape,
+                send_shape if first_time else pltpu.HBM(send_shape.shape, F32),
+                sds((8, LANE)),
+            ),
             [
                 pltpu.VMEM((tiles, 24, LANE), F32),
                 pltpu.VMEM((tiles, 24, LANE), F32),
+                pltpu.VMEM((24 * 8, LANE), F32),
                 att_left,
-            ],
+            ]
+            + own,
+            **specs,
         )(back, total, later, note, pos, seg, order, att_right, table)
         results.append((src_sum, att_sum))
-    weight = jnp.where(lax.axis_index("wide") == 0, 1.0, 0.0).astype(F32) * jnp.ones((8, LANE), F32)
-    (src0, att0), (src1, att1), (src2, att2a, att2b) = results
-    dots, att2 = call(dots_kernel, (sds((devices, LANE)), sds((16, SEG_DEV))))(
-        src0, src1, src2, att0, att1, att2a, att2b, square, scale, weight
+    counted = lax.axis_index("wide") % (wide // 2) == 0
+    side = jnp.where(row_iota(8) == 0, upper, counted).astype(F32)
+    (src0, att0), (src1, att1), (src2, mine, later) = results
+    dots, kept = call(dots_kernel, (sds((devices, LANE)), sds((16, SEG_DEV // 2))))(
+        src0, src1, src2, att0, att1, mine, later, square, scale, side
     )
     dots = lax.all_to_all(dots, ("wide", "narrow"), 0, 0, tiled=True)
+    back = across(kept, wide // 2)
     sol_src, sol_att, dir_src, dir_att = call(
         finish_kernel,
         (
@@ -570,7 +623,8 @@
             sds((src_rows, SRC_DEV)),
             sds((att_rows, SEG_DEV)),
         ),
-    )(dots, scale, src0, src1, src2, att0, att1, att2)
+        [pltpu.VMEM((16, SEG_DEV), F32)],
+    )(dots, scale, side, src0, src1, src2, att0, att1, kept, back)
     return (sol_src, sol_att, dir_src, dir_att)
 
 

time: 82.2 us -> 80.5 us (0.979)
  waiting for transfers between devices: 7.73 us -> 2.26 us
  starting transfers between devices: 14.3 us -> 16.9 us
  blocking collectives: 39.6 us -> 40.6 us
    ppermute x6 -> x7, waiting for transfers between devices: 2.79 us -> 0.02 us  [across(): return lax.ppermute(values, 'wide', [(i, i ^ step) for i in range(wide)])]
    all_to_all x1, waiting for transfers between devices: 4.94 us -> 2.24 us  [exchange(): return lax.all_to_all(values, 'narrow', 0, 0)]
    ppermute x6 -> x7, starting transfers between devices: 10.9 us -> 13.5 us  [across(): return lax.ppermute(values, 'wide', [(i, i ^ step) for i in range(wide)])]
    all_to_all x1, blocking collectives: 8.92 us -> 9.93 us  [on_device(): dots = lax.all_to_all(dots, ('wide', 'narrow'), 0, 0, tiled=True)]
  transfers between devices with their start and end apart: 7 -> 8, of which waited for: 2 -> 1; matrix products, arithmetic and copies ran while one was open for 0% -> 0% of each run, Pallas kernels for 1% -> 1%
where the time goes in v7:
time: 80.5 us; the launch traced here: 80.1 us
  blocking collectives  40.6 us (50%)
  Pallas kernels  19.5 us (24%)
  starting transfers between devices  16.9 us (21%)
  waiting for transfers between devices  2.26 us (3%)
    all_to_all x4, blocking collectives, exchange(): return lax.all_to_all(values, 'narrow', 0, 0)  30.7 us
    ppermute x7, starting transfers between devices, across(): return lax.ppermute(values, 'wide', [(i, i ^ step) for i in range(wide)])  13.5 us
    all_to_all x1, blocking collectives, on_device(): dots = lax.all_to_all(dots, ('wide', 'narrow'), 0, 0, tiled=True)  9.93 us
    pallas_call x2, Pallas kernels, on_device(): call(functools.partial(product_kernel, narrow, first_time), (sds((16, SEG...  8.84 us
    pallas_call x1, Pallas kernels, on_device(): call(functools.partial(start_kernel, narrow), (sds(table_shape), sds((8,...  6.57 us
    all_to_all x1, starting transfers between devices, exchange(): return lax.all_to_all(values, 'narrow', 0, 0)  3.35 us
    all_to_all x1, waiting for transfers between devices, exchange(): return lax.all_to_all(values, 'narrow', 0, 0)  2.24 us
  transfers between devices with their start and end apart: 8, of which 1 were waited for; matrix products, arithmetic and copies ran while one was open for 0% of the time, Pallas kernels for 1%

profile of v7, /device:TPU:0, one launch (start us, length us, event | category | flops | bytes accessed | tf_op | source)
XLA Modules:
  0.0 80.1 jit_solution(8276924581421906417)
XLA Ops:
  0.6 6.6 %shard_map.93 = (f32[16,21,64,128]{3,2,1,0:T(8,128)S(1)}, f32[8,128]{1,0:T(8,128)S(1)}, s32[16,128]{1,0:T(8,128)S(1)}, s32[16,128]{1,0:T(8,128)S(1)}, s32[16,128...) custom-call(f32[2,1024,8,128]{3,2,1,0:T(8,128)} %bitcast.16, ...), custom_call_target="tpu_custom_call" | custom-call | tf_op jit(solution)/shard_map/pallas_call | solution.py:514
  7.2 3.1 %collective-permute-start = (f32[16,1152]{1,0:T(8,128)S(1)}, f32[16,1152]{1,0:T(8,128)S(1)}, u32[]{:S(2)}, u32[]{:S(2)}) collective-permute-start(f32[16,1152]{1,0:T(8,128)S(1)} %get-tuple-element.31.refs_1_), channel_id=1, source_target_pairs={{0,8},{8,0},{16,24},{24,16},{1,9},{9,1},{17,25},{25,17},{2,10},{10... | collective-permute-start | bytes 221192 | tf_op jit(solution)/shard_map/ppermute | solution.py:486
  10.3 8.5 %all_to_all.36.refs_0_ = f32[8,8,256]{2,1,0:T(8,128)S(1)} all-to-all(f32[8,8,256]{2,1,0:T(8,128)S(1)} %get-tuple-element.30), channel_id=1, replica_groups=mesh['wide'=4,'narrow'=8] {'narrow'}, dimensions={0} | all-to-all | bytes 131072 | tf_op jit(solution)/shard_map/all_to_all | solution.py:489
  18.8 0.0 collective-permute-done.refs_2_
  18.9 1.4 %shard_map.94 = (f32[8,2048]{1,0:T(8,128)S(1)}, f32[8,8,256]{2,1,0:T(8,128)S(1)}, f32[16,1152]{1,0:T(8,128)S(1)}, s32[16,128]{1,0:T(8,128)S(1)}, bf16[2048,256]{1,0:T(8,128)(2,1)S(1)}) custom-call(f32[8,8,256]{2,1,0:T(8,128)S(1)} %all_to_all.36.refs_0_, f32[16,1152]{1,0:T(8,128)S(1)} %get-tuple-element.31.refs_1_, f32[16,1152]{1,0:T(8,128)S(1)} %collective-permute-done.refs_2_), custom_call_target="tpu_custom_call" | custom-call | tf_op jit(solution)/shard_map/pallas_call | solution.py:576
  20.3 2.7 %collective-permute-start.1 = (f32[16,1152]{1,0:T(8,128)S(1)}, f32[16,1152]{1,0:T(8,128)S(1)}, u32[]{:S(2)}, u32[]{:S(2)}) collective-permute-start(f32[16,1152]{1,0:T(8,128)S(1)} %get-tuple-element.34.half_ref), channel_id=1, source_target_pairs={{0,16},{8,24},{16,0},{24,8},{1,17},{9,25},{17,1},{25,9},{2,18},{10... | collective-permute-start | bytes 221192 | tf_op jit(solution)/shard_map/ppermute | solution.py:486
  22.9 7.4 %all_to_all.37.recv_ref = f32[8,8,256]{2,1,0:T(8,128)S(1)} all-to-all(f32[8,8,256]{2,1,0:T(8,128)S(1)} %get-tuple-element.33), channel_id=1, replica_groups=mesh['wide'=4,'narrow'=8] {'narrow'}, dimensions={0} | all-to-all | bytes 131072 | tf_op jit(solution)/shard_map/all_to_all | solution.py:489
  30.3 4.2 %shard_map.95 = (f32[16,1024]{1,0:T(8,128)S(1)}, f32[16,1152]{1,0:T(8,128)S(1)}, f32[8,8,256]{2,1,0:T(8,128)S(1)}, f32[8,128]{1,0:T(8,128)}) custom-call(f32[8,8,256]{2,1,0:T(8,128)S(1)} %all_to_all.37.recv_ref, f32[16,1152]{1,0:T(8,128)S(1)} %get-tuple-element.34.half_ref, f32[16,1152]{1,0:T(8,128)S(1)} %collective-permute-done.1.later_ref, ...), custom_call_target="tpu_custom_call" | custom-call | tf_op jit(solution)/shard_map/pallas_call | solution.py:592
  34.5 0.4 collective-permute-start.2
  34.9 7.4 %all_to_all.38.refs_0_ = f32[8,8,256]{2,1,0:T(8,128)S(1)} all-to-all(f32[8,8,256]{2,1,0:T(8,128)S(1)} %get-tuple-element.40), channel_id=1, replica_groups=mesh['wide'=4,'narrow'=8] {'narrow'}, dimensions={0} | all-to-all | bytes 131072 | tf_op jit(solution)/shard_map/all_to_all | solution.py:489
  42.3 1.1 %shard_map.96 = (f32[8,2048]{1,0:T(8,128)S(1)}, f32[8,8,256]{2,1,0:T(8,128)S(1)}, f32[16,1152]{1,0:T(8,128)S(1)}, f32[8,128]{1,0:T(8,128)S(1)}) custom-call(f32[8,8,256]{2,1,0:T(8,128)S(1)} %all_to_all.38.refs_0_, f32[16,1152]{1,0:T(8,128)S(1)} %get-tuple-element.41.refs_1_, f32[16,1152]{1,0:T(8,128)S(1)} %collective-permute-done.2.refs_2_, ...), custom_call_target="tpu_custom_call" | custom-call | tf_op jit(solution)/shard_map/pallas_call | solution.py:580
  43.4 0.4 collective-permute-start.3
  43.8 7.4 %all_to_all.39.recv_ref = f32[8,8,256]{2,1,0:T(8,128)S(1)} all-to-all(f32[8,8,256]{2,1,0:T(8,128)S(1)} %get-tuple-element.45), channel_id=1, replica_groups=mesh['wide'=4,'narrow'=8] {'narrow'}, dimensions={0} | all-to-all | bytes 131072 | tf_op jit(solution)/shard_map/all_to_all | solution.py:489
  51.2 4.7 %shard_map.97 = (f32[16,1024]{1,0:T(8,128)S(1)}, f32[16,1152]{1,0:T(8,128)S(1)}, f32[8,8,256]{2,1,0:T(8,128)}, f32[8,128]{1,0:T(8,128)S(1)}) custom-call(f32[8,8,256]{2,1,0:T(8,128)S(1)} %all_to_all.39.recv_ref, f32[16,1152]{1,0:T(8,128)S(1)} %get-tuple-element.46.half_ref, f32[16,1152]{1,0:T(8,128)S(1)} %collective-permute-done.3.later_ref, ...), custom_call_target="tpu_custom_call" | custom-call | tf_op jit(solution)/shard_map/pallas_call | solution.py:592
  55.9 1.6 %collective-permute-start.4 = (f32[16,1152]{1,0:T(8,128)S(1)}, f32[16,1152]{1,0:T(8,128)S(1)}, u32[]{:S(2)}, u32[]{:S(2)}) collective-permute-start(f32[16,1152]{1,0:T(8,128)S(1)} %get-tuple-element.51), channel_id=1, source_target_pairs={{0,8},{8,0},{16,24},{24,16},{1,9},{9,1},{17,25},{25,17},{2,10},{10... | collective-permute-start | bytes 221192 | tf_op jit(solution)/shard_map/ppermute | solution.py:486
  57.5 3.4 %all-to-all-start.4 = ((f32[8,8,256]{2,1,0:T(8,128)}), f32[8,8,256]{2,1,0:T(8,128)S(1)}, u32[]{:S(2)}, u32[]{:S(2)}) async-start(f32[8,8,256]{2,1,0:T(8,128)} %get-tuple-element.48), calls=%async_computation.4 | async-start | bytes 131072 | tf_op jit(solution)/shard_map/all_to_all | solution.py:489
  60.9 2.7 %collective-permute-start.5 = (f32[16,512]{1,0:T(8,128)S(1)}, f32[16,512]{1,0:T(8,128)S(1)}, u32[]{:S(2)}, u32[]{:S(2)}) collective-permute-start(f32[16,512]{1,0:T(8,128)S(1)} %get-tuple-element.56), channel_id=1, source_target_pairs={{0,16},{8,24},{16,0},{24,8},{1,17},{9,25},{17,1},{25,9},{2,18},{10... | collective-permute-start | bytes 98312 | tf_op jit(solution)/shard_map/ppermute | solution.py:486
  63.6 2.2 %all-to-all-done.4.refs_0_ = f32[8,8,256]{2,1,0:T(8,128)S(1)} async-done(((f32[8,8,256]{2,1,0:T(8,128)}), f32[8,8,256]{2,1,0:T(8,128)S(1)}, u32[]{:S(2)}, u32[]{:S(2)}) %all-to-all-start.4) | async-done | bytes 65568 | tf_op jit(solution)/shard_map/all_to_all | solution.py:489
  65.8 0.4 shard_map.98.src2
  66.3 0.1 iota.7.side_ref
  66.3 0.3 shard_map.99
  66.6 2.6 %collective-permute-start.6 = (f32[16,512]{1,0:T(8,128)S(1)}, f32[16,512]{1,0:T(8,128)S(1)}, u32[]{:S(2)}, u32[]{:S(2)}) collective-permute-start(f32[16,512]{1,0:T(8,128)S(1)} %get-tuple-element.55.kept), channel_id=1, source_target_pairs={{0,16},{8,24},{16,0},{24,8},{1,17},{9,25},{17,1},{25,9},{2,18},{10... | collective-permute-start | bytes 98312 | tf_op jit(solution)/shard_map/ppermute | solution.py:486
  69.2 9.9 %all_to_all.40 = f32[32,1,128]{2,1,0:T(1,128)S(1)} all-to-all(f32[32,1,128]{2,1,0:T(1,128)S(1)} %bitcast.15), channel_id=1, replica_groups=mesh['wide'=4,'narrow'=8] {'wide','narrow'}, dimensions={0} | all-to-all | bytes 32768 | tf_op jit(solution)/shard_map/all_to_all | solution.py:616
  79.2 0.9 %shard_map.100 = (f32[5,2048]{1,0:T(8,128)}, f32[16,1024]{1,0:T(8,128)}, f32[5,2048]{1,0:T(8,128)}, f32[16,1024]{1,0:T(8,128)}) custom-call(f32[32,128]{1,0:T(8,128)S(1)} %bitcast.14, f32[8,128]{1,0:T(8,128)S(1)} %get-tuple-element.53.scale_ref, f32[8,128]{1,0:T(8,128)S(1)} %iota.7.side_ref, f32[8,2048]{1,0:T(8,128)S(1)} %get-tuple-element.32.src0, ...), custom_call_target="tpu_custom_call" | custom-call | tf_op jit(solution)/shard_map/pallas_call | solution.py:618
  (10 shorter events, 0.0 us)
Async XLA Ops:
  7.2 11.6 %collective-permute-start = (f32[16,1152]{1,0:T(8,128)S(1)}, f32[16,1152]{1,0:T(8,128)S(1)}, u32[]{:S(2)}, u32[]{:S(2)}) collective-permute-start(f32[16,1152]{1,0:T(8,128)S(1)} %get-tuple-element.31.refs_1_), channel_id=1, source_target_pairs={{0,8},{8,0},{16,24},{24,16},{1,9},{9,1},{17,25},{25,17},{2,10},{10... | collective-permute-start | bytes 221192 | tf_op jit(solution)/shard_map/ppermute | solution.py:486
  20.3 10.0 %collective-permute-start.1 = (f32[16,1152]{1,0:T(8,128)S(1)}, f32[16,1152]{1,0:T(8,128)S(1)}, u32[]{:S(2)}, u32[]{:S(2)}) collective-permute-start(f32[16,1152]{1,0:T(8,128)S(1)} %get-tuple-element.34.half_ref), channel_id=1, source_target_pairs={{0,16},{8,24},{16,0},{24,8},{1,17},{9,25},{17,1},{25,9},{2,18},{10... | collective-permute-start | bytes 221192 | tf_op jit(solution)/shard_map/ppermute | solution.py:486
  34.5 7.8 %collective-permute-start.2 = (f32[16,1152]{1,0:T(8,128)S(1)}, f32[16,1152]{1,0:T(8,128)S(1)}, u32[]{:S(2)}, u32[]{:S(2)}) collective-permute-start(f32[16,1152]{1,0:T(8,128)S(1)} %get-tuple-element.41.refs_1_), channel_id=1, source_target_pairs={{0,8},{8,0},{16,24},{24,16},{1,9},{9,1},{17,25},{25,17},{2,10},{10... | collective-permute-start | bytes 221192 | tf_op jit(solution)/shard_map/ppermute | solution.py:486
  43.4 7.8 %collective-permute-start.3 = (f32[16,1152]{1,0:T(8,128)S(1)}, f32[16,1152]{1,0:T(8,128)S(1)}, u32[]{:S(2)}, u32[]{:S(2)}) collective-permute-start(f32[16,1152]{1,0:T(8,128)S(1)} %get-tuple-element.46.half_ref), channel_id=1, source_target_pairs={{0,16},{8,24},{16,0},{24,8},{1,17},{9,25},{17,1},{25,9},{2,18},{10... | collective-permute-start | bytes 221192 | tf_op jit(solution)/shard_map/ppermute | solution.py:486
  55.9 5.0 %collective-permute-start.4 = (f32[16,1152]{1,0:T(8,128)S(1)}, f32[16,1152]{1,0:T(8,128)S(1)}, u32[]{:S(2)}, u32[]{:S(2)}) collective-permute-start(f32[16,1152]{1,0:T(8,128)S(1)} %get-tuple-element.51), channel_id=1, source_target_pairs={{0,8},{8,0},{16,24},{24,16},{1,9},{9,1},{17,25},{25,17},{2,10},{10... | collective-permute-start | bytes 221192 | tf_op jit(solution)/shard_map/ppermute | solution.py:486
  57.5 8.3 %all-to-all-start.4 = ((f32[8,8,256]{2,1,0:T(8,128)}), f32[8,8,256]{2,1,0:T(8,128)S(1)}, u32[]{:S(2)}, u32[]{:S(2)}) async-start(f32[8,8,256]{2,1,0:T(8,128)} %get-tuple-element.48), calls=%async_computation.4 | async-start | bytes 131072 | tf_op jit(solution)/shard_map/all_to_all | solution.py:489
  60.9 5.4 %collective-permute-start.5 = (f32[16,512]{1,0:T(8,128)S(1)}, f32[16,512]{1,0:T(8,128)S(1)}, u32[]{:S(2)}, u32[]{:S(2)}) collective-permute-start(f32[16,512]{1,0:T(8,128)S(1)} %get-tuple-element.56), channel_id=1, source_target_pairs={{0,16},{8,24},{16,0},{24,8},{1,17},{9,25},{17,1},{25,9},{2,18},{10... | collective-permute-start | bytes 98312 | tf_op jit(solution)/shard_map/ppermute | solution.py:486
  66.6 12.5 %collective-permute-start.6 = (f32[16,512]{1,0:T(8,128)S(1)}, f32[16,512]{1,0:T(8,128)S(1)}, u32[]{:S(2)}, u32[]{:S(2)}) collective-permute-start(f32[16,512]{1,0:T(8,128)S(1)} %get-tuple-element.55.kept), channel_id=1, source_target_pairs={{0,16},{8,24},{16,0},{24,8},{1,17},{9,25},{17,1},{25,9},{2,18},{10... | collective-permute-start | bytes 98312 | tf_op jit(solution)/shard_map/ppermute | solution.py:486
